TPU v7x, 32 devices: a whole 2x2x4 slice. The times are simulated.
32 devices in a mesh: fsdp: 8 (over y, x, core), head: 4 (over z).
Axes of the slice: x: 2, y: 2, z: 4, core: 2. Of those that a mesh axis runs over, the one named last changes fastest.
Arguments:
- query_nope: float32 [2048, 2048], P('fsdp', 'head'), may hold values from -6 to 6
- query_rope: float32 [2048, 1024], P('fsdp', 'head'), may hold values from -12 to 12
- latent: float32 [2048, 512], P(('fsdp', 'head')), may hold values from -6 to 6
- rope_key: float32 [2048, 64], P(('fsdp', 'head')), may hold values from -4 to 4
- cotangent: float32 [2048, 2048], P('fsdp', 'head'), may hold values from -6 to 6
- bounds: int32 [8, 2], P('fsdp'), may hold values from 1 to 256, as said below
- key_up: float32 [512, 2048], P('fsdp', 'head'), may hold values from -0.25 to 0.25
- value_up: float32 [512, 2048], P('fsdp', 'head'), may hold values from -0.25 to 0.25
Outputs:
- query_nope_grad: float32 [2048, 2048], P('fsdp', 'head')
- query_rope_grad: float32 [2048, 1024], P('fsdp', 'head')
- latent_grad: float32 [2048, 512], P(('fsdp', 'head'))
- rope_key_grad: float32 [2048, 64], P(('fsdp', 'head'))
- key_up_grad: float32 [512, 2048], P('fsdp', 'head')
- value_up_grad: float32 [512, 2048], P('fsdp', 'head')
Inputs may be any that keep to these rules, and one draw needn't show every extreme that they name: bounds[s, 0] is the length of sequence s's image prefix, attended in both directions, and bounds[s, 1] its number of valid tokens; 1 <= bounds[s, 0] < 128 < bounds[s, 1]; some sequence has all 256 tokens valid.
All inputs are finite; a program needn't handle non-finite values.
Results may differ from a plain program's by a relative error of at most 0.0003.
Values sent between devices are 32-bit elements; how exact they have to be, the bound alone decides.
No kernel may reach another device: no remote copies, remote signals or barrier semaphores. Data moves between devices by JAX's collectives and lax.ppermute only.
A program may use at most 64 MiB of HBM per device.

v0:
```python
import functools

import jax
import jax.numpy as jnp
from jax import lax
from jax.experimental import pallas as pl
from jax.experimental.pallas import tpu as pltpu
from jax.sharding import PartitionSpec as P

NOPE = 128
ROPE = 64
VHEAD = 128
F32 = jnp.float32
BF16 = jnp.bfloat16


HBM = pl.BlockSpec(memory_space=pltpu.HBM)
VMEM = pl.BlockSpec(memory_space=pltpu.VMEM)
SMEM = pl.BlockSpec(memory_space=pltpu.SMEM)


def split(x):
    high = x.astype(BF16)
    return high, (x - high.astype(F32)).astype(BF16)


def product(left, right, left_dim, right_dim):
    dims = (((left_dim,), (right_dim,)), ((), ()))
    dot = functools.partial(lax.dot_general, dimension_numbers=dims, preferred_element_type=F32)
    return dot(left[0], right[0]) + (dot(left[0], right[1]) + dot(left[1], right[0]))


def columns(pair, start, size):
    return pair[0][:, start : start + size], pair[1][:, start : start + size]


def rows_at(index, rows):
    return pl.ds(pl.multiple_of(index * rows, 8), rows)


def pack_tokens(rows, lat, out_ref, wide, narrow):
    folds = lat // ROPE
    fold = rows // folds
    out_ref[:rows, :] = wide
    for part in range(folds):
        out_ref[rows : rows + fold, part * ROPE : (part + 1) * ROPE] = narrow[part * fold : (part + 1) * fold, :]


def unpack_narrow(rows, lat, block):
    folds = lat // ROPE
    fold = rows // folds
    return jnp.concatenate([block[rows : rows + fold, part * ROPE : (part + 1) * ROPE] for part in range(folds)], axis=0)


def pack_kernel(latent_ref, rope_ref, key_ref, value_ref, tokens_out, ups_out, rope, sems):
    rows, lat = latent_ref.shape
    rows_up = key_ref.shape[0]
    copies = [
        pltpu.make_async_copy(rope_ref, rope, sems.at[0]),
        pltpu.make_async_copy(key_ref, ups_out.at[pl.ds(0, rows_up)], sems.at[1]),
        pltpu.make_async_copy(value_ref, ups_out.at[pl.ds(rows_up, rows_up)], sems.at[2]),
        pltpu.make_async_copy(latent_ref, tokens_out.at[pl.ds(0, rows)], sems.at[3]),
    ]
    for copy in copies:
        copy.start()
    copies[0].wait()
    folds = lat // ROPE
    fold = rows // folds
    for part in range(folds):
        tokens_out[rows : rows + fold, part * ROPE : (part + 1) * ROPE] = rope[part * fold : (part + 1) * fold, :]
    for copy in copies[1:]:
        copy.wait()


def attention_kernel(ways, chips, place_ref, limit_ref, *refs):
    token_refs, refs = refs[:ways], refs[ways:]
    up_refs, refs = refs[: 2 * chips], refs[2 * chips :]
    nope_hbm, rope_hbm, cot_hbm, nope_out, rope_out = refs[:5]
    share_refs, refs = refs[5 : 5 + ways], refs[5 + ways :]
    keep_refs, refs = refs[:chips], refs[chips:]
    (send_ref, latent_all, shared_all, key_all, value_all, up_grad,
     nope_ref, rope_ref, cot_ref, nope_grad, rope_grad, sems) = refs
    length, width = nope_ref.shape
    lat = latent_all.shape[1]
    rows = length // ways
    rows_up = up_refs[0].shape[0] // 2
    head_count = width // NOPE
    factor = (NOPE + ROPE) ** (-0.5)
    mine, row = place_ref[0], place_ref[1]

    loads = [
        pltpu.make_async_copy(nope_hbm, nope_ref, sems.at[0]),
        pltpu.make_async_copy(rope_hbm, rope_ref, sems.at[1]),
        pltpu.make_async_copy(cot_hbm, cot_ref, sems.at[2]),
    ]
    for copy in loads:
        copy.start()

    for step in range(ways):
        owner = lax.rem(mine + (ways - step), ways)
        block = token_refs[step][...]
        latent_all[rows_at(owner, rows), :] = block[:rows, :]
        shared_all[rows_at(owner, rows), :] = unpack_narrow(rows, lat, block)
    for step in range(2 * chips):
        at = rows_at(jnp.bitwise_xor(row, step), rows_up)
        key_all[at, :] = up_refs[step][:rows_up, :]
        value_all[at, :] = up_refs[step][rows_up:, :]

    latent, shared = split(latent_all[...]), split(shared_all[...])
    key_up, value_up = split(key_all[...]), split(value_all[...])
    key_rows = split(product(latent, key_up, 1, 0))
    value_rows = split(product(latent, value_up, 1, 0))

    query_pos = lax.broadcasted_iota(jnp.int32, (length, length), 0)
    key_pos = lax.broadcasted_iota(jnp.int32, (length, length), 1)
    visible = (key_pos < limit_ref[0, 1]) & ((key_pos <= query_pos) | (key_pos < limit_ref[0, 0]))
    for copy in loads:
        copy.wait()

    key_grads, value_grads, stores = [], [], []
    shared_grad = jnp.zeros((length, ROPE), F32)
    for head in range(head_count):
        nope = split(nope_ref[:, head * NOPE : (head + 1) * NOPE])
        rope = split(rope_ref[:, head * ROPE : (head + 1) * ROPE])
        cot = split(cot_ref[:, head * VHEAD : (head + 1) * VHEAD])
        keys = columns(key_rows, head * NOPE, NOPE)
        values = columns(value_rows, head * VHEAD, VHEAD)
        scores = (product(nope, keys, 1, 1) + product(rope, shared, 1, 1)) * factor
        scores = jnp.where(visible, scores, -jnp.inf)
        weight = jnp.exp(scores - jnp.max(scores, axis=1, keepdims=True))
        attend = weight / jnp.sum(weight, axis=1, keepdims=True)
        grad_attend = product(cot, values, 1, 1)
        row_dot = jnp.sum(attend * grad_attend, axis=1, keepdims=True)
        grad_scores = split(attend * (grad_attend - row_dot) * factor)
        attend = split(attend)
        value_grads.append(product(attend, cot, 0, 0))
        nope_grad[:, head * NOPE : (head + 1) * NOPE] = product(grad_scores, keys, 1, 0)
        rope_grad[:, head * ROPE : (head + 1) * ROPE] = product(grad_scores, shared, 1, 0)
        key_grads.append(product(grad_scores, nope, 0, 0))
        shared_grad = shared_grad + product(grad_scores, rope, 0, 0)
    stores = [
        pltpu.make_async_copy(nope_grad, nope_out, sems.at[0]),
        pltpu.make_async_copy(rope_grad, rope_out, sems.at[1]),
    ]
    for copy in stores:
        copy.start()
    key_grad = split(jnp.concatenate(key_grads, axis=1))
    value_grad = split(jnp.concatenate(value_grads, axis=1))

    latent_all[...] = product(key_grad, key_up, 1, 1) + product(value_grad, value_up, 1, 1)
    shared_all[...] = shared_grad
    for step in range(ways):
        at = rows_at(lax.rem(mine + step, ways), rows)
        pack_tokens(rows, lat, share_refs[step], latent_all[at, :], shared_all[at, :])

    up_grad[:, :width] = product(latent, key_grad, 0, 0)
    up_grad[:, width:] = product(latent, value_grad, 0, 0)
    for step in range(chips):
        keep_refs[step][...] = up_grad[rows_at(jnp.bitwise_xor(row, 2 * step), rows_up), :]
        send_ref[step, :, :] = up_grad[rows_at(jnp.bitwise_xor(row, 2 * step + 1), rows_up), :]
    for copy in stores:
        copy.wait()


def join_kernel(chips, *refs):
    received = refs[0]
    for step in range(chips):
        refs[1 + chips + step][...] = refs[1 + step][...] + received[step, :, :]


def token_sum_kernel(ways, *refs):
    latent_out, rope_out = refs[ways:]
    rows, lat = latent_out.shape
    total = refs[0][...]
    for step in range(1, ways):
        total = total + refs[step][...]
    latent_out[...] = total[:rows, :]
    rope_out[...] = unpack_narrow(rows, lat, total)


def up_sum_kernel(chips, *refs):
    key_out, value_out = refs[chips:]
    width = key_out.shape[1]
    total = refs[0][...]
    for step in range(1, chips):
        total = total + refs[step][...]
    key_out[...] = total[:, :width]
    value_out[...] = total[:, width:]


def vmem(*arrays):
    return [pltpu.with_memory_space_constraint(array, pltpu.VMEM) for array in arrays]


def stored(*arrays):
    return [pltpu.with_memory_space_constraint(array, pltpu.HBM) for array in arrays]


def hbm(*dims):
    return pltpu.HBM(dims, F32)


def limit(mebibytes):
    return pltpu.CompilerParams(vmem_limit_bytes=mebibytes << 20)


def on_device(fsdp, ways, query_nope, query_rope, latent, rope_key, cotangent, bounds, key_up, value_up):
    chips = fsdp // 2
    rows, lat = latent.shape
    rows_up, width = key_up.shape
    length = query_nope.shape[0]
    packed = rows + rows * ROPE // lat
    dma = pltpu.SemaphoreType.DMA

    def swap(x, step):
        return lax.ppermute(x, "fsdp", [(i, i ^ step) for i in range(fsdp)])

    def shift(x, step):
        return lax.ppermute(x, "head", [(i, (i + step) % ways) for i in range(ways)])

    tokens, ups = pl.pallas_call(
        pack_kernel, out_shape=(pltpu.VMEM((packed, lat), F32), pltpu.VMEM((2 * rows_up, width), F32)),
        in_specs=[HBM] * 4, out_specs=[VMEM] * 2,
        scratch_shapes=[pltpu.VMEM((rows, ROPE), F32), dma((4,))],
        compiler_params=limit(4), name="pack",
    )(*stored(latent, rope_key, key_up, value_up))
    token_blocks = [tokens] + [shift(tokens, step) for step in range(1, ways)]
    even = [ups] + [swap(ups, 2 * step) for step in range(1, chips)]
    odd = [swap(block, 1) for block in even]
    up_blocks = [block for pair in zip(even, odd) for block in pair]

    place = jnp.stack([lax.axis_index("head"), lax.axis_index("fsdp")]).astype(jnp.int32)
    out = pl.pallas_call(
        functools.partial(attention_kernel, ways, chips),
        out_shape=(
            hbm(length, width), hbm(*query_rope.shape), *([pltpu.VMEM((packed, lat), F32)] * ways),
            *([pltpu.VMEM((rows_up, 2 * width), F32)] * chips), pltpu.VMEM((chips, rows_up, 2 * width), F32),
        ),
        in_specs=[SMEM] * 2 + [VMEM] * (ways + fsdp) + [HBM] * 3,
        out_specs=[HBM] * 2 + [VMEM] * (ways + chips + 1),
        scratch_shapes=[
            pltpu.VMEM((length, lat), F32), pltpu.VMEM((length, ROPE), F32),
            pltpu.VMEM((lat, width), F32), pltpu.VMEM((lat, width), F32), pltpu.VMEM((lat, 2 * width), F32),
            pltpu.VMEM((length, width), F32), pltpu.VMEM(query_rope.shape, F32), pltpu.VMEM((length, width), F32),
            pltpu.VMEM((length, width), F32), pltpu.VMEM(query_rope.shape, F32), dma((3,)),
        ],
        compiler_params=limit(28), name="attention",
    )(place, bounds, *vmem(*token_blocks, *up_blocks), *stored(query_nope, query_rope, cotangent))
    nope_grad, rope_grad = out[:2]
    shares, keep, send = out[2 : 2 + ways], out[2 + ways : 2 + ways + chips], out[-1]

    received = swap(send, 1)
    joined = pl.pallas_call(
        functools.partial(join_kernel, chips), out_shape=[pltpu.VMEM((rows_up, 2 * width), F32)] * chips,
        in_specs=[VMEM] * (1 + chips), out_specs=[VMEM] * chips, compiler_params=limit(4), name="join",
    )(*vmem(received, *keep))
    arrived = [joined[0]] + [swap(joined[step], 2 * step) for step in range(1, chips)]
    pieces = [shares[0]] + [shift(shares[step], step) for step in range(1, ways)]
    latent_grad, rope_key_grad = pl.pallas_call(
        functools.partial(token_sum_kernel, ways), out_shape=(hbm(rows, lat), hbm(rows, ROPE)),
        in_specs=[VMEM] * ways, out_specs=[VMEM] * 2, compiler_params=limit(4), name="token_sum",
    )(*vmem(*pieces))
    key_up_grad, value_up_grad = pl.pallas_call(
        functools.partial(up_sum_kernel, chips), out_shape=(hbm(rows_up, width), hbm(rows_up, width)),
        in_specs=[VMEM] * chips, out_specs=[VMEM] * 2, compiler_params=limit(4), name="up_sum",
    )(*vmem(*arrived))
    return nope_grad, rope_grad, latent_grad, rope_key_grad, key_up_grad, value_up_grad


def solution(mesh):
    fsdp, ways = mesh.shape["fsdp"], mesh.shape["head"]

    def body(*args):
        return on_device(fsdp, ways, *args)

    return jax.shard_map(
        body,
        mesh=mesh,
        in_specs=(
            P("fsdp", "head"),
            P("fsdp", "head"),
            P(("fsdp", "head"), None),
            P(("fsdp", "head"), None),
            P("fsdp", "head"),
            P("fsdp", None),
            P("fsdp", "head"),
            P("fsdp", "head"),
        ),
        out_specs=(
            P("fsdp", "head"),
            P("fsdp", "head"),
            P(("fsdp", "head"), None),
            P(("fsdp", "head"), None),
            P("fsdp", "head"),
            P("fsdp", "head"),
        ),
        check_vma=False,
    )
```

profile of v0, /device:TPU:0, one launch (start us, length us, event | category | flops | bytes accessed | tf_op | source)
XLA Modules:
  0.0 54.9 jit_solution(3805762764057560440)
XLA Ops:
  0.6 1.1 %pack.1 = (f32[72,512]{1,0:T(8,128)S(1)}, f32[128,512]{1,0:T(8,128)S(1)}) custom-call(f32[64,512]{1,0:T(8,128)} %latent_ref.1, f32[64,64]{1,0:T(8,128)} %rope_ref.1, f32[64,512]{1,0:T(8,128)} %key_ref.1, f32[64,512]{1,0:T(8,128)} %value_ref.1), custom_call_target="tpu_custom_call" | custom-call | tf_op jit(solution)/shard_map/pack/pallas_call | solution.py:221
  1.7 4.0 %collective-permute-start.8 = (f32[128,512]{1,0:T(8,128)S(1)}, f32[128,512]{1,0:T(8,128)S(1)}, u32[]{:S(2)}, u32[]{:S(2)}) collective-permute-start(f32[128,512]{1,0:T(8,128)S(1)} %get-tuple-element.28.refs_4_), channel_id=1, source_target_pairs={{0,24},{4,28},{8,16},{12,20},{16,8},{20,12},{24,0},{28,4},{1,25},{... | collective-permute-start | bytes 786440 | tf_op jit(solution)/shard_map/ppermute | solution.py:216
  5.7 0.5 collective-permute-start.6
  6.2 0.1 collective-permute-start.4
  6.4 4.0 %collective-permute-start.2 = (f32[72,512]{1,0:T(8,128)S(1)}, f32[72,512]{1,0:T(8,128)S(1)}, u32[]{:S(2)}, u32[]{:S(2)}) collective-permute-start(f32[72,512]{1,0:T(8,128)S(1)} %get-tuple-element.27.refs_0_), channel_id=1, source_target_pairs={{0,3},{1,0},{2,1},{3,2},{4,7},{5,4},{6,5},{7,6},{8,11},{9,8},{10,9... | collective-permute-start | bytes 442376 | tf_op jit(solution)/shard_map/ppermute | solution.py:219
  10.4 3.9 %collective-permute-done.2.refs_3_ = f32[72,512]{1,0:T(8,128)S(1)} collective-permute-done((f32[72,512]{1,0:T(8,128)S(1)}, f32[72,512]{1,0:T(8,128)S(1)}, u32[]{:S(2)}, u32[]{:S(2)}) %collective-permute-start.2) | collective-permute-done | bytes 147488 | tf_op jit(solution)/shard_map/ppermute | solution.py:219
  14.2 0.0 collective-permute-start.3
  14.3 0.5 collective-permute-start.9
  14.8 2.9 %collective-permute-done.6.refs_8_ = f32[128,512]{1,0:T(8,128)S(1)} collective-permute-done((f32[128,512]{1,0:T(8,128)S(1)}, f32[128,512]{1,0:T(8,128)S(1)}, u32[]{:S(2)}, u32[]{:S(2)}) %collective-permute-start.6) | collective-permute-done | bytes 262176 | tf_op jit(solution)/shard_map/ppermute | solution.py:216
  17.6 0.0 collective-permute-start.7
  17.7 0.3 collective-permute-done.4.refs_6_
  17.9 0.2 collective-permute-start.5
  18.2 1.1 %collective-permute-done.1.refs_2_ = f32[72,512]{1,0:T(8,128)S(1)} collective-permute-done((f32[72,512]{1,0:T(8,128)S(1)}, f32[72,512]{1,0:T(8,128)S(1)}, u32[]{:S(2)}, u32[]{:S(2)}) %collective-permute-start.1) | collective-permute-done | bytes 147488 | tf_op jit(solution)/shard_map/ppermute | solution.py:219
  19.2 0.7 %collective-permute-start = (f32[72,512]{1,0:T(8,128)S(1)}, f32[72,512]{1,0:T(8,128)S(1)}, u32[]{:S(2)}, u32[]{:S(2)}) collective-permute-start(f32[72,512]{1,0:T(8,128)S(1)} %get-tuple-element.27.refs_0_), channel_id=1, source_target_pairs={{0,1},{1,2},{2,3},{3,0},{4,5},{5,6},{6,7},{7,4},{8,9},{9,10},{10,1... | collective-permute-start | bytes 442376 | tf_op jit(solution)/shard_map/ppermute | solution.py:219
  19.9 0.1 pad_add_fusion.place_ref
  20.0 6.2 %collective-permute-done.refs_1_ = f32[72,512]{1,0:T(8,128)S(1)} collective-permute-done((f32[72,512]{1,0:T(8,128)S(1)}, f32[72,512]{1,0:T(8,128)S(1)}, u32[]{:S(2)}, u32[]{:S(2)}) %collective-permute-start) | collective-permute-done | bytes 147488 | tf_op jit(solution)/shard_map/ppermute | solution.py:219
  26.2 9.8 %attention.1 = (f32[256,512]{1,0:T(8,128)}, f32[256,256]{1,0:T(8,128)}, f32[72,512]{1,0:T(8,128)S(1)}, f32[72,512]{1,0:T(8,128)S(1)}, f32[72,512]{1,0:T(8,128)S(...) custom-call(s32[2]{0:T(128)S(1)} %pad_add_fusion.place_ref, ...), custom_call_target="tpu_custom_call" | custom-call | tf_op jit(solution)/shard_map/attention/pallas_call | solution.py:233
  36.1 0.1 collective-permute-start.13
  36.1 0.1 collective-permute-start.10
  36.2 2.6 %collective-permute-done.13.refs_0_ = f32[4,64,1024]{2,1,0:T(8,128)S(1)} collective-permute-done((f32[4,64,1024]{2,1,0:T(8,128)S(1)}, f32[4,64,1024]{2,1,0:T(8,128)S(1)}, u32[]{:S(2)}, u32[]{:S(2)}) %collective-permute-start.13) | collective-permute-done | bytes 1048608 | tf_op jit(solution)/shard_map/ppermute | solution.py:216
  38.8 0.1 join.1
  38.9 1.6 %collective-permute-start.14 = (f32[64,1024]{1,0:T(8,128)S(1)}, f32[64,1024]{1,0:T(8,128)S(1)}, u32[]{:S(2)}, u32[]{:S(2)}) collective-permute-start(f32[64,1024]{1,0:T(8,128)S(1)} %get-tuple-element.43), channel_id=1, source_target_pairs={{0,8},{4,12},{8,0},{12,4},{16,24},{20,28},{24,16},{28,20},{1,9},{5... | collective-permute-start | bytes 786440 | tf_op jit(solution)/shard_map/ppermute | solution.py:216
  40.5 1.5 %collective-permute-start.15 = (f32[64,1024]{1,0:T(8,128)S(1)}, f32[64,1024]{1,0:T(8,128)S(1)}, u32[]{:S(2)}, u32[]{:S(2)}) collective-permute-start(f32[64,1024]{1,0:T(8,128)S(1)} %get-tuple-element.44), channel_id=1, source_target_pairs={{0,16},{4,20},{8,24},{12,28},{16,0},{20,4},{24,8},{28,12},{1,17},{... | collective-permute-start | bytes 786440 | tf_op jit(solution)/shard_map/ppermute | solution.py:216
  42.0 0.5 collective-permute-start.16
  42.5 0.6 %collective-permute-start.11 = (f32[72,512]{1,0:T(8,128)S(1)}, f32[72,512]{1,0:T(8,128)S(1)}, u32[]{:S(2)}, u32[]{:S(2)}) collective-permute-start(f32[72,512]{1,0:T(8,128)S(1)} %get-tuple-element.33), channel_id=1, source_target_pairs={{0,2},{1,3},{2,0},{3,1},{4,6},{5,7},{6,4},{7,5},{8,10},{9,11},{10,... | collective-permute-start | bytes 442376 | tf_op jit(solution)/shard_map/ppermute | solution.py:219
  43.1 1.1 %collective-permute-done.10.refs_1_ = f32[72,512]{1,0:T(8,128)S(1)} collective-permute-done((f32[72,512]{1,0:T(8,128)S(1)}, f32[72,512]{1,0:T(8,128)S(1)}, u32[]{:S(2)}, u32[]{:S(2)}) %collective-permute-start.10) | collective-permute-done | bytes 147488 | tf_op jit(solution)/shard_map/ppermute | solution.py:219
  44.2 0.2 collective-permute-start.12
  44.4 6.6 %collective-permute-done.11.refs_2_ = f32[72,512]{1,0:T(8,128)S(1)} collective-permute-done((f32[72,512]{1,0:T(8,128)S(1)}, f32[72,512]{1,0:T(8,128)S(1)}, u32[]{:S(2)}, u32[]{:S(2)}) %collective-permute-start.11) | collective-permute-done | bytes 147488 | tf_op jit(solution)/shard_map/ppermute | solution.py:219
  51.0 1.6 %collective-permute-done.12.refs_3_ = f32[72,512]{1,0:T(8,128)S(1)} collective-permute-done((f32[72,512]{1,0:T(8,128)S(1)}, f32[72,512]{1,0:T(8,128)S(1)}, u32[]{:S(2)}, u32[]{:S(2)}) %collective-permute-start.12) | collective-permute-done | bytes 147488 | tf_op jit(solution)/shard_map/ppermute | solution.py:219
  52.6 0.7 %token_sum.1 = (f32[64,512]{1,0:T(8,128)}, f32[64,64]{1,0:T(8,128)}) custom-call(f32[72,512]{1,0:T(8,128)S(1)} %get-tuple-element.31.refs_0_, f32[72,512]{1,0:T(8,128)S(1)} %collective-permute-done.10.refs_1_, f32[72,512]{1,0:T(8,128)S(1)} %collective-permute-done.11.refs_2_, f32[72,512]{1,0:T(8,128)S(1)} %collective-permute-done.12.refs_3_), custom_call_target="tpu_custom_call" | custom-call | tf_op jit(solution)/shard_map/token_sum/pallas_call | solution.py:259
  53.3 0.9 %collective-permute-done.15.refs_2_ = f32[64,1024]{1,0:T(8,128)S(1)} collective-permute-done((f32[64,1024]{1,0:T(8,128)S(1)}, f32[64,1024]{1,0:T(8,128)S(1)}, u32[]{:S(2)}, u32[]{:S(2)}) %collective-permute-start.15) | collective-permute-done | bytes 262176 | tf_op jit(solution)/shard_map/ppermute | solution.py:216
  54.2 0.7 %up_sum.1 = (f32[64,512]{1,0:T(8,128)}, f32[64,512]{1,0:T(8,128)}) custom-call(f32[64,1024]{1,0:T(8,128)S(1)} %get-tuple-element.42.refs_0_, f32[64,1024]{1,0:T(8,128)S(1)} %collective-permute-done.14.refs_1_, f32[64,1024]{1,0:T(8,128)S(1)} %collective-permute-done.15.refs_2_, f32[64,1024]{1,0:T(8,128)S(1)} %collective-permute-done.16.refs_3_), custom_call_target="tpu_custom_call" | custom-call | tf_op jit(solution)/shard_map/up_sum/pallas_call | solution.py:263
  (10 shorter events, 0.0 us)
Async XLA Ops:
  1.7 12.5 %collective-permute-start.8 = (f32[128,512]{1,0:T(8,128)S(1)}, f32[128,512]{1,0:T(8,128)S(1)}, u32[]{:S(2)}, u32[]{:S(2)}) collective-permute-start(f32[128,512]{1,0:T(8,128)S(1)} %get-tuple-element.28.refs_4_), channel_id=1, source_target_pairs={{0,24},{4,28},{8,16},{12,20},{16,8},{20,12},{24,0},{28,4},{1,25},{... | collective-permute-start | bytes 786440 | tf_op jit(solution)/shard_map/ppermute | solution.py:216
  5.7 11.9 %collective-permute-start.6 = (f32[128,512]{1,0:T(8,128)S(1)}, f32[128,512]{1,0:T(8,128)S(1)}, u32[]{:S(2)}, u32[]{:S(2)}) collective-permute-start(f32[128,512]{1,0:T(8,128)S(1)} %get-tuple-element.28.refs_4_), channel_id=1, source_target_pairs={{0,16},{4,20},{8,24},{12,28},{16,0},{20,4},{24,8},{28,12},{1,17},{... | collective-permute-start | bytes 786440 | tf_op jit(solution)/shard_map/ppermute | solution.py:216
  6.2 11.7 %collective-permute-start.4 = (f32[128,512]{1,0:T(8,128)S(1)}, f32[128,512]{1,0:T(8,128)S(1)}, u32[]{:S(2)}, u32[]{:S(2)}) collective-permute-start(f32[128,512]{1,0:T(8,128)S(1)} %get-tuple-element.28.refs_4_), channel_id=1, source_target_pairs={{0,8},{4,12},{8,0},{12,4},{16,24},{20,28},{24,16},{28,20},{1,9},{5... | collective-permute-start | bytes 786440 | tf_op jit(solution)/shard_map/ppermute | solution.py:216
  6.4 7.9 %collective-permute-start.2 = (f32[72,512]{1,0:T(8,128)S(1)}, f32[72,512]{1,0:T(8,128)S(1)}, u32[]{:S(2)}, u32[]{:S(2)}) collective-permute-start(f32[72,512]{1,0:T(8,128)S(1)} %get-tuple-element.27.refs_0_), channel_id=1, source_target_pairs={{0,3},{1,0},{2,1},{3,2},{4,7},{5,4},{6,5},{7,6},{8,11},{9,8},{10,9... | collective-permute-start | bytes 442376 | tf_op jit(solution)/shard_map/ppermute | solution.py:219
  10.4 8.9 %collective-permute-start.1 = (f32[72,512]{1,0:T(8,128)S(1)}, f32[72,512]{1,0:T(8,128)S(1)}, u32[]{:S(2)}, u32[]{:S(2)}) collective-permute-start(f32[72,512]{1,0:T(8,128)S(1)} %get-tuple-element.27.refs_0_), channel_id=1, source_target_pairs={{0,2},{1,3},{2,0},{3,1},{4,6},{5,7},{6,4},{7,5},{8,10},{9,11},{10,... | collective-permute-start | bytes 442376 | tf_op jit(solution)/shard_map/ppermute | solution.py:219
  14.2 11.9 %collective-permute-start.3 = (f32[128,512]{1,0:T(8,128)S(1)}, f32[128,512]{1,0:T(8,128)S(1)}, u32[]{:S(2)}, u32[]{:S(2)}) collective-permute-start(f32[128,512]{1,0:T(8,128)S(1)} %get-tuple-element.28.refs_4_), channel_id=1, source_target_pairs={{0,4},{4,0},{8,12},{12,8},{16,20},{20,16},{24,28},{28,24},{1,5},{5... | collective-permute-start | bytes 786440 | tf_op jit(solution)/shard_map/ppermute | solution.py:216
  14.3 11.9 %collective-permute-start.9 = (f32[128,512]{1,0:T(8,128)S(1)}, f32[128,512]{1,0:T(8,128)S(1)}, u32[]{:S(2)}, u32[]{:S(2)}) collective-permute-start(f32[128,512]{1,0:T(8,128)S(1)} %collective-permute-done.8.refs_10_), channel_id=1, source_target_pairs={{0,4},{4,0},{8,12},{12,8},{16,20},{20,16},{24,28},{28,24},{1,5},{5... | collective-permute-start | bytes 786440 | tf_op jit(solution)/shard_map/ppermute | solution.py:216
  17.6 8.5 %collective-permute-start.7 = (f32[128,512]{1,0:T(8,128)S(1)}, f32[128,512]{1,0:T(8,128)S(1)}, u32[]{:S(2)}, u32[]{:S(2)}) collective-permute-start(f32[128,512]{1,0:T(8,128)S(1)} %collective-permute-done.6.refs_8_), channel_id=1, source_target_pairs={{0,4},{4,0},{8,12},{12,8},{16,20},{20,16},{24,28},{28,24},{1,5},{5... | collective-permute-start | bytes 786440 | tf_op jit(solution)/shard_map/ppermute | solution.py:216
  17.9 8.3 %collective-permute-start.5 = (f32[128,512]{1,0:T(8,128)S(1)}, f32[128,512]{1,0:T(8,128)S(1)}, u32[]{:S(2)}, u32[]{:S(2)}) collective-permute-start(f32[128,512]{1,0:T(8,128)S(1)} %collective-permute-done.4.refs_6_), channel_id=1, source_target_pairs={{0,4},{4,0},{8,12},{12,8},{16,20},{20,16},{24,28},{28,24},{1,5},{5... | collective-permute-start | bytes 786440 | tf_op jit(solution)/shard_map/ppermute | solution.py:216
  19.2 6.9 %collective-permute-start = (f32[72,512]{1,0:T(8,128)S(1)}, f32[72,512]{1,0:T(8,128)S(1)}, u32[]{:S(2)}, u32[]{:S(2)}) collective-permute-start(f32[72,512]{1,0:T(8,128)S(1)} %get-tuple-element.27.refs_0_), channel_id=1, source_target_pairs={{0,1},{1,2},{2,3},{3,0},{4,5},{5,6},{6,7},{7,4},{8,9},{9,10},{10,1... | collective-permute-start | bytes 442376 | tf_op jit(solution)/shard_map/ppermute | solution.py:219
  19.9 6.3 %copy-start = (s32[1,2]{1,0:T(1,128)S(1)}, s32[1,2]{1,0:T(1,128)}, u32[]{:S(2)}) copy-start(s32[1,2]{1,0:T(1,128)} %limit_ref.1) | copy-start | bytes 28
  36.1 2.7 %collective-permute-start.13 = (f32[4,64,1024]{2,1,0:T(8,128)S(1)}, f32[4,64,1024]{2,1,0:T(8,128)S(1)}, u32[]{:S(2)}, u32[]{:S(2)}) collective-permute-start(f32[4,64,1024]{2,1,0:T(8,128)S(1)} %get-tuple-element.37), channel_id=1, source_target_pairs={{0,4},{4,0},{8,12},{12,8},{16,20},{20,16},{24,28},{28,24},{1,5},{5... | collective-permute-start | bytes 3145736 | tf_op jit(solution)/shard_map/ppermute | solution.py:216
  36.1 8.0 %collective-permute-start.10 = (f32[72,512]{1,0:T(8,128)S(1)}, f32[72,512]{1,0:T(8,128)S(1)}, u32[]{:S(2)}, u32[]{:S(2)}) collective-permute-start(f32[72,512]{1,0:T(8,128)S(1)} %get-tuple-element.32), channel_id=1, source_target_pairs={{0,1},{1,2},{2,3},{3,0},{4,5},{5,6},{6,7},{7,4},{8,9},{9,10},{10,1... | collective-permute-start | bytes 442376 | tf_op jit(solution)/shard_map/ppermute | solution.py:219
  38.9 14.4 %collective-permute-start.14 = (f32[64,1024]{1,0:T(8,128)S(1)}, f32[64,1024]{1,0:T(8,128)S(1)}, u32[]{:S(2)}, u32[]{:S(2)}) collective-permute-start(f32[64,1024]{1,0:T(8,128)S(1)} %get-tuple-element.43), channel_id=1, source_target_pairs={{0,8},{4,12},{8,0},{12,4},{16,24},{20,28},{24,16},{28,20},{1,9},{5... | collective-permute-start | bytes 786440 | tf_op jit(solution)/shard_map/ppermute | solution.py:216
  40.5 13.7 %collective-permute-start.15 = (f32[64,1024]{1,0:T(8,128)S(1)}, f32[64,1024]{1,0:T(8,128)S(1)}, u32[]{:S(2)}, u32[]{:S(2)}) collective-permute-start(f32[64,1024]{1,0:T(8,128)S(1)} %get-tuple-element.44), channel_id=1, source_target_pairs={{0,16},{4,20},{8,24},{12,28},{16,0},{20,4},{24,8},{28,12},{1,17},{... | collective-permute-start | bytes 786440 | tf_op jit(solution)/shard_map/ppermute | solution.py:216
  42.0 12.2 %collective-permute-start.16 = (f32[64,1024]{1,0:T(8,128)S(1)}, f32[64,1024]{1,0:T(8,128)S(1)}, u32[]{:S(2)}, u32[]{:S(2)}) collective-permute-start(f32[64,1024]{1,0:T(8,128)S(1)} %get-tuple-element.45), channel_id=1, source_target_pairs={{0,24},{4,28},{8,16},{12,20},{16,8},{20,12},{24,0},{28,4},{1,25},{... | collective-permute-start | bytes 786440 | tf_op jit(solution)/shard_map/ppermute | solution.py:216
  42.5 8.5 %collective-permute-start.11 = (f32[72,512]{1,0:T(8,128)S(1)}, f32[72,512]{1,0:T(8,128)S(1)}, u32[]{:S(2)}, u32[]{:S(2)}) collective-permute-start(f32[72,512]{1,0:T(8,128)S(1)} %get-tuple-element.33), channel_id=1, source_target_pairs={{0,2},{1,3},{2,0},{3,1},{4,6},{5,7},{6,4},{7,5},{8,10},{9,11},{10,... | collective-permute-start | bytes 442376 | tf_op jit(solution)/shard_map/ppermute | solution.py:219
  44.2 8.4 %collective-permute-start.12 = (f32[72,512]{1,0:T(8,128)S(1)}, f32[72,512]{1,0:T(8,128)S(1)}, u32[]{:S(2)}, u32[]{:S(2)}) collective-permute-start(f32[72,512]{1,0:T(8,128)S(1)} %get-tuple-element.34), channel_id=1, source_target_pairs={{0,3},{1,0},{2,1},{3,2},{4,7},{5,4},{6,5},{7,6},{8,11},{9,8},{10,9... | collective-permute-start | bytes 442376 | tf_op jit(solution)/shard_map/ppermute | solution.py:219
where the time goes:
time: 55.1 us; the launch traced here: 54.9 us
  waiting for transfers between devices  27 us (49%)
  starting transfers between devices  14.6 us (26%)
  Pallas kernels  12.5 us (23%)
  between operations  0.7 us (1%)
    ppermute x6, waiting for transfers between devices, shift(): lax.ppermute(x, 'head', [(i, (i + step) % ways) for i in range(ways)])  20.4 us
    pallas_call x1, Pallas kernels, on_device(): pl.pallas_call(functools.partial(attention_kernel, ways, chips), out_shap...  9.84 us
    ppermute x11, starting transfers between devices, swap(): return lax.ppermute(x, 'fsdp', [(i, i ^ step) for i in range(fsdp)])  9 us
    ppermute x11, waiting for transfers between devices, swap(): return lax.ppermute(x, 'fsdp', [(i, i ^ step) for i in range(fsdp)])  6.62 us
    ppermute x6, starting transfers between devices, shift(): lax.ppermute(x, 'head', [(i, (i + step) % ways) for i in range(ways)])  5.61 us
  transfers between devices with their start and end apart: 17, of which 10 were waited for; matrix products, arithmetic and copies ran while one was open for 0% of the time, Pallas kernels for 1%

commit v1 on v0

--- a/solution.py
+++ b/solution.py
@@ -32,6 +32,20 @@
 
 def columns(pair, start, size):
     return pair[0][:, start : start + size], pair[1][:, start : start + size]
+
+
+def keep_pair(refs, x):
+    pair = split(x)
+    refs[0][...], refs[1][...] = pair
+    return pair
+
+
+def paired(ways):
+    return ways & (ways - 1) == 0
+
+
+def partner(mine, step, ways):
+    return jnp.bitwise_xor(mine, step) if paired(ways) else lax.rem(mine + step, ways)
 
 
 def rows_at(index, rows):
@@ -72,94 +86,121 @@
         copy.wait()
 
 
-def attention_kernel(ways, chips, place_ref, limit_ref, *refs):
+def prepare_kernel(limit_ref, nope_ref, rope_ref, cot_ref, mask_ref, *refs):
+    factor = (NOPE + ROPE) ** (-0.5)
+    query_pos = lax.broadcasted_iota(jnp.int32, mask_ref.shape, 0)
+    key_pos = lax.broadcasted_iota(jnp.int32, mask_ref.shape, 1)
+    visible = (key_pos < limit_ref[0, 1]) & ((key_pos <= query_pos) | (key_pos < limit_ref[0, 0]))
+    mask_ref[...] = jnp.where(visible, 0.0, -jnp.inf)
+    keep_pair(refs[0:2], nope_ref[...] * factor)
+    keep_pair(refs[2:4], rope_ref[...] * factor)
+    keep_pair(refs[4:6], cot_ref[...])
+
+
+def attention_kernel(ways, chips, *refs):
     token_refs, refs = refs[:ways], refs[ways:]
     up_refs, refs = refs[: 2 * chips], refs[2 * chips :]
-    nope_hbm, rope_hbm, cot_hbm, nope_out, rope_out = refs[:5]
-    share_refs, refs = refs[5 : 5 + ways], refs[5 + ways :]
+    mask_ref, nope_refs, rope_refs, cot_refs, refs = refs[0], refs[1:3], refs[3:5], refs[5:7], refs[7:]
     keep_refs, refs = refs[:chips], refs[chips:]
-    (send_ref, latent_all, shared_all, key_all, value_all, up_grad,
-     nope_ref, rope_ref, cot_ref, nope_grad, rope_grad, sems) = refs
-    length, width = nope_ref.shape
+    send_ref, shared_grad_ref = refs[:2]
+    grad_scores_refs, key_rows_refs, shared_refs = refs[2:4], refs[4:6], refs[6:8]
+    key_grad_refs, value_grad_refs, key_up_refs, value_up_refs = refs[8:10], refs[10:12], refs[12:14], refs[14:16]
+    latent_all, shared_all, key_all, value_all, up_grad = refs[16:]
+    length, width = nope_refs[0].shape
     lat = latent_all.shape[1]
     rows = length // ways
     rows_up = up_refs[0].shape[0] // 2
     head_count = width // NOPE
-    factor = (NOPE + ROPE) ** (-0.5)
-    mine, row = place_ref[0], place_ref[1]
-
-    loads = [
-        pltpu.make_async_copy(nope_hbm, nope_ref, sems.at[0]),
-        pltpu.make_async_copy(rope_hbm, rope_ref, sems.at[1]),
-        pltpu.make_async_copy(cot_hbm, cot_ref, sems.at[2]),
-    ]
-    for copy in loads:
-        copy.start()
+    mine, row = lax.axis_index("head"), lax.axis_index("fsdp")
 
     for step in range(ways):
-        owner = lax.rem(mine + (ways - step), ways)
+        at = rows_at(partner(mine, step, ways), rows)
         block = token_refs[step][...]
-        latent_all[rows_at(owner, rows), :] = block[:rows, :]
-        shared_all[rows_at(owner, rows), :] = unpack_narrow(rows, lat, block)
+        latent_all[at, :] = block[:rows, :]
+        shared_all[at, :] = unpack_narrow(rows, lat, block)
     for step in range(2 * chips):
         at = rows_at(jnp.bitwise_xor(row, step), rows_up)
         key_all[at, :] = up_refs[step][:rows_up, :]
         value_all[at, :] = up_refs[step][rows_up:, :]
 
-    latent, shared = split(latent_all[...]), split(shared_all[...])
-    key_up, value_up = split(key_all[...]), split(value_all[...])
-    key_rows = split(product(latent, key_up, 1, 0))
+    latent = split(latent_all[...])
+    shared = keep_pair(shared_refs, shared_all[...])
+    key_up = keep_pair(key_up_refs, key_all[...])
+    value_up = keep_pair(value_up_refs, value_all[...])
+    key_rows = keep_pair(key_rows_refs, product(latent, key_up, 1, 0))
     value_rows = split(product(latent, value_up, 1, 0))
 
-    query_pos = lax.broadcasted_iota(jnp.int32, (length, length), 0)
-    key_pos = lax.broadcasted_iota(jnp.int32, (length, length), 1)
-    visible = (key_pos < limit_ref[0, 1]) & ((key_pos <= query_pos) | (key_pos < limit_ref[0, 0]))
-    for copy in loads:
-        copy.wait()
-
-    key_grads, value_grads, stores = [], [], []
-    shared_grad = jnp.zeros((length, ROPE), F32)
-    for head in range(head_count):
-        nope = split(nope_ref[:, head * NOPE : (head + 1) * NOPE])
-        rope = split(rope_ref[:, head * ROPE : (head + 1) * ROPE])
-        cot = split(cot_ref[:, head * VHEAD : (head + 1) * VHEAD])
+    def of_head(refs, head, size):
+        return refs[0][:, head * size : (head + 1) * size], refs[1][:, head * size : (head + 1) * size]
+
+    def front(head):
         keys = columns(key_rows, head * NOPE, NOPE)
         values = columns(value_rows, head * VHEAD, VHEAD)
-        scores = (product(nope, keys, 1, 1) + product(rope, shared, 1, 1)) * factor
-        scores = jnp.where(visible, scores, -jnp.inf)
+        scores = product(of_head(nope_refs, head, NOPE), keys, 1, 1)
+        scores = scores + product(of_head(rope_refs, head, ROPE), shared, 1, 1)
+        return scores + mask_ref[...], product(of_head(cot_refs, head, VHEAD), values, 1, 1)
+
+    def middle(head, scores, grad_attend):
         weight = jnp.exp(scores - jnp.max(scores, axis=1, keepdims=True))
-        attend = weight / jnp.sum(weight, axis=1, keepdims=True)
-        grad_attend = product(cot, values, 1, 1)
-        row_dot = jnp.sum(attend * grad_attend, axis=1, keepdims=True)
-        grad_scores = split(attend * (grad_attend - row_dot) * factor)
-        attend = split(attend)
-        value_grads.append(product(attend, cot, 0, 0))
-        nope_grad[:, head * NOPE : (head + 1) * NOPE] = product(grad_scores, keys, 1, 0)
-        rope_grad[:, head * ROPE : (head + 1) * ROPE] = product(grad_scores, shared, 1, 0)
-        key_grads.append(product(grad_scores, nope, 0, 0))
-        shared_grad = shared_grad + product(grad_scores, rope, 0, 0)
-    stores = [
-        pltpu.make_async_copy(nope_grad, nope_out, sems.at[0]),
-        pltpu.make_async_copy(rope_grad, rope_out, sems.at[1]),
-    ]
-    for copy in stores:
-        copy.start()
-    key_grad = split(jnp.concatenate(key_grads, axis=1))
-    value_grad = split(jnp.concatenate(value_grads, axis=1))
-
-    latent_all[...] = product(key_grad, key_up, 1, 1) + product(value_grad, value_up, 1, 1)
-    shared_all[...] = shared_grad
-    for step in range(ways):
-        at = rows_at(lax.rem(mine + step, ways), rows)
-        pack_tokens(rows, lat, share_refs[step], latent_all[at, :], shared_all[at, :])
+        attend = weight * (1.0 / jnp.sum(weight, axis=1, keepdims=True))
+        weighted = attend * grad_attend
+        grad_scores = keep_pair(
+            [ref.at[head] for ref in grad_scores_refs],
+            weighted - attend * jnp.sum(weighted, axis=1, keepdims=True),
+        )
+        return split(attend), grad_scores
+
+    def back(head, attend, grad_scores):
+        return (
+            product(attend, of_head(cot_refs, head, VHEAD), 0, 0),
+            product(grad_scores, of_head(nope_refs, head, NOPE), 0, 0),
+            product(grad_scores, of_head(rope_refs, head, ROPE), 0, 0),
+        )
+
+    value_grads, key_grads = [], []
+    shared_grad = jnp.zeros((length, ROPE), F32)
+    ready = front(0)
+    for head in range(head_count):
+        later = front(head + 1) if head + 1 < head_count else None
+        value_part, key_part, shared_part = back(head, *middle(head, *ready))
+        value_grads.append(value_part)
+        key_grads.append(key_part)
+        shared_grad = shared_grad + shared_part
+        ready = later
+    shared_grad_ref[...] = shared_grad
+    key_grad = keep_pair(key_grad_refs, jnp.concatenate(key_grads, axis=1))
+    value_grad = keep_pair(value_grad_refs, jnp.concatenate(value_grads, axis=1))
 
     up_grad[:, :width] = product(latent, key_grad, 0, 0)
     up_grad[:, width:] = product(latent, value_grad, 0, 0)
     for step in range(chips):
         keep_refs[step][...] = up_grad[rows_at(jnp.bitwise_xor(row, 2 * step), rows_up), :]
         send_ref[step, :, :] = up_grad[rows_at(jnp.bitwise_xor(row, 2 * step + 1), rows_up), :]
-    for copy in stores:
-        copy.wait()
+
+
+def share_kernel(ways, shared_grad_ref, *refs):
+    key_grad, value_grad, key_up, value_up = [
+        (refs[2 * which][...], refs[2 * which + 1][...]) for which in range(4)
+    ]
+    share_refs, latent_all = refs[8 : 8 + ways], refs[8 + ways]
+    rows = shared_grad_ref.shape[0] // ways
+    lat = latent_all.shape[1]
+    latent_all[...] = product(key_grad, key_up, 1, 1) + product(value_grad, value_up, 1, 1)
+    for step in range(ways):
+        at = rows_at(partner(lax.axis_index("head"), step, ways), rows)
+        pack_tokens(rows, lat, share_refs[step], latent_all[at, :], shared_grad_ref[at, :])
+
+
+def query_kernel(*refs):
+    high_ref, low_ref = refs[:2]
+    key_rows, shared = [(refs[2 * which][...], refs[2 * which + 1][...]) for which in (1, 2)]
+    nope_out, rope_out = refs[6:]
+    factor = (NOPE + ROPE) ** (-0.5)
+    for head in range(high_ref.shape[0]):
+        grad_scores = high_ref[head, :, :], low_ref[head, :, :]
+        keys = columns(key_rows, head * NOPE, NOPE)
+        nope_out[:, head * NOPE : (head + 1) * NOPE] = product(grad_scores, keys, 1, 0) * factor
+        rope_out[:, head * ROPE : (head + 1) * ROPE] = product(grad_scores, shared, 1, 0) * factor
 
 
 def join_kernel(chips, *refs):
@@ -216,7 +257,8 @@
         return lax.ppermute(x, "fsdp", [(i, i ^ step) for i in range(fsdp)])
 
     def shift(x, step):
-        return lax.ppermute(x, "head", [(i, (i + step) % ways) for i in range(ways)])
+        to = [(i, i ^ step if paired(ways) else (i + step) % ways) for i in range(ways)]
+        return lax.ppermute(x, "head", to)
 
     tokens, ups = pl.pallas_call(
         pack_kernel, out_shape=(pltpu.VMEM((packed, lat), F32), pltpu.VMEM((2 * rows_up, width), F32)),
@@ -224,30 +266,45 @@
         scratch_shapes=[pltpu.VMEM((rows, ROPE), F32), dma((4,))],
         compiler_params=limit(4), name="pack",
     )(*stored(latent, rope_key, key_up, value_up))
-    token_blocks = [tokens] + [shift(tokens, step) for step in range(1, ways)]
+    token_blocks = [tokens] + [shift(tokens, step if paired(ways) else ways - step) for step in range(1, ways)]
     even = [ups] + [swap(ups, 2 * step) for step in range(1, chips)]
     odd = [swap(block, 1) for block in even]
     up_blocks = [block for pair in zip(even, odd) for block in pair]
 
-    place = jnp.stack([lax.axis_index("head"), lax.axis_index("fsdp")]).astype(jnp.int32)
+    heads = width // NOPE
+    wide, square = (length, width), (lat, width)
+    pairs = [(heads, length, length), wide, (length, ROPE), wide, wide, square, square]
+    queries = pl.pallas_call(
+        prepare_kernel,
+        out_shape=[pltpu.VMEM((length, length), F32)]
+        + [pltpu.VMEM(dims, BF16) for dims in (wide, query_rope.shape, wide) for _ in range(2)],
+        in_specs=[SMEM] + [VMEM] * 3, out_specs=[VMEM] * 7, compiler_params=limit(8), name="prepare",
+    )(*stored(bounds, query_nope, query_rope, cotangent))
     out = pl.pallas_call(
         functools.partial(attention_kernel, ways, chips),
         out_shape=(
-            hbm(length, width), hbm(*query_rope.shape), *([pltpu.VMEM((packed, lat), F32)] * ways),
             *([pltpu.VMEM((rows_up, 2 * width), F32)] * chips), pltpu.VMEM((chips, rows_up, 2 * width), F32),
+            pltpu.VMEM((length, ROPE), F32), *[pltpu.VMEM(dims, BF16) for dims in pairs for _ in range(2)],
         ),
-        in_specs=[SMEM] * 2 + [VMEM] * (ways + fsdp) + [HBM] * 3,
-        out_specs=[HBM] * 2 + [VMEM] * (ways + chips + 1),
+        in_specs=[VMEM] * (ways + fsdp + 7),
+        out_specs=[VMEM] * (chips + 2 + 2 * len(pairs)),
         scratch_shapes=[
             pltpu.VMEM((length, lat), F32), pltpu.VMEM((length, ROPE), F32),
-            pltpu.VMEM((lat, width), F32), pltpu.VMEM((lat, width), F32), pltpu.VMEM((lat, 2 * width), F32),
-            pltpu.VMEM((length, width), F32), pltpu.VMEM(query_rope.shape, F32), pltpu.VMEM((length, width), F32),
-            pltpu.VMEM((length, width), F32), pltpu.VMEM(query_rope.shape, F32), dma((3,)),
+            pltpu.VMEM(square, F32), pltpu.VMEM(square, F32), pltpu.VMEM((lat, 2 * width), F32),
         ],
-        compiler_params=limit(28), name="attention",
-    )(place, bounds, *vmem(*token_blocks, *up_blocks), *stored(query_nope, query_rope, cotangent))
-    nope_grad, rope_grad = out[:2]
-    shares, keep, send = out[2 : 2 + ways], out[2 + ways : 2 + ways + chips], out[-1]
+        compiler_params=limit(24), name="attention",
+    )(*vmem(*token_blocks, *up_blocks, *queries))
+    keep, send, shared_grad, pairs = out[:chips], out[chips], out[chips + 1], out[chips + 2 :]
+
+    shares = pl.pallas_call(
+        functools.partial(share_kernel, ways), out_shape=[pltpu.VMEM((packed, lat), F32)] * ways,
+        in_specs=[VMEM] * 9, out_specs=[VMEM] * ways,
+        scratch_shapes=[pltpu.VMEM((length, lat), F32)], compiler_params=limit(8), name="share",
+    )(*vmem(shared_grad, *pairs[6:]))
+    nope_grad, rope_grad = pl.pallas_call(
+        query_kernel, out_shape=(hbm(*wide), hbm(*query_rope.shape)),
+        in_specs=[VMEM] * 6, out_specs=[VMEM] * 2, compiler_params=limit(8), name="query",
+    )(*vmem(*pairs[:6]))
 
     received = swap(send, 1)
     joined = pl.pallas_call(

time: 55.1 us -> 53.4 us (0.969); the launches traced: 54.9 us -> 52.6 us
  waiting for transfers between devices: 27 us -> 23 us
  starting transfers between devices: 14.6 us -> 16.7 us
    pallas_call x1, Pallas kernels: 9.84 us -> 5.15 us  [on_device(): pl.pallas_call(functools.partial(attention_kernel, ways, chips), out_shap...]
    pallas_call x0 -> x3, Pallas kernels: none -> 4.43 us  [the longest x1 1.78 us: on_device(): pl.pallas_call(query_kernel, out_shape=(hbm(*wide), hbm(*query_rope.shape...]
    ppermute x11, waiting for transfers between devices: 6.62 us -> 3.82 us  [swap(): return lax.ppermute(x, 'fsdp', [(i, i ^ step) for i in range(fsdp)])]
    ppermute x6, starting transfers between devices: 5.61 us -> 7.68 us  [shift(): return lax.ppermute(x, 'head', to)]
    ppermute x6, waiting for transfers between devices: 20.4 us -> 19.1 us  [shift(): return lax.ppermute(x, 'head', to)]
  transfers between devices with their start and end apart: 17 -> 17, of which waited for: 10 -> 7; matrix products, arithmetic and copies ran while one was open for 0% -> 0% of each run, Pallas kernels for 1% -> 10%
where the time goes in v1:
time: 53.4 us; the launch traced here: 52.6 us
  waiting for transfers between devices  23 us (43%)
  starting transfers between devices  16.7 us (31%)
  Pallas kernels  12.2 us (23%)
  between operations  0.71 us (1%)
    ppermute x6, waiting for transfers between devices, shift(): return lax.ppermute(x, 'head', to)  19.1 us
    ppermute x11, starting transfers between devices, swap(): return lax.ppermute(x, 'fsdp', [(i, i ^ step) for i in range(fsdp)])  9 us
    ppermute x6, starting transfers between devices, shift(): return lax.ppermute(x, 'head', to)  7.68 us
    pallas_call x1, Pallas kernels, on_device(): pl.pallas_call(functools.partial(attention_kernel, ways, chips), out_shap...  5.15 us
    ppermute x11, waiting for transfers between devices, swap(): return lax.ppermute(x, 'fsdp', [(i, i ^ step) for i in range(fsdp)])  3.82 us
    pallas_call x1, Pallas kernels, on_device(): pl.pallas_call(query_kernel, out_shape=(hbm(*wide), hbm(*query_rope.shape...  1.78 us
    pallas_call x1, Pallas kernels, on_device(): pl.pallas_call(prepare_kernel, out_shape=[pltpu.VMEM((length, length), F3...  1.6 us
    pallas_call x1, Pallas kernels, on_device(): pl.pallas_call(pack_kernel, out_shape=(pltpu.VMEM((packed, lat), F32), pl...  1.09 us
  transfers between devices with their start and end apart: 17, of which 7 were waited for; matrix products, arithmetic and copies ran while one was open for 0% of the time, Pallas kernels for 10%

profile of v1, /device:TPU:0, one launch (start us, length us, event | category | flops | bytes accessed | tf_op | source)
XLA Modules:
  0.0 52.6 jit_solution(9980679069487889696)
XLA Ops:
  0.6 1.1 %pack.1 = (f32[72,512]{1,0:T(8,128)S(1)}, f32[128,512]{1,0:T(8,128)S(1)}) custom-call(f32[64,512]{1,0:T(8,128)} %latent_ref.1, f32[64,64]{1,0:T(8,128)} %rope_ref.2, f32[64,512]{1,0:T(8,128)} %key_ref.1, f32[64,512]{1,0:T(8,128)} %value_ref.1), custom_call_target="tpu_custom_call" | custom-call | tf_op jit(solution)/shard_map/pack/pallas_call | solution.py:263
  1.7 4.0 %collective-permute-start.8 = (f32[128,512]{1,0:T(8,128)S(1)}, f32[128,512]{1,0:T(8,128)S(1)}, u32[]{:S(2)}, u32[]{:S(2)}) collective-permute-start(f32[128,512]{1,0:T(8,128)S(1)} %get-tuple-element.50.refs_4_), channel_id=1, source_target_pairs={{0,24},{4,28},{8,16},{12,20},{16,8},{20,12},{24,0},{28,4},{1,25},{... | collective-permute-start | bytes 786440 | tf_op jit(solution)/shard_map/ppermute | solution.py:257
  5.7 0.5 collective-permute-start.6
  6.2 0.1 collective-permute-start.4
  6.4 4.0 %collective-permute-start.2 = (f32[72,512]{1,0:T(8,128)S(1)}, f32[72,512]{1,0:T(8,128)S(1)}, u32[]{:S(2)}, u32[]{:S(2)}) collective-permute-start(f32[72,512]{1,0:T(8,128)S(1)} %get-tuple-element.49.refs_0_), channel_id=1, source_target_pairs={{0,3},{1,2},{2,1},{3,0},{4,7},{5,6},{6,5},{7,4},{8,11},{9,10},{10,... | collective-permute-start | bytes 442376 | tf_op jit(solution)/shard_map/ppermute | solution.py:261
  10.4 4.7 %collective-permute-done.2.refs_3_ = f32[72,512]{1,0:T(8,128)S(1)} collective-permute-done((f32[72,512]{1,0:T(8,128)S(1)}, f32[72,512]{1,0:T(8,128)S(1)}, u32[]{:S(2)}, u32[]{:S(2)}) %collective-permute-start.2) | collective-permute-done | bytes 147488 | tf_op jit(solution)/shard_map/ppermute | solution.py:261
  15.1 0.0 collective-permute-done.8.refs_10_
  15.1 0.5 collective-permute-start.9
  15.6 2.1 %collective-permute-done.6.refs_8_ = f32[128,512]{1,0:T(8,128)S(1)} collective-permute-done((f32[128,512]{1,0:T(8,128)S(1)}, f32[128,512]{1,0:T(8,128)S(1)}, u32[]{:S(2)}, u32[]{:S(2)}) %collective-permute-start.6) | collective-permute-done | bytes 262176 | tf_op jit(solution)/shard_map/ppermute | solution.py:257
  17.6 0.0 collective-permute-start.7
  17.7 0.3 collective-permute-done.4.refs_6_
  17.9 0.2 collective-permute-start.5
  18.2 3.8 %collective-permute-done.1.refs_2_ = f32[72,512]{1,0:T(8,128)S(1)} collective-permute-done((f32[72,512]{1,0:T(8,128)S(1)}, f32[72,512]{1,0:T(8,128)S(1)}, u32[]{:S(2)}, u32[]{:S(2)}) %collective-permute-start.1) | collective-permute-done | bytes 147488 | tf_op jit(solution)/shard_map/ppermute | solution.py:261
  22.0 1.6 %prepare.1 = (f32[256,256]{1,0:T(8,128)S(1)}, bf16[256,512]{1,0:T(8,128)(2,1)S(1)}, bf16[256,512]{1,0:T(8,128)(2,1)S(1)}, bf16[256,256]{1,0:T(8,128)(2,1)S(1)}, ...) custom-call(s32[1,2]{1,0:T(1,128)} %limit_ref.1, f32[256,512]{1,0:T(8,128)} %nope_ref.1, ...), custom_call_target="tpu_custom_call" | custom-call | tf_op jit(solution)/shard_map/prepare/pallas_call | solution.py:277
  23.6 3.5 %collective-permute-done.refs_1_ = f32[72,512]{1,0:T(8,128)S(1)} collective-permute-done((f32[72,512]{1,0:T(8,128)S(1)}, f32[72,512]{1,0:T(8,128)S(1)}, u32[]{:S(2)}, u32[]{:S(2)}) %collective-permute-start) | collective-permute-done | bytes 147488 | tf_op jit(solution)/shard_map/ppermute | solution.py:261
  27.1 0.0 collective-permute-done.3.refs_5_
  27.1 0.0 collective-permute-done.9.refs_11_
  27.2 5.1 %attention.1 = (f32[64,1024]{1,0:T(8,128)S(1)}, f32[64,1024]{1,0:T(8,128)S(1)}, f32[64,1024]{1,0:T(8,128)S(1)}, f32[64,1024]{1,0:T(8,128)S(1)}, f32[4,64,1024]{2...) custom-call(f32[72,512]{1,0:T(8,128)S(1)} %get-tuple-element.49.refs, ...), custom_call_target="tpu_custom_call" | custom-call | tf_op jit(solution)/shard_map/attention/pallas_call | solution.py:283
  32.3 0.1 collective-permute-start.13
  32.4 1.1 %share.1 = (f32[72,512]{1,0:T(8,128)S(1)}, f32[72,512]{1,0:T(8,128)S(1)}, f32[72,512]{1,0:T(8,128)S(1)}, f32[72,512]{1,0:T(8,128)S(1)}) custom-call(f32[256,64]{1,0:T(8,128)S(1)} %get-tuple-element.66.shared_grad_ref, bf16[256,512]{1,0:T(8,128)(2,1)S(1)} %get-tuple-element.67.refs_0_, bf16[256,512]{1,0:T(8,128)(2,1)S(1)} %get-tuple-element.68.refs_1_, ...), custom_call_target="tpu_custom_call" | custom-call | tf_op jit(solution)/shard_map/share/pallas_call | solution.py:299
  33.5 0.1 collective-permute-start.10
  33.6 1.5 %collective-permute-done.13.refs_0_ = f32[4,64,1024]{2,1,0:T(8,128)S(1)} collective-permute-done((f32[4,64,1024]{2,1,0:T(8,128)S(1)}, f32[4,64,1024]{2,1,0:T(8,128)S(1)}, u32[]{:S(2)}, u32[]{:S(2)}) %collective-permute-start.13) | collective-permute-done | bytes 1048608 | tf_op jit(solution)/shard_map/ppermute | solution.py:257
  35.0 0.1 join.1
  35.2 1.6 %collective-permute-start.14 = (f32[64,1024]{1,0:T(8,128)S(1)}, f32[64,1024]{1,0:T(8,128)S(1)}, u32[]{:S(2)}, u32[]{:S(2)}) collective-permute-start(f32[64,1024]{1,0:T(8,128)S(1)} %get-tuple-element.87), channel_id=1, source_target_pairs={{0,8},{4,12},{8,0},{12,4},{16,24},{20,28},{24,16},{28,20},{1,9},{5... | collective-permute-start | bytes 786440 | tf_op jit(solution)/shard_map/ppermute | solution.py:257
  36.7 1.5 %collective-permute-start.15 = (f32[64,1024]{1,0:T(8,128)S(1)}, f32[64,1024]{1,0:T(8,128)S(1)}, u32[]{:S(2)}, u32[]{:S(2)}) collective-permute-start(f32[64,1024]{1,0:T(8,128)S(1)} %get-tuple-element.88), channel_id=1, source_target_pairs={{0,16},{4,20},{8,24},{12,28},{16,0},{20,4},{24,8},{28,12},{1,17},{... | collective-permute-start | bytes 786440 | tf_op jit(solution)/shard_map/ppermute | solution.py:257
  38.2 0.5 collective-permute-start.16
  38.7 1.7 %collective-permute-start.11 = (f32[72,512]{1,0:T(8,128)S(1)}, f32[72,512]{1,0:T(8,128)S(1)}, u32[]{:S(2)}, u32[]{:S(2)}) collective-permute-start(f32[72,512]{1,0:T(8,128)S(1)} %get-tuple-element.77), channel_id=1, source_target_pairs={{0,2},{1,3},{2,0},{3,1},{4,6},{5,7},{6,4},{7,5},{8,10},{9,11},{10,... | collective-permute-start | bytes 442376 | tf_op jit(solution)/shard_map/ppermute | solution.py:261
  40.4 1.8 %collective-permute-start.12 = (f32[72,512]{1,0:T(8,128)S(1)}, f32[72,512]{1,0:T(8,128)S(1)}, u32[]{:S(2)}, u32[]{:S(2)}) collective-permute-start(f32[72,512]{1,0:T(8,128)S(1)} %get-tuple-element.78), channel_id=1, source_target_pairs={{0,3},{1,2},{2,1},{3,0},{4,7},{5,6},{6,5},{7,4},{8,11},{9,10},{10,... | collective-permute-start | bytes 442376 | tf_op jit(solution)/shard_map/ppermute | solution.py:261
  42.3 1.8 %query.1 = (f32[256,512]{1,0:T(8,128)}, f32[256,256]{1,0:T(8,128)}) custom-call(bf16[4,256,256]{2,1,0:T(8,128)(2,1)S(1)} %get-tuple-element.58.refs_0_, bf16[4,256,256]{2,1,0:T(8,128)(2,1)S(1)} %get-tuple-element.59.refs_1_, bf16[256,512]{1,0:T(8,128)(2,1)S(1)} %get-tuple-element.60.refs_2_, bf16[256,512]{1,0:T(8,128)(2,1)S(1)} %get-tuple-element.61.refs_3_, ...), custom_call_target="tpu_custom_call" | custom-call | tf_op jit(solution)/shard_map/query/pallas_call | solution.py:304
  44.0 7.1 %collective-permute-done.11.refs_2_ = f32[72,512]{1,0:T(8,128)S(1)} collective-permute-done((f32[72,512]{1,0:T(8,128)S(1)}, f32[72,512]{1,0:T(8,128)S(1)}, u32[]{:S(2)}, u32[]{:S(2)}) %collective-permute-start.11) | collective-permute-done | bytes 147488 | tf_op jit(solution)/shard_map/ppermute | solution.py:261
  51.1 0.7 %token_sum.1 = (f32[64,512]{1,0:T(8,128)}, f32[64,64]{1,0:T(8,128)}) custom-call(f32[72,512]{1,0:T(8,128)S(1)} %get-tuple-element.75.refs_0_, f32[72,512]{1,0:T(8,128)S(1)} %collective-permute-done.10.refs_1_, f32[72,512]{1,0:T(8,128)S(1)} %collective-permute-done.11.refs_2_, f32[72,512]{1,0:T(8,128)S(1)} %collective-permute-done.12.refs_3_), custom_call_target="tpu_custom_call" | custom-call | tf_op jit(solution)/shard_map/token_sum/pallas_call | solution.py:316
  51.8 0.7 %up_sum.1 = (f32[64,512]{1,0:T(8,128)}, f32[64,512]{1,0:T(8,128)}) custom-call(f32[64,1024]{1,0:T(8,128)S(1)} %get-tuple-element.86.refs_0_, f32[64,1024]{1,0:T(8,128)S(1)} %collective-permute-done.14.refs_1_, f32[64,1024]{1,0:T(8,128)S(1)} %collective-permute-done.15.refs_2_, f32[64,1024]{1,0:T(8,128)S(1)} %collective-permute-done.16.refs_3_), custom_call_target="tpu_custom_call" | custom-call | tf_op jit(solution)/shard_map/up_sum/pallas_call | solution.py:320
  (10 shorter events, 0.0 us)
Async XLA Ops:
  1.7 13.3 %collective-permute-start.8 = (f32[128,512]{1,0:T(8,128)S(1)}, f32[128,512]{1,0:T(8,128)S(1)}, u32[]{:S(2)}, u32[]{:S(2)}) collective-permute-start(f32[128,512]{1,0:T(8,128)S(1)} %get-tuple-element.50.refs_4_), channel_id=1, source_target_pairs={{0,24},{4,28},{8,16},{12,20},{16,8},{20,12},{24,0},{28,4},{1,25},{... | collective-permute-start | bytes 786440 | tf_op jit(solution)/shard_map/ppermute | solution.py:257
  5.7 11.9 %collective-permute-start.6 = (f32[128,512]{1,0:T(8,128)S(1)}, f32[128,512]{1,0:T(8,128)S(1)}, u32[]{:S(2)}, u32[]{:S(2)}) collective-permute-start(f32[128,512]{1,0:T(8,128)S(1)} %get-tuple-element.50.refs_4_), channel_id=1, source_target_pairs={{0,16},{4,20},{8,24},{12,28},{16,0},{20,4},{24,8},{28,12},{1,17},{... | collective-permute-start | bytes 786440 | tf_op jit(solution)/shard_map/ppermute | solution.py:257
  6.2 11.7 %collective-permute-start.4 = (f32[128,512]{1,0:T(8,128)S(1)}, f32[128,512]{1,0:T(8,128)S(1)}, u32[]{:S(2)}, u32[]{:S(2)}) collective-permute-start(f32[128,512]{1,0:T(8,128)S(1)} %get-tuple-element.50.refs_4_), channel_id=1, source_target_pairs={{0,8},{4,12},{8,0},{12,4},{16,24},{20,28},{24,16},{28,20},{1,9},{5... | collective-permute-start | bytes 786440 | tf_op jit(solution)/shard_map/ppermute | solution.py:257
  6.4 8.7 %collective-permute-start.2 = (f32[72,512]{1,0:T(8,128)S(1)}, f32[72,512]{1,0:T(8,128)S(1)}, u32[]{:S(2)}, u32[]{:S(2)}) collective-permute-start(f32[72,512]{1,0:T(8,128)S(1)} %get-tuple-element.49.refs_0_), channel_id=1, source_target_pairs={{0,3},{1,2},{2,1},{3,0},{4,7},{5,6},{6,5},{7,4},{8,11},{9,10},{10,... | collective-permute-start | bytes 442376 | tf_op jit(solution)/shard_map/ppermute | solution.py:261
  10.4 11.6 %collective-permute-start.1 = (f32[72,512]{1,0:T(8,128)S(1)}, f32[72,512]{1,0:T(8,128)S(1)}, u32[]{:S(2)}, u32[]{:S(2)}) collective-permute-start(f32[72,512]{1,0:T(8,128)S(1)} %get-tuple-element.49.refs_0_), channel_id=1, source_target_pairs={{0,2},{1,3},{2,0},{3,1},{4,6},{5,7},{6,4},{7,5},{8,10},{9,11},{10,... | collective-permute-start | bytes 442376 | tf_op jit(solution)/shard_map/ppermute | solution.py:261
  15.0 12.1 %collective-permute-start.3 = (f32[128,512]{1,0:T(8,128)S(1)}, f32[128,512]{1,0:T(8,128)S(1)}, u32[]{:S(2)}, u32[]{:S(2)}) collective-permute-start(f32[128,512]{1,0:T(8,128)S(1)} %get-tuple-element.50.refs_4_), channel_id=1, source_target_pairs={{0,4},{4,0},{8,12},{12,8},{16,20},{20,16},{24,28},{28,24},{1,5},{5... | collective-permute-start | bytes 786440 | tf_op jit(solution)/shard_map/ppermute | solution.py:257
  15.1 12.1 %collective-permute-start.9 = (f32[128,512]{1,0:T(8,128)S(1)}, f32[128,512]{1,0:T(8,128)S(1)}, u32[]{:S(2)}, u32[]{:S(2)}) collective-permute-start(f32[128,512]{1,0:T(8,128)S(1)} %collective-permute-done.8.refs_10_), channel_id=1, source_target_pairs={{0,4},{4,0},{8,12},{12,8},{16,20},{20,16},{24,28},{28,24},{1,5},{5... | collective-permute-start | bytes 786440 | tf_op jit(solution)/shard_map/ppermute | solution.py:257
  17.6 9.5 %collective-permute-start.7 = (f32[128,512]{1,0:T(8,128)S(1)}, f32[128,512]{1,0:T(8,128)S(1)}, u32[]{:S(2)}, u32[]{:S(2)}) collective-permute-start(f32[128,512]{1,0:T(8,128)S(1)} %collective-permute-done.6.refs_8_), channel_id=1, source_target_pairs={{0,4},{4,0},{8,12},{12,8},{16,20},{20,16},{24,28},{28,24},{1,5},{5... | collective-permute-start | bytes 786440 | tf_op jit(solution)/shard_map/ppermute | solution.py:257
  17.9 9.2 %collective-permute-start.5 = (f32[128,512]{1,0:T(8,128)S(1)}, f32[128,512]{1,0:T(8,128)S(1)}, u32[]{:S(2)}, u32[]{:S(2)}) collective-permute-start(f32[128,512]{1,0:T(8,128)S(1)} %collective-permute-done.4.refs_6_), channel_id=1, source_target_pairs={{0,4},{4,0},{8,12},{12,8},{16,20},{20,16},{24,28},{28,24},{1,5},{5... | collective-permute-start | bytes 786440 | tf_op jit(solution)/shard_map/ppermute | solution.py:257
  22.0 5.1 %collective-permute-start = (f32[72,512]{1,0:T(8,128)S(1)}, f32[72,512]{1,0:T(8,128)S(1)}, u32[]{:S(2)}, u32[]{:S(2)}) collective-permute-start(f32[72,512]{1,0:T(8,128)S(1)} %get-tuple-element.49.refs_0_), channel_id=1, source_target_pairs={{0,1},{1,0},{2,3},{3,2},{4,5},{5,4},{6,7},{7,6},{8,9},{9,8},{10,11... | collective-permute-start | bytes 442376 | tf_op jit(solution)/shard_map/ppermute | solution.py:261
  32.3 2.7 %collective-permute-start.13 = (f32[4,64,1024]{2,1,0:T(8,128)S(1)}, f32[4,64,1024]{2,1,0:T(8,128)S(1)}, u32[]{:S(2)}, u32[]{:S(2)}) collective-permute-start(f32[4,64,1024]{2,1,0:T(8,128)S(1)} %get-tuple-element.81), channel_id=1, source_target_pairs={{0,4},{4,0},{8,12},{12,8},{16,20},{20,16},{24,28},{28,24},{1,5},{5... | collective-permute-start | bytes 3145736 | tf_op jit(solution)/shard_map/ppermute | solution.py:257
  33.5 7.0 %collective-permute-start.10 = (f32[72,512]{1,0:T(8,128)S(1)}, f32[72,512]{1,0:T(8,128)S(1)}, u32[]{:S(2)}, u32[]{:S(2)}) collective-permute-start(f32[72,512]{1,0:T(8,128)S(1)} %get-tuple-element.76), channel_id=1, source_target_pairs={{0,1},{1,0},{2,3},{3,2},{4,5},{5,4},{6,7},{7,6},{8,9},{9,8},{10,11... | collective-permute-start | bytes 442376 | tf_op jit(solution)/shard_map/ppermute | solution.py:261
  35.2 16.6 %collective-permute-start.14 = (f32[64,1024]{1,0:T(8,128)S(1)}, f32[64,1024]{1,0:T(8,128)S(1)}, u32[]{:S(2)}, u32[]{:S(2)}) collective-permute-start(f32[64,1024]{1,0:T(8,128)S(1)} %get-tuple-element.87), channel_id=1, source_target_pairs={{0,8},{4,12},{8,0},{12,4},{16,24},{20,28},{24,16},{28,20},{1,9},{5... | collective-permute-start | bytes 786440 | tf_op jit(solution)/shard_map/ppermute | solution.py:257
  36.7 15.1 %collective-permute-start.15 = (f32[64,1024]{1,0:T(8,128)S(1)}, f32[64,1024]{1,0:T(8,128)S(1)}, u32[]{:S(2)}, u32[]{:S(2)}) collective-permute-start(f32[64,1024]{1,0:T(8,128)S(1)} %get-tuple-element.88), channel_id=1, source_target_pairs={{0,16},{4,20},{8,24},{12,28},{16,0},{20,4},{24,8},{28,12},{1,17},{... | collective-permute-start | bytes 786440 | tf_op jit(solution)/shard_map/ppermute | solution.py:257
  38.2 13.6 %collective-permute-start.16 = (f32[64,1024]{1,0:T(8,128)S(1)}, f32[64,1024]{1,0:T(8,128)S(1)}, u32[]{:S(2)}, u32[]{:S(2)}) collective-permute-start(f32[64,1024]{1,0:T(8,128)S(1)} %get-tuple-element.89), channel_id=1, source_target_pairs={{0,24},{4,28},{8,16},{12,20},{16,8},{20,12},{24,0},{28,4},{1,25},{... | collective-permute-start | bytes 786440 | tf_op jit(solution)/shard_map/ppermute | solution.py:257
  38.7 12.4 %collective-permute-start.11 = (f32[72,512]{1,0:T(8,128)S(1)}, f32[72,512]{1,0:T(8,128)S(1)}, u32[]{:S(2)}, u32[]{:S(2)}) collective-permute-start(f32[72,512]{1,0:T(8,128)S(1)} %get-tuple-element.77), channel_id=1, source_target_pairs={{0,2},{1,3},{2,0},{3,1},{4,6},{5,7},{6,4},{7,5},{8,10},{9,11},{10,... | collective-permute-start | bytes 442376 | tf_op jit(solution)/shard_map/ppermute | solution.py:261
  40.4 10.7 %collective-permute-start.12 = (f32[72,512]{1,0:T(8,128)S(1)}, f32[72,512]{1,0:T(8,128)S(1)}, u32[]{:S(2)}, u32[]{:S(2)}) collective-permute-start(f32[72,512]{1,0:T(8,128)S(1)} %get-tuple-element.78), channel_id=1, source_target_pairs={{0,3},{1,2},{2,1},{3,0},{4,7},{5,6},{6,5},{7,4},{8,11},{9,10},{10,... | collective-permute-start | bytes 442376 | tf_op jit(solution)/shard_map/ppermute | solution.py:261

commit v2 on v1

--- a/solution.py
+++ b/solution.py
@@ -38,6 +38,10 @@
     pair = split(x)
     refs[0][...], refs[1][...] = pair
     return pair
+
+
+def square(chips):
+    return chips == 4
 
 
 def paired(ways):
@@ -204,9 +208,18 @@
 
 
 def join_kernel(chips, *refs):
-    received = refs[0]
+    received, keep, outs = refs[0], refs[1 : 1 + chips], refs[1 + chips :]
+    width = outs[0].shape[1]
     for step in range(chips):
-        refs[1 + chips + step][...] = refs[1 + step][...] + received[step, :, :]
+        total = keep[step][...] + received[step, :, :]
+        outs[step][...] = total[:, :width]
+        outs[chips + step][...] = total[:, width:]
+
+
+def add_kernel(*refs):
+    count = len(refs) // 3
+    for which in range(count):
+        refs[2 * count + which][...] = refs[which][...] + refs[count + which][...]
 
 
 def token_sum_kernel(ways, *refs):
@@ -219,14 +232,13 @@
     rope_out[...] = unpack_narrow(rows, lat, total)
 
 
-def up_sum_kernel(chips, *refs):
-    key_out, value_out = refs[chips:]
-    width = key_out.shape[1]
-    total = refs[0][...]
-    for step in range(1, chips):
-        total = total + refs[step][...]
-    key_out[...] = total[:, :width]
-    value_out[...] = total[:, width:]
+def up_sum_kernel(*refs):
+    count = len(refs) // 2 - 1
+    for out, parts in ((refs[-2], refs[:count]), (refs[-1], refs[count:-2])):
+        total = parts[0][...]
+        for part in parts[1:]:
+            total = total + part[...]
+        out[...] = total
 
 
 def vmem(*arrays):
@@ -272,8 +284,8 @@
     up_blocks = [block for pair in zip(even, odd) for block in pair]
 
     heads = width // NOPE
-    wide, square = (length, width), (lat, width)
-    pairs = [(heads, length, length), wide, (length, ROPE), wide, wide, square, square]
+    wide, whole = (length, width), (lat, width)
+    pairs = [(heads, length, length), wide, (length, ROPE), wide, wide, whole, whole]
     queries = pl.pallas_call(
         prepare_kernel,
         out_shape=[pltpu.VMEM((length, length), F32)]
@@ -290,7 +302,7 @@
         out_specs=[VMEM] * (chips + 2 + 2 * len(pairs)),
         scratch_shapes=[
             pltpu.VMEM((length, lat), F32), pltpu.VMEM((length, ROPE), F32),
-            pltpu.VMEM(square, F32), pltpu.VMEM(square, F32), pltpu.VMEM((lat, 2 * width), F32),
+            pltpu.VMEM(whole, F32), pltpu.VMEM(whole, F32), pltpu.VMEM((lat, 2 * width), F32),
         ],
         compiler_params=limit(24), name="attention",
     )(*vmem(*token_blocks, *up_blocks, *queries))
@@ -306,21 +318,34 @@
         in_specs=[VMEM] * 6, out_specs=[VMEM] * 2, compiler_params=limit(8), name="query",
     )(*vmem(*pairs[:6]))
 
+    block = pltpu.VMEM((rows_up, width), F32)
     received = swap(send, 1)
     joined = pl.pallas_call(
-        functools.partial(join_kernel, chips), out_shape=[pltpu.VMEM((rows_up, 2 * width), F32)] * chips,
-        in_specs=[VMEM] * (1 + chips), out_specs=[VMEM] * chips, compiler_params=limit(4), name="join",
+        functools.partial(join_kernel, chips), out_shape=[block] * (2 * chips),
+        in_specs=[VMEM] * (1 + chips), out_specs=[VMEM] * (2 * chips), compiler_params=limit(6), name="join",
     )(*vmem(received, *keep))
-    arrived = [joined[0]] + [swap(joined[step], 2 * step) for step in range(1, chips)]
+    keys, values = list(joined[:chips]), list(joined[chips:])
+    if square(chips):
+        relayed = swap(keys[3], 2), swap(values[3], 4)
+        direct = swap(keys[1], 2), swap(values[2], 4)
+        added = pl.pallas_call(
+            add_kernel, out_shape=[block] * 2, in_specs=[VMEM] * 4, out_specs=[VMEM] * 2,
+            compiler_params=limit(4), name="relay",
+        )(*vmem(keys[2], values[1], *relayed))
+        key_parts = [keys[0], direct[0], swap(added[0], 4)]
+        value_parts = [values[0], direct[1], swap(added[1], 2)]
+    else:
+        key_parts = keys[:1] + [swap(keys[step], 2 * step) for step in range(1, chips)]
+        value_parts = values[:1] + [swap(values[step], 2 * step) for step in range(1, chips)]
     pieces = [shares[0]] + [shift(shares[step], step) for step in range(1, ways)]
     latent_grad, rope_key_grad = pl.pallas_call(
         functools.partial(token_sum_kernel, ways), out_shape=(hbm(rows, lat), hbm(rows, ROPE)),
         in_specs=[VMEM] * ways, out_specs=[VMEM] * 2, compiler_params=limit(4), name="token_sum",
     )(*vmem(*pieces))
     key_up_grad, value_up_grad = pl.pallas_call(
-        functools.partial(up_sum_kernel, chips), out_shape=(hbm(rows_up, width), hbm(rows_up, width)),
-        in_specs=[VMEM] * chips, out_specs=[VMEM] * 2, compiler_params=limit(4), name="up_sum",
-    )(*vmem(*arrived))
+        up_sum_kernel, out_shape=(hbm(rows_up, width), hbm(rows_up, width)),
+        in_specs=[VMEM] * (2 * len(key_parts)), out_specs=[VMEM] * 2, compiler_params=limit(4), name="up_sum",
+    )(*vmem(*key_parts, *value_parts))
     return nope_grad, rope_grad, latent_grad, rope_key_grad, key_up_grad, value_up_grad
 
 

time: 53.4 us -> 52 us (0.974)
  waiting for transfers between devices: 23 us -> 17.4 us
  starting transfers between devices: 16.7 us -> 21.1 us
    ppermute x6, waiting for transfers between devices: 19.1 us -> 12.1 us  [shift(): return lax.ppermute(x, 'head', to)]
    ppermute x11 -> x14, starting transfers between devices: 9 us -> 12.6 us  [swap(): return lax.ppermute(x, 'fsdp', [(i, i ^ step) for i in range(fsdp)])]
    ppermute x11 -> x14, waiting for transfers between devices: 3.82 us -> 5.31 us  [swap(): return lax.ppermute(x, 'fsdp', [(i, i ^ step) for i in range(fsdp)])]
    ppermute x6, starting transfers between devices: 7.68 us -> 8.46 us  [shift(): return lax.ppermute(x, 'head', to)]
  transfers between devices with their start and end apart: 17 -> 20, of which waited for: 7 -> 9; matrix products, arithmetic and copies ran while one was open for 0% -> 0% of each run, Pallas kernels for 10% -> 10%
where the time goes in v2:
time: 52 us; the launch traced here: 51.4 us
  starting transfers between devices  21.1 us (41%)
  waiting for transfers between devices  17.4 us (33%)
  Pallas kernels  12.2 us (23%)
  between operations  0.72 us (1%)
    ppermute x14, starting transfers between devices, swap(): return lax.ppermute(x, 'fsdp', [(i, i ^ step) for i in range(fsdp)])  12.6 us
    ppermute x6, waiting for transfers between devices, shift(): return lax.ppermute(x, 'head', to)  12.1 us
    ppermute x6, starting transfers between devices, shift(): return lax.ppermute(x, 'head', to)  8.46 us
    ppermute x14, waiting for transfers between devices, swap(): return lax.ppermute(x, 'fsdp', [(i, i ^ step) for i in range(fsdp)])  5.31 us
    pallas_call x1, Pallas kernels, on_device(): pl.pallas_call(functools.partial(attention_kernel, ways, chips), out_shap...  5.15 us
    pallas_call x1, Pallas kernels, on_device(): pl.pallas_call(query_kernel, out_shape=(hbm(*wide), hbm(*query_rope.shape...  1.78 us
    pallas_call x1, Pallas kernels, on_device(): pl.pallas_call(prepare_kernel, out_shape=[pltpu.VMEM((length, length), F3...  1.6 us
    pallas_call x1, Pallas kernels, on_device(): pl.pallas_call(pack_kernel, out_shape=(pltpu.VMEM((packed, lat), F32), pl...  1.09 us
  transfers between devices with their start and end apart: 20, of which 9 were waited for; matrix products, arithmetic and copies ran while one was open for 0% of the time, Pallas kernels for 10%

profile of v2, /device:TPU:0, one launch (start us, length us, event | category | flops | bytes accessed | tf_op | source)
XLA Modules:
  0.0 51.4 jit_solution(8607345010663645914)
XLA Ops:
  0.6 1.1 %pack.1 = (f32[72,512]{1,0:T(8,128)S(1)}, f32[128,512]{1,0:T(8,128)S(1)}) custom-call(f32[64,512]{1,0:T(8,128)} %latent_ref.1, f32[64,64]{1,0:T(8,128)} %rope_ref.2, f32[64,512]{1,0:T(8,128)} %key_ref.1, f32[64,512]{1,0:T(8,128)} %value_ref.1), custom_call_target="tpu_custom_call" | custom-call | tf_op jit(solution)/shard_map/pack/pallas_call | solution.py:275
  1.7 4.0 %collective-permute-start.8 = (f32[128,512]{1,0:T(8,128)S(1)}, f32[128,512]{1,0:T(8,128)S(1)}, u32[]{:S(2)}, u32[]{:S(2)}) collective-permute-start(f32[128,512]{1,0:T(8,128)S(1)} %get-tuple-element.56.refs_4_), channel_id=1, source_target_pairs={{0,24},{4,28},{8,16},{12,20},{16,8},{20,12},{24,0},{28,4},{1,25},{... | collective-permute-start | bytes 786440 | tf_op jit(solution)/shard_map/ppermute | solution.py:269
  5.7 0.5 collective-permute-start.6
  6.2 0.1 collective-permute-start.4
  6.4 4.0 %collective-permute-start.2 = (f32[72,512]{1,0:T(8,128)S(1)}, f32[72,512]{1,0:T(8,128)S(1)}, u32[]{:S(2)}, u32[]{:S(2)}) collective-permute-start(f32[72,512]{1,0:T(8,128)S(1)} %get-tuple-element.55.refs_0_), channel_id=1, source_target_pairs={{0,3},{1,2},{2,1},{3,0},{4,7},{5,6},{6,5},{7,4},{8,11},{9,10},{10,... | collective-permute-start | bytes 442376 | tf_op jit(solution)/shard_map/ppermute | solution.py:273
  10.4 4.7 %collective-permute-done.2.refs_3_ = f32[72,512]{1,0:T(8,128)S(1)} collective-permute-done((f32[72,512]{1,0:T(8,128)S(1)}, f32[72,512]{1,0:T(8,128)S(1)}, u32[]{:S(2)}, u32[]{:S(2)}) %collective-permute-start.2) | collective-permute-done | bytes 147488 | tf_op jit(solution)/shard_map/ppermute | solution.py:273
  15.1 0.5 collective-permute-start.9
  15.6 2.1 %collective-permute-done.6.refs_8_ = f32[128,512]{1,0:T(8,128)S(1)} collective-permute-done((f32[128,512]{1,0:T(8,128)S(1)}, f32[128,512]{1,0:T(8,128)S(1)}, u32[]{:S(2)}, u32[]{:S(2)}) %collective-permute-start.6) | collective-permute-done | bytes 262176 | tf_op jit(solution)/shard_map/ppermute | solution.py:269
  17.7 0.3 collective-permute-done.4.refs_6_
  17.9 0.2 collective-permute-start.5
  18.2 3.8 %collective-permute-done.1.refs_2_ = f32[72,512]{1,0:T(8,128)S(1)} collective-permute-done((f32[72,512]{1,0:T(8,128)S(1)}, f32[72,512]{1,0:T(8,128)S(1)}, u32[]{:S(2)}, u32[]{:S(2)}) %collective-permute-start.1) | collective-permute-done | bytes 147488 | tf_op jit(solution)/shard_map/ppermute | solution.py:273
  22.0 1.6 %prepare.1 = (f32[256,256]{1,0:T(8,128)S(1)}, bf16[256,512]{1,0:T(8,128)(2,1)S(1)}, bf16[256,512]{1,0:T(8,128)(2,1)S(1)}, bf16[256,256]{1,0:T(8,128)(2,1)S(1)}, ...) custom-call(s32[1,2]{1,0:T(1,128)} %limit_ref.1, f32[256,512]{1,0:T(8,128)} %nope_ref.1, ...), custom_call_target="tpu_custom_call" | custom-call | tf_op jit(solution)/shard_map/prepare/pallas_call | solution.py:289
  23.6 3.5 %collective-permute-done.refs_1_ = f32[72,512]{1,0:T(8,128)S(1)} collective-permute-done((f32[72,512]{1,0:T(8,128)S(1)}, f32[72,512]{1,0:T(8,128)S(1)}, u32[]{:S(2)}, u32[]{:S(2)}) %collective-permute-start) | collective-permute-done | bytes 147488 | tf_op jit(solution)/shard_map/ppermute | solution.py:273
  27.2 5.1 %attention.1 = (f32[64,1024]{1,0:T(8,128)S(1)}, f32[64,1024]{1,0:T(8,128)S(1)}, f32[64,1024]{1,0:T(8,128)S(1)}, f32[64,1024]{1,0:T(8,128)S(1)}, f32[4,64,1024]{2...) custom-call(f32[72,512]{1,0:T(8,128)S(1)} %get-tuple-element.55.refs, ...), custom_call_target="tpu_custom_call" | custom-call | tf_op jit(solution)/shard_map/attention/pallas_call | solution.py:295
  32.4 1.1 %share.1 = (f32[72,512]{1,0:T(8,128)S(1)}, f32[72,512]{1,0:T(8,128)S(1)}, f32[72,512]{1,0:T(8,128)S(1)}, f32[72,512]{1,0:T(8,128)S(1)}) custom-call(f32[256,64]{1,0:T(8,128)S(1)} %get-tuple-element.72.shared_grad_ref, bf16[256,512]{1,0:T(8,128)(2,1)S(1)} %get-tuple-element.73.refs_0_, bf16[256,512]{1,0:T(8,128)(2,1)S(1)} %get-tuple-element.74.refs_1_, ...), custom_call_target="tpu_custom_call" | custom-call | tf_op jit(solution)/shard_map/share/pallas_call | solution.py:311
  33.5 0.1 collective-permute-start.10
  33.6 3.0 %collective-permute-start.11 = (f32[72,512]{1,0:T(8,128)S(1)}, f32[72,512]{1,0:T(8,128)S(1)}, u32[]{:S(2)}, u32[]{:S(2)}) collective-permute-start(f32[72,512]{1,0:T(8,128)S(1)} %get-tuple-element.83), channel_id=1, source_target_pairs={{0,2},{1,3},{2,0},{3,1},{4,6},{5,7},{6,4},{7,5},{8,10},{9,11},{10,... | collective-permute-start | bytes 442376 | tf_op jit(solution)/shard_map/ppermute | solution.py:273
  36.6 0.1 join.1
  36.7 1.6 %collective-permute-start.15 = (f32[64,512]{1,0:T(8,128)S(1)}, f32[64,512]{1,0:T(8,128)S(1)}, u32[]{:S(2)}, u32[]{:S(2)}) collective-permute-start(f32[64,512]{1,0:T(8,128)S(1)} %get-tuple-element.96), channel_id=1, source_target_pairs={{0,8},{4,12},{8,0},{12,4},{16,24},{20,28},{24,16},{28,20},{1,9},{5... | collective-permute-start | bytes 393224 | tf_op jit(solution)/shard_map/ppermute | solution.py:269
  38.2 1.5 %collective-permute-start.16 = (f32[64,512]{1,0:T(8,128)S(1)}, f32[64,512]{1,0:T(8,128)S(1)}, u32[]{:S(2)}, u32[]{:S(2)}) collective-permute-start(f32[64,512]{1,0:T(8,128)S(1)} %get-tuple-element.97), channel_id=1, source_target_pairs={{0,16},{4,20},{8,24},{12,28},{16,0},{20,4},{24,8},{28,12},{1,17},{... | collective-permute-start | bytes 393224 | tf_op jit(solution)/shard_map/ppermute | solution.py:269
  39.8 1.3 %collective-permute-start.12 = (f32[72,512]{1,0:T(8,128)S(1)}, f32[72,512]{1,0:T(8,128)S(1)}, u32[]{:S(2)}, u32[]{:S(2)}) collective-permute-start(f32[72,512]{1,0:T(8,128)S(1)} %get-tuple-element.84), channel_id=1, source_target_pairs={{0,3},{1,2},{2,1},{3,0},{4,7},{5,6},{6,5},{7,4},{8,11},{9,10},{10,... | collective-permute-start | bytes 442376 | tf_op jit(solution)/shard_map/ppermute | solution.py:273
  41.1 1.0 %collective-permute-done.15.refs_2_ = f32[64,512]{1,0:T(8,128)S(1)} collective-permute-done((f32[64,512]{1,0:T(8,128)S(1)}, f32[64,512]{1,0:T(8,128)S(1)}, u32[]{:S(2)}, u32[]{:S(2)}) %collective-permute-start.15) | collective-permute-done | bytes 131104 | tf_op jit(solution)/shard_map/ppermute | solution.py:269
  42.1 1.5 %collective-permute-start.14 = (f32[64,512]{1,0:T(8,128)S(1)}, f32[64,512]{1,0:T(8,128)S(1)}, u32[]{:S(2)}, u32[]{:S(2)}) collective-permute-start(f32[64,512]{1,0:T(8,128)S(1)} %get-tuple-element.93), channel_id=1, source_target_pairs={{0,8},{4,12},{8,0},{12,4},{16,24},{20,28},{24,16},{28,20},{1,9},{5... | collective-permute-start | bytes 393224 | tf_op jit(solution)/shard_map/ppermute | solution.py:269
  43.6 1.5 %collective-permute-start.18 = (f32[64,512]{1,0:T(8,128)S(1)}, f32[64,512]{1,0:T(8,128)S(1)}, u32[]{:S(2)}, u32[]{:S(2)}) collective-permute-start(f32[64,512]{1,0:T(8,128)S(1)} %get-tuple-element.100), channel_id=1, source_target_pairs={{0,16},{4,20},{8,24},{12,28},{16,0},{20,4},{24,8},{28,12},{1,17},{... | collective-permute-start | bytes 393224 | tf_op jit(solution)/shard_map/ppermute | solution.py:269
  45.1 0.6 %collective-permute-start.17 = (f32[64,512]{1,0:T(8,128)S(1)}, f32[64,512]{1,0:T(8,128)S(1)}, u32[]{:S(2)}, u32[]{:S(2)}) collective-permute-start(f32[64,512]{1,0:T(8,128)S(1)} %get-tuple-element.98), channel_id=1, source_target_pairs={{0,16},{4,20},{8,24},{12,28},{16,0},{20,4},{24,8},{28,12},{1,17},{... | collective-permute-start | bytes 393224 | tf_op jit(solution)/shard_map/ppermute | solution.py:269
  45.7 0.5 %collective-permute-start.19 = (f32[64,512]{1,0:T(8,128)S(1)}, f32[64,512]{1,0:T(8,128)S(1)}, u32[]{:S(2)}, u32[]{:S(2)}) collective-permute-start(f32[64,512]{1,0:T(8,128)S(1)} %get-tuple-element.101), channel_id=1, source_target_pairs={{0,8},{4,12},{8,0},{12,4},{16,24},{20,28},{24,16},{28,20},{1,9},{5... | collective-permute-start | bytes 393224 | tf_op jit(solution)/shard_map/ppermute | solution.py:269
  46.3 1.8 %query.1 = (f32[256,512]{1,0:T(8,128)}, f32[256,256]{1,0:T(8,128)}) custom-call(bf16[4,256,256]{2,1,0:T(8,128)(2,1)S(1)} %get-tuple-element.64.refs_0_, bf16[4,256,256]{2,1,0:T(8,128)(2,1)S(1)} %get-tuple-element.65.refs_1_, bf16[256,512]{1,0:T(8,128)(2,1)S(1)} %get-tuple-element.66.refs_2_, bf16[256,512]{1,0:T(8,128)(2,1)S(1)} %get-tuple-element.67.refs_3_, ...), custom_call_target="tpu_custom_call" | custom-call | tf_op jit(solution)/shard_map/query/pallas_call | solution.py:316
  48.0 0.7 %token_sum.1 = (f32[64,512]{1,0:T(8,128)}, f32[64,64]{1,0:T(8,128)}) custom-call(f32[72,512]{1,0:T(8,128)S(1)} %get-tuple-element.81.refs_0_, f32[72,512]{1,0:T(8,128)S(1)} %collective-permute-done.10.refs_1_, f32[72,512]{1,0:T(8,128)S(1)} %collective-permute-done.11.refs_2_, f32[72,512]{1,0:T(8,128)S(1)} %collective-permute-done.12.refs_3_), custom_call_target="tpu_custom_call" | custom-call | tf_op jit(solution)/shard_map/token_sum/pallas_call | solution.py:341
  48.7 0.5 collective-permute-done.18.refs_4_
  49.2 1.4 %collective-permute-done.17.refs_2_ = f32[64,512]{1,0:T(8,128)S(1)} collective-permute-done((f32[64,512]{1,0:T(8,128)S(1)}, f32[64,512]{1,0:T(8,128)S(1)}, u32[]{:S(2)}, u32[]{:S(2)}) %collective-permute-start.17) | collective-permute-done | bytes 131104 | tf_op jit(solution)/shard_map/ppermute | solution.py:269
  50.6 0.1 collective-permute-done.19.refs_5_
  50.7 0.7 %up_sum.1 = (f32[64,512]{1,0:T(8,128)}, f32[64,512]{1,0:T(8,128)}) custom-call(f32[64,512]{1,0:T(8,128)S(1)} %get-tuple-element.92.refs_0_, f32[64,512]{1,0:T(8,128)S(1)} %collective-permute-done.14.refs_1_, f32[64,512]{1,0:T(8,128)S(1)} %collective-permute-done.17.refs_2_, f32[64,512]{1,0:T(8,128)S(1)} %get-tuple-element.99.refs_3_, ...), custom_call_target="tpu_custom_call" | custom-call | tf_op jit(solution)/shard_map/up_sum/pallas_call | solution.py:345
  (17 shorter events, 0.2 us)
Async XLA Ops:
  1.7 13.3 %collective-permute-start.8 = (f32[128,512]{1,0:T(8,128)S(1)}, f32[128,512]{1,0:T(8,128)S(1)}, u32[]{:S(2)}, u32[]{:S(2)}) collective-permute-start(f32[128,512]{1,0:T(8,128)S(1)} %get-tuple-element.56.refs_4_), channel_id=1, source_target_pairs={{0,24},{4,28},{8,16},{12,20},{16,8},{20,12},{24,0},{28,4},{1,25},{... | collective-permute-start | bytes 786440 | tf_op jit(solution)/shard_map/ppermute | solution.py:269
  5.7 11.9 %collective-permute-start.6 = (f32[128,512]{1,0:T(8,128)S(1)}, f32[128,512]{1,0:T(8,128)S(1)}, u32[]{:S(2)}, u32[]{:S(2)}) collective-permute-start(f32[128,512]{1,0:T(8,128)S(1)} %get-tuple-element.56.refs_4_), channel_id=1, source_target_pairs={{0,16},{4,20},{8,24},{12,28},{16,0},{20,4},{24,8},{28,12},{1,17},{... | collective-permute-start | bytes 786440 | tf_op jit(solution)/shard_map/ppermute | solution.py:269
  6.2 11.7 %collective-permute-start.4 = (f32[128,512]{1,0:T(8,128)S(1)}, f32[128,512]{1,0:T(8,128)S(1)}, u32[]{:S(2)}, u32[]{:S(2)}) collective-permute-start(f32[128,512]{1,0:T(8,128)S(1)} %get-tuple-element.56.refs_4_), channel_id=1, source_target_pairs={{0,8},{4,12},{8,0},{12,4},{16,24},{20,28},{24,16},{28,20},{1,9},{5... | collective-permute-start | bytes 786440 | tf_op jit(solution)/shard_map/ppermute | solution.py:269
  6.4 8.7 %collective-permute-start.2 = (f32[72,512]{1,0:T(8,128)S(1)}, f32[72,512]{1,0:T(8,128)S(1)}, u32[]{:S(2)}, u32[]{:S(2)}) collective-permute-start(f32[72,512]{1,0:T(8,128)S(1)} %get-tuple-element.55.refs_0_), channel_id=1, source_target_pairs={{0,3},{1,2},{2,1},{3,0},{4,7},{5,6},{6,5},{7,4},{8,11},{9,10},{10,... | collective-permute-start | bytes 442376 | tf_op jit(solution)/shard_map/ppermute | solution.py:273
  10.4 11.6 %collective-permute-start.1 = (f32[72,512]{1,0:T(8,128)S(1)}, f32[72,512]{1,0:T(8,128)S(1)}, u32[]{:S(2)}, u32[]{:S(2)}) collective-permute-start(f32[72,512]{1,0:T(8,128)S(1)} %get-tuple-element.55.refs_0_), channel_id=1, source_target_pairs={{0,2},{1,3},{2,0},{3,1},{4,6},{5,7},{6,4},{7,5},{8,10},{9,11},{10,... | collective-permute-start | bytes 442376 | tf_op jit(solution)/shard_map/ppermute | solution.py:273
  15.0 12.1 %collective-permute-start.3 = (f32[128,512]{1,0:T(8,128)S(1)}, f32[128,512]{1,0:T(8,128)S(1)}, u32[]{:S(2)}, u32[]{:S(2)}) collective-permute-start(f32[128,512]{1,0:T(8,128)S(1)} %get-tuple-element.56.refs_4_), channel_id=1, source_target_pairs={{0,4},{4,0},{8,12},{12,8},{16,20},{20,16},{24,28},{28,24},{1,5},{5... | collective-permute-start | bytes 786440 | tf_op jit(solution)/shard_map/ppermute | solution.py:269
  15.1 12.1 %collective-permute-start.9 = (f32[128,512]{1,0:T(8,128)S(1)}, f32[128,512]{1,0:T(8,128)S(1)}, u32[]{:S(2)}, u32[]{:S(2)}) collective-permute-start(f32[128,512]{1,0:T(8,128)S(1)} %collective-permute-done.8.refs_10_), channel_id=1, source_target_pairs={{0,4},{4,0},{8,12},{12,8},{16,20},{20,16},{24,28},{28,24},{1,5},{5... | collective-permute-start | bytes 786440 | tf_op jit(solution)/shard_map/ppermute | solution.py:269
  17.6 9.5 %collective-permute-start.7 = (f32[128,512]{1,0:T(8,128)S(1)}, f32[128,512]{1,0:T(8,128)S(1)}, u32[]{:S(2)}, u32[]{:S(2)}) collective-permute-start(f32[128,512]{1,0:T(8,128)S(1)} %collective-permute-done.6.refs_8_), channel_id=1, source_target_pairs={{0,4},{4,0},{8,12},{12,8},{16,20},{20,16},{24,28},{28,24},{1,5},{5... | collective-permute-start | bytes 786440 | tf_op jit(solution)/shard_map/ppermute | solution.py:269
  17.9 9.2 %collective-permute-start.5 = (f32[128,512]{1,0:T(8,128)S(1)}, f32[128,512]{1,0:T(8,128)S(1)}, u32[]{:S(2)}, u32[]{:S(2)}) collective-permute-start(f32[128,512]{1,0:T(8,128)S(1)} %collective-permute-done.4.refs_6_), channel_id=1, source_target_pairs={{0,4},{4,0},{8,12},{12,8},{16,20},{20,16},{24,28},{28,24},{1,5},{5... | collective-permute-start | bytes 786440 | tf_op jit(solution)/shard_map/ppermute | solution.py:269
  22.0 5.1 %collective-permute-start = (f32[72,512]{1,0:T(8,128)S(1)}, f32[72,512]{1,0:T(8,128)S(1)}, u32[]{:S(2)}, u32[]{:S(2)}) collective-permute-start(f32[72,512]{1,0:T(8,128)S(1)} %get-tuple-element.55.refs_0_), channel_id=1, source_target_pairs={{0,1},{1,0},{2,3},{3,2},{4,5},{5,4},{6,7},{7,6},{8,9},{9,8},{10,11... | collective-permute-start | bytes 442376 | tf_op jit(solution)/shard_map/ppermute | solution.py:273
  32.3 4.3 %collective-permute-start.13 = (f32[4,64,1024]{2,1,0:T(8,128)S(1)}, f32[4,64,1024]{2,1,0:T(8,128)S(1)}, u32[]{:S(2)}, u32[]{:S(2)}) collective-permute-start(f32[4,64,1024]{2,1,0:T(8,128)S(1)} %get-tuple-element.87), channel_id=1, source_target_pairs={{0,4},{4,0},{8,12},{12,8},{16,20},{20,16},{24,28},{28,24},{1,5},{5... | collective-permute-start | bytes 3145736 | tf_op jit(solution)/shard_map/ppermute | solution.py:269
  33.5 11.7 %collective-permute-start.10 = (f32[72,512]{1,0:T(8,128)S(1)}, f32[72,512]{1,0:T(8,128)S(1)}, u32[]{:S(2)}, u32[]{:S(2)}) collective-permute-start(f32[72,512]{1,0:T(8,128)S(1)} %get-tuple-element.82), channel_id=1, source_target_pairs={{0,1},{1,0},{2,3},{3,2},{4,5},{5,4},{6,7},{7,6},{8,9},{9,8},{10,11... | collective-permute-start | bytes 442376 | tf_op jit(solution)/shard_map/ppermute | solution.py:273
  33.6 12.1 %collective-permute-start.11 = (f32[72,512]{1,0:T(8,128)S(1)}, f32[72,512]{1,0:T(8,128)S(1)}, u32[]{:S(2)}, u32[]{:S(2)}) collective-permute-start(f32[72,512]{1,0:T(8,128)S(1)} %get-tuple-element.83), channel_id=1, source_target_pairs={{0,2},{1,3},{2,0},{3,1},{4,6},{5,7},{6,4},{7,5},{8,10},{9,11},{10,... | collective-permute-start | bytes 442376 | tf_op jit(solution)/shard_map/ppermute | solution.py:273
  36.7 5.4 %collective-permute-start.15 = (f32[64,512]{1,0:T(8,128)S(1)}, f32[64,512]{1,0:T(8,128)S(1)}, u32[]{:S(2)}, u32[]{:S(2)}) collective-permute-start(f32[64,512]{1,0:T(8,128)S(1)} %get-tuple-element.96), channel_id=1, source_target_pairs={{0,8},{4,12},{8,0},{12,4},{16,24},{20,28},{24,16},{28,20},{1,9},{5... | collective-permute-start | bytes 393224 | tf_op jit(solution)/shard_map/ppermute | solution.py:269
  38.2 5.3 %collective-permute-start.16 = (f32[64,512]{1,0:T(8,128)S(1)}, f32[64,512]{1,0:T(8,128)S(1)}, u32[]{:S(2)}, u32[]{:S(2)}) collective-permute-start(f32[64,512]{1,0:T(8,128)S(1)} %get-tuple-element.97), channel_id=1, source_target_pairs={{0,16},{4,20},{8,24},{12,28},{16,0},{20,4},{24,8},{28,12},{1,17},{... | collective-permute-start | bytes 393224 | tf_op jit(solution)/shard_map/ppermute | solution.py:269
  39.8 8.3 %collective-permute-start.12 = (f32[72,512]{1,0:T(8,128)S(1)}, f32[72,512]{1,0:T(8,128)S(1)}, u32[]{:S(2)}, u32[]{:S(2)}) collective-permute-start(f32[72,512]{1,0:T(8,128)S(1)} %get-tuple-element.84), channel_id=1, source_target_pairs={{0,3},{1,2},{2,1},{3,0},{4,7},{5,6},{6,5},{7,4},{8,11},{9,10},{10,... | collective-permute-start | bytes 442376 | tf_op jit(solution)/shard_map/ppermute | solution.py:273
  42.1 6.6 %collective-permute-start.14 = (f32[64,512]{1,0:T(8,128)S(1)}, f32[64,512]{1,0:T(8,128)S(1)}, u32[]{:S(2)}, u32[]{:S(2)}) collective-permute-start(f32[64,512]{1,0:T(8,128)S(1)} %get-tuple-element.93), channel_id=1, source_target_pairs={{0,8},{4,12},{8,0},{12,4},{16,24},{20,28},{24,16},{28,20},{1,9},{5... | collective-permute-start | bytes 393224 | tf_op jit(solution)/shard_map/ppermute | solution.py:269
  43.6 5.6 %collective-permute-start.18 = (f32[64,512]{1,0:T(8,128)S(1)}, f32[64,512]{1,0:T(8,128)S(1)}, u32[]{:S(2)}, u32[]{:S(2)}) collective-permute-start(f32[64,512]{1,0:T(8,128)S(1)} %get-tuple-element.100), channel_id=1, source_target_pairs={{0,16},{4,20},{8,24},{12,28},{16,0},{20,4},{24,8},{28,12},{1,17},{... | collective-permute-start | bytes 393224 | tf_op jit(solution)/shard_map/ppermute | solution.py:269
  45.1 5.4 %collective-permute-start.17 = (f32[64,512]{1,0:T(8,128)S(1)}, f32[64,512]{1,0:T(8,128)S(1)}, u32[]{:S(2)}, u32[]{:S(2)}) collective-permute-start(f32[64,512]{1,0:T(8,128)S(1)} %get-tuple-element.98), channel_id=1, source_target_pairs={{0,16},{4,20},{8,24},{12,28},{16,0},{20,4},{24,8},{28,12},{1,17},{... | collective-permute-start | bytes 393224 | tf_op jit(solution)/shard_map/ppermute | solution.py:269
  45.7 5.0 %collective-permute-start.19 = (f32[64,512]{1,0:T(8,128)S(1)}, f32[64,512]{1,0:T(8,128)S(1)}, u32[]{:S(2)}, u32[]{:S(2)}) collective-permute-start(f32[64,512]{1,0:T(8,128)S(1)} %get-tuple-element.101), channel_id=1, source_target_pairs={{0,8},{4,12},{8,0},{12,4},{16,24},{20,28},{24,16},{28,20},{1,9},{5... | collective-permute-start | bytes 393224 | tf_op jit(solution)/shard_map/ppermute | solution.py:269

commit v3 on v2

--- a/solution.py
+++ b/solution.py
@@ -28,6 +28,15 @@
     dims = (((left_dim,), (right_dim,)), ((), ()))
     dot = functools.partial(lax.dot_general, dimension_numbers=dims, preferred_element_type=F32)
     return dot(left[0], right[0]) + (dot(left[0], right[1]) + dot(left[1], right[0]))
+
+
+def joined_dot(left, right):
+    left, right = jnp.concatenate(left, axis=1), jnp.concatenate(right, axis=1)
+    return lax.dot_general(left, right, (((1,), (1,)), ((), ())), preferred_element_type=F32)
+
+
+def over_rows(left, right):
+    return lax.dot_general(left, right, (((0,), (0,)), ((), ())), preferred_element_type=F32)
 
 
 def columns(pair, start, size):
@@ -96,15 +105,19 @@
     key_pos = lax.broadcasted_iota(jnp.int32, mask_ref.shape, 1)
     visible = (key_pos < limit_ref[0, 1]) & ((key_pos <= query_pos) | (key_pos < limit_ref[0, 0]))
     mask_ref[...] = jnp.where(visible, 0.0, -jnp.inf)
-    keep_pair(refs[0:2], nope_ref[...] * factor)
-    keep_pair(refs[2:4], rope_ref[...] * factor)
-    keep_pair(refs[4:6], cot_ref[...])
+    rope_ref_out, nope_refs, cot_refs = refs[0], refs[1:3], refs[3:5]
+    keep_pair(nope_refs, nope_ref[...] * factor)
+    keep_pair(cot_refs, cot_ref[...])
+    rope = split(rope_ref[...] * factor)
+    for head in range(rope_ref_out.shape[0]):
+        high, low = columns(rope, head * ROPE, ROPE)
+        rope_ref_out[head, :, :] = jnp.concatenate([high, low, high], axis=1)
 
 
 def attention_kernel(ways, chips, *refs):
     token_refs, refs = refs[:ways], refs[ways:]
     up_refs, refs = refs[: 2 * chips], refs[2 * chips :]
-    mask_ref, nope_refs, rope_refs, cot_refs, refs = refs[0], refs[1:3], refs[3:5], refs[5:7], refs[7:]
+    mask_ref, rope_ref, nope_refs, cot_refs, refs = refs[0], refs[1], refs[2:4], refs[4:6], refs[6:]
     keep_refs, refs = refs[:chips], refs[chips:]
     send_ref, shared_grad_ref = refs[:2]
     grad_scores_refs, key_rows_refs, shared_refs = refs[2:4], refs[4:6], refs[6:8]
@@ -134,15 +147,13 @@
     key_rows = keep_pair(key_rows_refs, product(latent, key_up, 1, 0))
     value_rows = split(product(latent, value_up, 1, 0))
 
-    def of_head(refs, head, size):
-        return refs[0][:, head * size : (head + 1) * size], refs[1][:, head * size : (head + 1) * size]
+    shared_parts = jnp.concatenate([shared[0], shared[0], shared[1]], axis=1)
 
     def front(head):
-        keys = columns(key_rows, head * NOPE, NOPE)
-        values = columns(value_rows, head * VHEAD, VHEAD)
-        scores = product(of_head(nope_refs, head, NOPE), keys, 1, 1)
-        scores = scores + product(of_head(rope_refs, head, ROPE), shared, 1, 1)
-        return scores + mask_ref[...], product(of_head(cot_refs, head, VHEAD), values, 1, 1)
+        nope, cot = columns(nope_refs, head * NOPE, NOPE), columns(cot_refs, head * VHEAD, VHEAD)
+        keys, values = columns(key_rows, head * NOPE, NOPE), columns(value_rows, head * VHEAD, VHEAD)
+        scores = joined_dot([*nope, nope[0], rope_ref[head]], [keys[0], *keys, shared_parts])
+        return scores + mask_ref[...], joined_dot([*cot, cot[0]], [values[0], *values])
 
     def middle(head, scores, grad_attend):
         weight = jnp.exp(scores - jnp.max(scores, axis=1, keepdims=True))
@@ -155,14 +166,19 @@
         return split(attend), grad_scores
 
     def back(head, attend, grad_scores):
+        nope, cot = columns(nope_refs, head * NOPE, NOPE), columns(cot_refs, head * VHEAD, VHEAD)
+        rope = rope_ref[head][:, : 2 * ROPE]
+        both_cot = over_rows(attend[0], jnp.concatenate(cot, axis=1))
+        both_nope = over_rows(grad_scores[0], jnp.concatenate(nope, axis=1))
+        low = over_rows(grad_scores[1], jnp.concatenate([nope[0], rope], axis=1))
         return (
-            product(attend, of_head(cot_refs, head, VHEAD), 0, 0),
-            product(grad_scores, of_head(nope_refs, head, NOPE), 0, 0),
-            product(grad_scores, of_head(rope_refs, head, ROPE), 0, 0),
+            both_cot[:, :VHEAD] + both_cot[:, VHEAD:] + over_rows(attend[1], cot[0]),
+            both_nope[:, :NOPE] + both_nope[:, NOPE:] + low[:, :NOPE],
+            over_rows(grad_scores[0], rope) + low[:, NOPE:],
         )
 
     value_grads, key_grads = [], []
-    shared_grad = jnp.zeros((length, ROPE), F32)
+    shared_grad = jnp.zeros((length, 2 * ROPE), F32)
     ready = front(0)
     for head in range(head_count):
         later = front(head + 1) if head + 1 < head_count else None
@@ -171,7 +187,7 @@
         key_grads.append(key_part)
         shared_grad = shared_grad + shared_part
         ready = later
-    shared_grad_ref[...] = shared_grad
+    shared_grad_ref[...] = shared_grad[:, :ROPE] + shared_grad[:, ROPE:]
     key_grad = keep_pair(key_grad_refs, jnp.concatenate(key_grads, axis=1))
     value_grad = keep_pair(value_grad_refs, jnp.concatenate(value_grads, axis=1))
 
@@ -289,8 +305,8 @@
     queries = pl.pallas_call(
         prepare_kernel,
         out_shape=[pltpu.VMEM((length, length), F32)]
-        + [pltpu.VMEM(dims, BF16) for dims in (wide, query_rope.shape, wide) for _ in range(2)],
-        in_specs=[SMEM] + [VMEM] * 3, out_specs=[VMEM] * 7, compiler_params=limit(8), name="prepare",
+        + [pltpu.VMEM((heads, length, 3 * ROPE), BF16)] + [pltpu.VMEM(wide, BF16)] * 4,
+        in_specs=[SMEM] + [VMEM] * 3, out_specs=[VMEM] * 6, compiler_params=limit(8), name="prepare",
     )(*stored(bounds, query_nope, query_rope, cotangent))
     out = pl.pallas_call(
         functools.partial(attention_kernel, ways, chips),
@@ -298,7 +314,7 @@
             *([pltpu.VMEM((rows_up, 2 * width), F32)] * chips), pltpu.VMEM((chips, rows_up, 2 * width), F32),
             pltpu.VMEM((length, ROPE), F32), *[pltpu.VMEM(dims, BF16) for dims in pairs for _ in range(2)],
         ),
-        in_specs=[VMEM] * (ways + fsdp + 7),
+        in_specs=[VMEM] * (ways + fsdp + 6),
         out_specs=[VMEM] * (chips + 2 + 2 * len(pairs)),
         scratch_shapes=[
             pltpu.VMEM((length, lat), F32), pltpu.VMEM((length, ROPE), F32),

time: 52 us -> 51.5 us (level)
    pallas_call x1, Pallas kernels: 5.15 us -> 4.58 us  [on_device(): pl.pallas_call(functools.partial(attention_kernel, ways, chips), out_shap...]
  transfers between devices with their start and end apart: 20 -> 20, of which waited for: 9 -> 9; matrix products, arithmetic and copies ran while one was open for 0% -> 0% of each run, Pallas kernels for 10% -> 11%
where the time goes in v3:
time: 51.5 us; the launch traced here: 50.9 us
  starting transfers between devices  21.1 us (41%)
  waiting for transfers between devices  17.2 us (33%)
  Pallas kernels  11.8 us (23%)
  between operations  0.72 us (1%)
    ppermute x14, starting transfers between devices, swap(): return lax.ppermute(x, 'fsdp', [(i, i ^ step) for i in range(fsdp)])  12.6 us
    ppermute x6, waiting for transfers between devices, shift(): return lax.ppermute(x, 'head', to)  11.9 us
    ppermute x6, starting transfers between devices, shift(): return lax.ppermute(x, 'head', to)  8.46 us
    ppermute x14, waiting for transfers between devices, swap(): return lax.ppermute(x, 'fsdp', [(i, i ^ step) for i in range(fsdp)])  5.31 us
    pallas_call x1, Pallas kernels, on_device(): pl.pallas_call(functools.partial(attention_kernel, ways, chips), out_shap...  4.58 us
    pallas_call x1, Pallas kernels, on_device(): pl.pallas_call(query_kernel, out_shape=(hbm(*wide), hbm(*query_rope.shape...  1.77 us
    pallas_call x1, Pallas kernels, on_device(): pl.pallas_call(prepare_kernel, out_shape=[pltpu.VMEM((length, length), F3...  1.76 us
    pallas_call x1, Pallas kernels, on_device(): pl.pallas_call(pack_kernel, out_shape=(pltpu.VMEM((packed, lat), F32), pl...  1.09 us
  transfers between devices with their start and end apart: 20, of which 9 were waited for; matrix products, arithmetic and copies ran while one was open for 0% of the time, Pallas kernels for 11%

profile of v3, /device:TPU:0, one launch (start us, length us, event | category | flops | bytes accessed | tf_op | source)
XLA Modules:
  0.0 50.9 jit_solution(10864260265962356009)
XLA Ops:
  0.6 1.1 %pack.1 = (f32[72,512]{1,0:T(8,128)S(1)}, f32[128,512]{1,0:T(8,128)S(1)}) custom-call(f32[64,512]{1,0:T(8,128)} %latent_ref.1, f32[64,64]{1,0:T(8,128)} %rope_ref.2, f32[64,512]{1,0:T(8,128)} %key_ref.1, f32[64,512]{1,0:T(8,128)} %value_ref.1), custom_call_target="tpu_custom_call" | custom-call | tf_op jit(solution)/shard_map/pack/pallas_call | solution.py:291
  1.7 4.0 %collective-permute-start.8 = (f32[128,512]{1,0:T(8,128)S(1)}, f32[128,512]{1,0:T(8,128)S(1)}, u32[]{:S(2)}, u32[]{:S(2)}) collective-permute-start(f32[128,512]{1,0:T(8,128)S(1)} %get-tuple-element.55.refs_4_), channel_id=1, source_target_pairs={{0,24},{4,28},{8,16},{12,20},{16,8},{20,12},{24,0},{28,4},{1,25},{... | collective-permute-start | bytes 786440 | tf_op jit(solution)/shard_map/ppermute | solution.py:285
  5.7 0.5 collective-permute-start.6
  6.2 0.1 collective-permute-start.4
  6.4 4.0 %collective-permute-start.2 = (f32[72,512]{1,0:T(8,128)S(1)}, f32[72,512]{1,0:T(8,128)S(1)}, u32[]{:S(2)}, u32[]{:S(2)}) collective-permute-start(f32[72,512]{1,0:T(8,128)S(1)} %get-tuple-element.54.refs_0_), channel_id=1, source_target_pairs={{0,3},{1,2},{2,1},{3,0},{4,7},{5,6},{6,5},{7,4},{8,11},{9,10},{10,... | collective-permute-start | bytes 442376 | tf_op jit(solution)/shard_map/ppermute | solution.py:289
  10.4 4.7 %collective-permute-done.2.refs_3_ = f32[72,512]{1,0:T(8,128)S(1)} collective-permute-done((f32[72,512]{1,0:T(8,128)S(1)}, f32[72,512]{1,0:T(8,128)S(1)}, u32[]{:S(2)}, u32[]{:S(2)}) %collective-permute-start.2) | collective-permute-done | bytes 147488 | tf_op jit(solution)/shard_map/ppermute | solution.py:289
  15.1 0.5 collective-permute-start.9
  15.6 2.1 %collective-permute-done.6.refs_8_ = f32[128,512]{1,0:T(8,128)S(1)} collective-permute-done((f32[128,512]{1,0:T(8,128)S(1)}, f32[128,512]{1,0:T(8,128)S(1)}, u32[]{:S(2)}, u32[]{:S(2)}) %collective-permute-start.6) | collective-permute-done | bytes 262176 | tf_op jit(solution)/shard_map/ppermute | solution.py:285
  17.7 0.3 collective-permute-done.4.refs_6_
  17.9 0.2 collective-permute-start.5
  18.2 3.8 %collective-permute-done.1.refs_2_ = f32[72,512]{1,0:T(8,128)S(1)} collective-permute-done((f32[72,512]{1,0:T(8,128)S(1)}, f32[72,512]{1,0:T(8,128)S(1)}, u32[]{:S(2)}, u32[]{:S(2)}) %collective-permute-start.1) | collective-permute-done | bytes 147488 | tf_op jit(solution)/shard_map/ppermute | solution.py:289
  22.0 1.8 %prepare.1 = (f32[256,256]{1,0:T(8,128)S(1)}, bf16[4,256,192]{2,1,0:T(8,128)(2,1)S(1)}, bf16[256,512]{1,0:T(8,128)(2,1)S(1)}, bf16[256,512]{1,0:T(8,128)(2,1)S(1...) custom-call(s32[1,2]{1,0:T(1,128)} %limit_ref.1, f32[256,512]{1,0:T(8,128)} %nope_ref.1, ...), custom_call_target="tpu_custom_call" | custom-call | tf_op jit(solution)/shard_map/prepare/pallas_call | solution.py:305
  23.8 3.4 %collective-permute-done.refs_1_ = f32[72,512]{1,0:T(8,128)S(1)} collective-permute-done((f32[72,512]{1,0:T(8,128)S(1)}, f32[72,512]{1,0:T(8,128)S(1)}, u32[]{:S(2)}, u32[]{:S(2)}) %collective-permute-start) | collective-permute-done | bytes 147488 | tf_op jit(solution)/shard_map/ppermute | solution.py:289
  27.2 4.6 %attention.1 = (f32[64,1024]{1,0:T(8,128)S(1)}, f32[64,1024]{1,0:T(8,128)S(1)}, f32[64,1024]{1,0:T(8,128)S(1)}, f32[64,1024]{1,0:T(8,128)S(1)}, f32[4,64,1024]{2...) custom-call(f32[72,512]{1,0:T(8,128)S(1)} %get-tuple-element.54.refs, ...), custom_call_target="tpu_custom_call" | custom-call | tf_op jit(solution)/shard_map/attention/pallas_call | solution.py:311
  31.8 1.1 %share.1 = (f32[72,512]{1,0:T(8,128)S(1)}, f32[72,512]{1,0:T(8,128)S(1)}, f32[72,512]{1,0:T(8,128)S(1)}, f32[72,512]{1,0:T(8,128)S(1)}) custom-call(f32[256,64]{1,0:T(8,128)S(1)} %get-tuple-element.70.shared_grad_ref, bf16[256,512]{1,0:T(8,128)(2,1)S(1)} %get-tuple-element.71.refs_0_, bf16[256,512]{1,0:T(8,128)(2,1)S(1)} %get-tuple-element.72.refs_1_, ...), custom_call_target="tpu_custom_call" | custom-call | tf_op jit(solution)/shard_map/share/pallas_call | solution.py:327
  32.9 0.1 collective-permute-start.10
  33.0 3.0 %collective-permute-start.11 = (f32[72,512]{1,0:T(8,128)S(1)}, f32[72,512]{1,0:T(8,128)S(1)}, u32[]{:S(2)}, u32[]{:S(2)}) collective-permute-start(f32[72,512]{1,0:T(8,128)S(1)} %get-tuple-element.81), channel_id=1, source_target_pairs={{0,2},{1,3},{2,0},{3,1},{4,6},{5,7},{6,4},{7,5},{8,10},{9,11},{10,... | collective-permute-start | bytes 442376 | tf_op jit(solution)/shard_map/ppermute | solution.py:289
  36.0 0.1 join.1
  36.1 1.5 %collective-permute-start.15 = (f32[64,512]{1,0:T(8,128)S(1)}, f32[64,512]{1,0:T(8,128)S(1)}, u32[]{:S(2)}, u32[]{:S(2)}) collective-permute-start(f32[64,512]{1,0:T(8,128)S(1)} %get-tuple-element.94), channel_id=1, source_target_pairs={{0,8},{4,12},{8,0},{12,4},{16,24},{20,28},{24,16},{28,20},{1,9},{5... | collective-permute-start | bytes 393224 | tf_op jit(solution)/shard_map/ppermute | solution.py:285
  37.7 1.5 %collective-permute-start.16 = (f32[64,512]{1,0:T(8,128)S(1)}, f32[64,512]{1,0:T(8,128)S(1)}, u32[]{:S(2)}, u32[]{:S(2)}) collective-permute-start(f32[64,512]{1,0:T(8,128)S(1)} %get-tuple-element.95), channel_id=1, source_target_pairs={{0,16},{4,20},{8,24},{12,28},{16,0},{20,4},{24,8},{28,12},{1,17},{... | collective-permute-start | bytes 393224 | tf_op jit(solution)/shard_map/ppermute | solution.py:285
  39.2 1.3 %collective-permute-start.12 = (f32[72,512]{1,0:T(8,128)S(1)}, f32[72,512]{1,0:T(8,128)S(1)}, u32[]{:S(2)}, u32[]{:S(2)}) collective-permute-start(f32[72,512]{1,0:T(8,128)S(1)} %get-tuple-element.82), channel_id=1, source_target_pairs={{0,3},{1,2},{2,1},{3,0},{4,7},{5,6},{6,5},{7,4},{8,11},{9,10},{10,... | collective-permute-start | bytes 442376 | tf_op jit(solution)/shard_map/ppermute | solution.py:289
  40.5 1.0 %collective-permute-done.15.refs_2_ = f32[64,512]{1,0:T(8,128)S(1)} collective-permute-done((f32[64,512]{1,0:T(8,128)S(1)}, f32[64,512]{1,0:T(8,128)S(1)}, u32[]{:S(2)}, u32[]{:S(2)}) %collective-permute-start.15) | collective-permute-done | bytes 131104 | tf_op jit(solution)/shard_map/ppermute | solution.py:285
  41.5 1.5 %collective-permute-start.14 = (f32[64,512]{1,0:T(8,128)S(1)}, f32[64,512]{1,0:T(8,128)S(1)}, u32[]{:S(2)}, u32[]{:S(2)}) collective-permute-start(f32[64,512]{1,0:T(8,128)S(1)} %get-tuple-element.91), channel_id=1, source_target_pairs={{0,8},{4,12},{8,0},{12,4},{16,24},{20,28},{24,16},{28,20},{1,9},{5... | collective-permute-start | bytes 393224 | tf_op jit(solution)/shard_map/ppermute | solution.py:285
  43.0 1.5 %collective-permute-start.18 = (f32[64,512]{1,0:T(8,128)S(1)}, f32[64,512]{1,0:T(8,128)S(1)}, u32[]{:S(2)}, u32[]{:S(2)}) collective-permute-start(f32[64,512]{1,0:T(8,128)S(1)} %get-tuple-element.98), channel_id=1, source_target_pairs={{0,16},{4,20},{8,24},{12,28},{16,0},{20,4},{24,8},{28,12},{1,17},{... | collective-permute-start | bytes 393224 | tf_op jit(solution)/shard_map/ppermute | solution.py:285
  44.6 0.6 %collective-permute-start.17 = (f32[64,512]{1,0:T(8,128)S(1)}, f32[64,512]{1,0:T(8,128)S(1)}, u32[]{:S(2)}, u32[]{:S(2)}) collective-permute-start(f32[64,512]{1,0:T(8,128)S(1)} %get-tuple-element.96), channel_id=1, source_target_pairs={{0,16},{4,20},{8,24},{12,28},{16,0},{20,4},{24,8},{28,12},{1,17},{... | collective-permute-start | bytes 393224 | tf_op jit(solution)/shard_map/ppermute | solution.py:285
  45.1 0.5 %collective-permute-start.19 = (f32[64,512]{1,0:T(8,128)S(1)}, f32[64,512]{1,0:T(8,128)S(1)}, u32[]{:S(2)}, u32[]{:S(2)}) collective-permute-start(f32[64,512]{1,0:T(8,128)S(1)} %get-tuple-element.99), channel_id=1, source_target_pairs={{0,8},{4,12},{8,0},{12,4},{16,24},{20,28},{24,16},{28,20},{1,9},{5... | collective-permute-start | bytes 393224 | tf_op jit(solution)/shard_map/ppermute | solution.py:285
  45.7 1.8 %query.1 = (f32[256,512]{1,0:T(8,128)}, f32[256,256]{1,0:T(8,128)}) custom-call(bf16[4,256,256]{2,1,0:T(8,128)(2,1)S(1)} %get-tuple-element.62.refs_0_, bf16[4,256,256]{2,1,0:T(8,128)(2,1)S(1)} %get-tuple-element.63.refs_1_, bf16[256,512]{1,0:T(8,128)(2,1)S(1)} %get-tuple-element.64.refs_2_, bf16[256,512]{1,0:T(8,128)(2,1)S(1)} %get-tuple-element.65.refs_3_, ...), custom_call_target="tpu_custom_call" | custom-call | tf_op jit(solution)/shard_map/query/pallas_call | solution.py:332
  47.5 0.7 %token_sum.1 = (f32[64,512]{1,0:T(8,128)}, f32[64,64]{1,0:T(8,128)}) custom-call(f32[72,512]{1,0:T(8,128)S(1)} %get-tuple-element.79.refs_0_, f32[72,512]{1,0:T(8,128)S(1)} %collective-permute-done.10.refs_1_, f32[72,512]{1,0:T(8,128)S(1)} %collective-permute-done.11.refs_2_, f32[72,512]{1,0:T(8,128)S(1)} %collective-permute-done.12.refs_3_), custom_call_target="tpu_custom_call" | custom-call | tf_op jit(solution)/shard_map/token_sum/pallas_call | solution.py:357
  48.2 0.4 collective-permute-done.18.refs_4_
  48.6 1.4 %collective-permute-done.17.refs_2_ = f32[64,512]{1,0:T(8,128)S(1)} collective-permute-done((f32[64,512]{1,0:T(8,128)S(1)}, f32[64,512]{1,0:T(8,128)S(1)}, u32[]{:S(2)}, u32[]{:S(2)}) %collective-permute-start.17) | collective-permute-done | bytes 131104 | tf_op jit(solution)/shard_map/ppermute | solution.py:285
  50.0 0.1 collective-permute-done.19.refs_5_
  50.1 0.7 %up_sum.1 = (f32[64,512]{1,0:T(8,128)}, f32[64,512]{1,0:T(8,128)}) custom-call(f32[64,512]{1,0:T(8,128)S(1)} %get-tuple-element.90.refs_0_, f32[64,512]{1,0:T(8,128)S(1)} %collective-permute-done.14.refs_1_, f32[64,512]{1,0:T(8,128)S(1)} %collective-permute-done.17.refs_2_, f32[64,512]{1,0:T(8,128)S(1)} %get-tuple-element.97.refs_3_, ...), custom_call_target="tpu_custom_call" | custom-call | tf_op jit(solution)/shard_map/up_sum/pallas_call | solution.py:361
  (17 shorter events, 0.2 us)
Async XLA Ops:
  1.7 13.3 %collective-permute-start.8 = (f32[128,512]{1,0:T(8,128)S(1)}, f32[128,512]{1,0:T(8,128)S(1)}, u32[]{:S(2)}, u32[]{:S(2)}) collective-permute-start(f32[128,512]{1,0:T(8,128)S(1)} %get-tuple-element.55.refs_4_), channel_id=1, source_target_pairs={{0,24},{4,28},{8,16},{12,20},{16,8},{20,12},{24,0},{28,4},{1,25},{... | collective-permute-start | bytes 786440 | tf_op jit(solution)/shard_map/ppermute | solution.py:285
  5.7 11.9 %collective-permute-start.6 = (f32[128,512]{1,0:T(8,128)S(1)}, f32[128,512]{1,0:T(8,128)S(1)}, u32[]{:S(2)}, u32[]{:S(2)}) collective-permute-start(f32[128,512]{1,0:T(8,128)S(1)} %get-tuple-element.55.refs_4_), channel_id=1, source_target_pairs={{0,16},{4,20},{8,24},{12,28},{16,0},{20,4},{24,8},{28,12},{1,17},{... | collective-permute-start | bytes 786440 | tf_op jit(solution)/shard_map/ppermute | solution.py:285
  6.2 11.7 %collective-permute-start.4 = (f32[128,512]{1,0:T(8,128)S(1)}, f32[128,512]{1,0:T(8,128)S(1)}, u32[]{:S(2)}, u32[]{:S(2)}) collective-permute-start(f32[128,512]{1,0:T(8,128)S(1)} %get-tuple-element.55.refs_4_), channel_id=1, source_target_pairs={{0,8},{4,12},{8,0},{12,4},{16,24},{20,28},{24,16},{28,20},{1,9},{5... | collective-permute-start | bytes 786440 | tf_op jit(solution)/shard_map/ppermute | solution.py:285
  6.4 8.7 %collective-permute-start.2 = (f32[72,512]{1,0:T(8,128)S(1)}, f32[72,512]{1,0:T(8,128)S(1)}, u32[]{:S(2)}, u32[]{:S(2)}) collective-permute-start(f32[72,512]{1,0:T(8,128)S(1)} %get-tuple-element.54.refs_0_), channel_id=1, source_target_pairs={{0,3},{1,2},{2,1},{3,0},{4,7},{5,6},{6,5},{7,4},{8,11},{9,10},{10,... | collective-permute-start | bytes 442376 | tf_op jit(solution)/shard_map/ppermute | solution.py:289
  10.4 11.6 %collective-permute-start.1 = (f32[72,512]{1,0:T(8,128)S(1)}, f32[72,512]{1,0:T(8,128)S(1)}, u32[]{:S(2)}, u32[]{:S(2)}) collective-permute-start(f32[72,512]{1,0:T(8,128)S(1)} %get-tuple-element.54.refs_0_), channel_id=1, source_target_pairs={{0,2},{1,3},{2,0},{3,1},{4,6},{5,7},{6,4},{7,5},{8,10},{9,11},{10,... | collective-permute-start | bytes 442376 | tf_op jit(solution)/shard_map/ppermute | solution.py:289
  15.0 12.1 %collective-permute-start.3 = (f32[128,512]{1,0:T(8,128)S(1)}, f32[128,512]{1,0:T(8,128)S(1)}, u32[]{:S(2)}, u32[]{:S(2)}) collective-permute-start(f32[128,512]{1,0:T(8,128)S(1)} %get-tuple-element.55.refs_4_), channel_id=1, source_target_pairs={{0,4},{4,0},{8,12},{12,8},{16,20},{20,16},{24,28},{28,24},{1,5},{5... | collective-permute-start | bytes 786440 | tf_op jit(solution)/shard_map/ppermute | solution.py:285
  15.1 12.1 %collective-permute-start.9 = (f32[128,512]{1,0:T(8,128)S(1)}, f32[128,512]{1,0:T(8,128)S(1)}, u32[]{:S(2)}, u32[]{:S(2)}) collective-permute-start(f32[128,512]{1,0:T(8,128)S(1)} %collective-permute-done.8.refs_10_), channel_id=1, source_target_pairs={{0,4},{4,0},{8,12},{12,8},{16,20},{20,16},{24,28},{28,24},{1,5},{5... | collective-permute-start | bytes 786440 | tf_op jit(solution)/shard_map/ppermute | solution.py:285
  17.6 9.5 %collective-permute-start.7 = (f32[128,512]{1,0:T(8,128)S(1)}, f32[128,512]{1,0:T(8,128)S(1)}, u32[]{:S(2)}, u32[]{:S(2)}) collective-permute-start(f32[128,512]{1,0:T(8,128)S(1)} %collective-permute-done.6.refs_8_), channel_id=1, source_target_pairs={{0,4},{4,0},{8,12},{12,8},{16,20},{20,16},{24,28},{28,24},{1,5},{5... | collective-permute-start | bytes 786440 | tf_op jit(solution)/shard_map/ppermute | solution.py:285
  17.9 9.2 %collective-permute-start.5 = (f32[128,512]{1,0:T(8,128)S(1)}, f32[128,512]{1,0:T(8,128)S(1)}, u32[]{:S(2)}, u32[]{:S(2)}) collective-permute-start(f32[128,512]{1,0:T(8,128)S(1)} %collective-permute-done.4.refs_6_), channel_id=1, source_target_pairs={{0,4},{4,0},{8,12},{12,8},{16,20},{20,16},{24,28},{28,24},{1,5},{5... | collective-permute-start | bytes 786440 | tf_op jit(solution)/shard_map/ppermute | solution.py:285
  22.0 5.1 %collective-permute-start = (f32[72,512]{1,0:T(8,128)S(1)}, f32[72,512]{1,0:T(8,128)S(1)}, u32[]{:S(2)}, u32[]{:S(2)}) collective-permute-start(f32[72,512]{1,0:T(8,128)S(1)} %get-tuple-element.54.refs_0_), channel_id=1, source_target_pairs={{0,1},{1,0},{2,3},{3,2},{4,5},{5,4},{6,7},{7,6},{8,9},{9,8},{10,11... | collective-permute-start | bytes 442376 | tf_op jit(solution)/shard_map/ppermute | solution.py:289
  31.7 4.3 %collective-permute-start.13 = (f32[4,64,1024]{2,1,0:T(8,128)S(1)}, f32[4,64,1024]{2,1,0:T(8,128)S(1)}, u32[]{:S(2)}, u32[]{:S(2)}) collective-permute-start(f32[4,64,1024]{2,1,0:T(8,128)S(1)} %get-tuple-element.85), channel_id=1, source_target_pairs={{0,4},{4,0},{8,12},{12,8},{16,20},{20,16},{24,28},{28,24},{1,5},{5... | collective-permute-start | bytes 3145736 | tf_op jit(solution)/shard_map/ppermute | solution.py:285
  32.9 11.7 %collective-permute-start.10 = (f32[72,512]{1,0:T(8,128)S(1)}, f32[72,512]{1,0:T(8,128)S(1)}, u32[]{:S(2)}, u32[]{:S(2)}) collective-permute-start(f32[72,512]{1,0:T(8,128)S(1)} %get-tuple-element.80), channel_id=1, source_target_pairs={{0,1},{1,0},{2,3},{3,2},{4,5},{5,4},{6,7},{7,6},{8,9},{9,8},{10,11... | collective-permute-start | bytes 442376 | tf_op jit(solution)/shard_map/ppermute | solution.py:289
  33.0 12.1 %collective-permute-start.11 = (f32[72,512]{1,0:T(8,128)S(1)}, f32[72,512]{1,0:T(8,128)S(1)}, u32[]{:S(2)}, u32[]{:S(2)}) collective-permute-start(f32[72,512]{1,0:T(8,128)S(1)} %get-tuple-element.81), channel_id=1, source_target_pairs={{0,2},{1,3},{2,0},{3,1},{4,6},{5,7},{6,4},{7,5},{8,10},{9,11},{10,... | collective-permute-start | bytes 442376 | tf_op jit(solution)/shard_map/ppermute | solution.py:289
  36.1 5.4 %collective-permute-start.15 = (f32[64,512]{1,0:T(8,128)S(1)}, f32[64,512]{1,0:T(8,128)S(1)}, u32[]{:S(2)}, u32[]{:S(2)}) collective-permute-start(f32[64,512]{1,0:T(8,128)S(1)} %get-tuple-element.94), channel_id=1, source_target_pairs={{0,8},{4,12},{8,0},{12,4},{16,24},{20,28},{24,16},{28,20},{1,9},{5... | collective-permute-start | bytes 393224 | tf_op jit(solution)/shard_map/ppermute | solution.py:285
  37.7 5.3 %collective-permute-start.16 = (f32[64,512]{1,0:T(8,128)S(1)}, f32[64,512]{1,0:T(8,128)S(1)}, u32[]{:S(2)}, u32[]{:S(2)}) collective-permute-start(f32[64,512]{1,0:T(8,128)S(1)} %get-tuple-element.95), channel_id=1, source_target_pairs={{0,16},{4,20},{8,24},{12,28},{16,0},{20,4},{24,8},{28,12},{1,17},{... | collective-permute-start | bytes 393224 | tf_op jit(solution)/shard_map/ppermute | solution.py:285
  39.2 8.3 %collective-permute-start.12 = (f32[72,512]{1,0:T(8,128)S(1)}, f32[72,512]{1,0:T(8,128)S(1)}, u32[]{:S(2)}, u32[]{:S(2)}) collective-permute-start(f32[72,512]{1,0:T(8,128)S(1)} %get-tuple-element.82), channel_id=1, source_target_pairs={{0,3},{1,2},{2,1},{3,0},{4,7},{5,6},{6,5},{7,4},{8,11},{9,10},{10,... | collective-permute-start | bytes 442376 | tf_op jit(solution)/shard_map/ppermute | solution.py:289
  41.5 6.6 %collective-permute-start.14 = (f32[64,512]{1,0:T(8,128)S(1)}, f32[64,512]{1,0:T(8,128)S(1)}, u32[]{:S(2)}, u32[]{:S(2)}) collective-permute-start(f32[64,512]{1,0:T(8,128)S(1)} %get-tuple-element.91), channel_id=1, source_target_pairs={{0,8},{4,12},{8,0},{12,4},{16,24},{20,28},{24,16},{28,20},{1,9},{5... | collective-permute-start | bytes 393224 | tf_op jit(solution)/shard_map/ppermute | solution.py:285
  43.0 5.6 %collective-permute-start.18 = (f32[64,512]{1,0:T(8,128)S(1)}, f32[64,512]{1,0:T(8,128)S(1)}, u32[]{:S(2)}, u32[]{:S(2)}) collective-permute-start(f32[64,512]{1,0:T(8,128)S(1)} %get-tuple-element.98), channel_id=1, source_target_pairs={{0,16},{4,20},{8,24},{12,28},{16,0},{20,4},{24,8},{28,12},{1,17},{... | collective-permute-start | bytes 393224 | tf_op jit(solution)/shard_map/ppermute | solution.py:285
  44.6 5.4 %collective-permute-start.17 = (f32[64,512]{1,0:T(8,128)S(1)}, f32[64,512]{1,0:T(8,128)S(1)}, u32[]{:S(2)}, u32[]{:S(2)}) collective-permute-start(f32[64,512]{1,0:T(8,128)S(1)} %get-tuple-element.96), channel_id=1, source_target_pairs={{0,16},{4,20},{8,24},{12,28},{16,0},{20,4},{24,8},{28,12},{1,17},{... | collective-permute-start | bytes 393224 | tf_op jit(solution)/shard_map/ppermute | solution.py:285
  45.1 5.0 %collective-permute-start.19 = (f32[64,512]{1,0:T(8,128)S(1)}, f32[64,512]{1,0:T(8,128)S(1)}, u32[]{:S(2)}, u32[]{:S(2)}) collective-permute-start(f32[64,512]{1,0:T(8,128)S(1)} %get-tuple-element.99), channel_id=1, source_target_pairs={{0,8},{4,12},{8,0},{12,4},{16,24},{20,28},{24,16},{28,20},{1,9},{5... | collective-permute-start | bytes 393224 | tf_op jit(solution)/shard_map/ppermute | solution.py:285

commit v4 on v3

--- a/solution.py
+++ b/solution.py
@@ -53,12 +53,8 @@
     return chips == 4
 
 
-def paired(ways):
-    return ways & (ways - 1) == 0
-
-
 def partner(mine, step, ways):
-    return jnp.bitwise_xor(mine, step) if paired(ways) else lax.rem(mine + step, ways)
+    return lax.rem(mine + step, ways)
 
 
 def rows_at(index, rows):
@@ -119,10 +115,9 @@
     up_refs, refs = refs[: 2 * chips], refs[2 * chips :]
     mask_ref, rope_ref, nope_refs, cot_refs, refs = refs[0], refs[1], refs[2:4], refs[4:6], refs[6:]
     keep_refs, refs = refs[:chips], refs[chips:]
-    send_ref, shared_grad_ref = refs[:2]
-    grad_scores_refs, key_rows_refs, shared_refs = refs[2:4], refs[4:6], refs[6:8]
-    key_grad_refs, value_grad_refs, key_up_refs, value_up_refs = refs[8:10], refs[10:12], refs[12:14], refs[14:16]
-    latent_all, shared_all, key_all, value_all, up_grad = refs[16:]
+    send_ref, share_refs, refs = refs[0], refs[1 : 1 + ways], refs[1 + ways :]
+    grad_scores_refs, key_rows_refs, shared_refs = refs[0:2], refs[2:4], refs[4:6]
+    latent_all, shared_all, key_all, value_all, up_grad = refs[6:]
     length, width = nope_refs[0].shape
     lat = latent_all.shape[1]
     rows = length // ways
@@ -142,8 +137,7 @@
 
     latent = split(latent_all[...])
     shared = keep_pair(shared_refs, shared_all[...])
-    key_up = keep_pair(key_up_refs, key_all[...])
-    value_up = keep_pair(value_up_refs, value_all[...])
+    key_up, value_up = split(key_all[...]), split(value_all[...])
     key_rows = keep_pair(key_rows_refs, product(latent, key_up, 1, 0))
     value_rows = split(product(latent, value_up, 1, 0))
 
@@ -187,28 +181,20 @@
         key_grads.append(key_part)
         shared_grad = shared_grad + shared_part
         ready = later
-    shared_grad_ref[...] = shared_grad[:, :ROPE] + shared_grad[:, ROPE:]
-    key_grad = keep_pair(key_grad_refs, jnp.concatenate(key_grads, axis=1))
-    value_grad = keep_pair(value_grad_refs, jnp.concatenate(value_grads, axis=1))
+    key_grad = split(jnp.concatenate(key_grads, axis=1))
+    value_grad = split(jnp.concatenate(value_grads, axis=1))
+
+    latent_all[...] = product(key_grad, key_up, 1, 1) + product(value_grad, value_up, 1, 1)
+    shared_all[...] = shared_grad[:, :ROPE] + shared_grad[:, ROPE:]
+    for step in range(ways):
+        at = rows_at(partner(mine, step, ways), rows)
+        pack_tokens(rows, lat, share_refs[step], latent_all[at, :], shared_all[at, :])
 
     up_grad[:, :width] = product(latent, key_grad, 0, 0)
     up_grad[:, width:] = product(latent, value_grad, 0, 0)
     for step in range(chips):
         keep_refs[step][...] = up_grad[rows_at(jnp.bitwise_xor(row, 2 * step), rows_up), :]
         send_ref[step, :, :] = up_grad[rows_at(jnp.bitwise_xor(row, 2 * step + 1), rows_up), :]
-
-
-def share_kernel(ways, shared_grad_ref, *refs):
-    key_grad, value_grad, key_up, value_up = [
-        (refs[2 * which][...], refs[2 * which + 1][...]) for which in range(4)
-    ]
-    share_refs, latent_all = refs[8 : 8 + ways], refs[8 + ways]
-    rows = shared_grad_ref.shape[0] // ways
-    lat = latent_all.shape[1]
-    latent_all[...] = product(key_grad, key_up, 1, 1) + product(value_grad, value_up, 1, 1)
-    for step in range(ways):
-        at = rows_at(partner(lax.axis_index("head"), step, ways), rows)
-        pack_tokens(rows, lat, share_refs[step], latent_all[at, :], shared_grad_ref[at, :])
 
 
 def query_kernel(*refs):
@@ -238,23 +224,31 @@
         refs[2 * count + which][...] = refs[which][...] + refs[count + which][...]
 
 
-def token_sum_kernel(ways, *refs):
-    latent_out, rope_out = refs[ways:]
-    rows, lat = latent_out.shape
-    total = refs[0][...]
-    for step in range(1, ways):
-        total = total + refs[step][...]
-    latent_out[...] = total[:rows, :]
-    rope_out[...] = unpack_narrow(rows, lat, total)
-
-
-def up_sum_kernel(*refs):
-    count = len(refs) // 2 - 1
-    for out, parts in ((refs[-2], refs[:count]), (refs[-1], refs[count:-2])):
-        total = parts[0][...]
-        for part in parts[1:]:
-            total = total + part[...]
-        out[...] = total
+def sum_kernel(counts, *refs):
+    refs, outs, sums, sems = refs[: sum(counts)], refs[-9:-5], refs[-5:-1], refs[-1]
+    latent_sum, rope_sum, key_sum, value_sum = sums
+    copies = [pltpu.make_async_copy(src, out, sems.at[which]) for which, (src, out) in enumerate(zip(sums, outs))]
+
+    def total(count):
+        nonlocal refs
+        value = refs[0][...]
+        for ref in refs[1:count]:
+            value = value + ref[...]
+        refs = refs[count:]
+        return value
+
+    tokens = total(counts[0])
+    rows, lat = latent_sum.shape
+    latent_sum[...] = tokens[:rows, :]
+    copies[0].start()
+    key_sum[...] = total(counts[1])
+    copies[2].start()
+    value_sum[...] = total(counts[2])
+    copies[3].start()
+    rope_sum[...] = unpack_narrow(rows, lat, tokens)
+    copies[1].start()
+    for copy in copies:
+        copy.wait()
 
 
 def vmem(*arrays):
@@ -285,8 +279,7 @@
         return lax.ppermute(x, "fsdp", [(i, i ^ step) for i in range(fsdp)])
 
     def shift(x, step):
-        to = [(i, i ^ step if paired(ways) else (i + step) % ways) for i in range(ways)]
-        return lax.ppermute(x, "head", to)
+        return lax.ppermute(x, "head", [(i, (i + step) % ways) for i in range(ways)])
 
     tokens, ups = pl.pallas_call(
         pack_kernel, out_shape=(pltpu.VMEM((packed, lat), F32), pltpu.VMEM((2 * rows_up, width), F32)),
@@ -294,14 +287,14 @@
         scratch_shapes=[pltpu.VMEM((rows, ROPE), F32), dma((4,))],
         compiler_params=limit(4), name="pack",
     )(*stored(latent, rope_key, key_up, value_up))
-    token_blocks = [tokens] + [shift(tokens, step if paired(ways) else ways - step) for step in range(1, ways)]
+    token_blocks = [tokens] + [shift(tokens, ways - step) for step in range(1, ways)]
     even = [ups] + [swap(ups, 2 * step) for step in range(1, chips)]
     odd = [swap(block, 1) for block in even]
     up_blocks = [block for pair in zip(even, odd) for block in pair]
 
     heads = width // NOPE
     wide, whole = (length, width), (lat, width)
-    pairs = [(heads, length, length), wide, (length, ROPE), wide, wide, whole, whole]
+    pairs = [(heads, length, length), wide, (length, ROPE)]
     queries = pl.pallas_call(
         prepare_kernel,
         out_shape=[pltpu.VMEM((length, length), F32)]
@@ -312,27 +305,22 @@
         functools.partial(attention_kernel, ways, chips),
         out_shape=(
             *([pltpu.VMEM((rows_up, 2 * width), F32)] * chips), pltpu.VMEM((chips, rows_up, 2 * width), F32),
-            pltpu.VMEM((length, ROPE), F32), *[pltpu.VMEM(dims, BF16) for dims in pairs for _ in range(2)],
+            *([pltpu.VMEM((packed, lat), F32)] * ways), *[pltpu.VMEM(dims, BF16) for dims in pairs for _ in range(2)],
         ),
         in_specs=[VMEM] * (ways + fsdp + 6),
-        out_specs=[VMEM] * (chips + 2 + 2 * len(pairs)),
+        out_specs=[VMEM] * (chips + 1 + ways + 2 * len(pairs)),
         scratch_shapes=[
             pltpu.VMEM((length, lat), F32), pltpu.VMEM((length, ROPE), F32),
             pltpu.VMEM(whole, F32), pltpu.VMEM(whole, F32), pltpu.VMEM((lat, 2 * width), F32),
         ],
         compiler_params=limit(24), name="attention",
     )(*vmem(*token_blocks, *up_blocks, *queries))
-    keep, send, shared_grad, pairs = out[:chips], out[chips], out[chips + 1], out[chips + 2 :]
-
-    shares = pl.pallas_call(
-        functools.partial(share_kernel, ways), out_shape=[pltpu.VMEM((packed, lat), F32)] * ways,
-        in_specs=[VMEM] * 9, out_specs=[VMEM] * ways,
-        scratch_shapes=[pltpu.VMEM((length, lat), F32)], compiler_params=limit(8), name="share",
-    )(*vmem(shared_grad, *pairs[6:]))
+    keep, send, shares, pairs = out[:chips], out[chips], out[chips + 1 : chips + 1 + ways], out[chips + 1 + ways :]
+
     nope_grad, rope_grad = pl.pallas_call(
         query_kernel, out_shape=(hbm(*wide), hbm(*query_rope.shape)),
         in_specs=[VMEM] * 6, out_specs=[VMEM] * 2, compiler_params=limit(8), name="query",
-    )(*vmem(*pairs[:6]))
+    )(*vmem(*pairs))
 
     block = pltpu.VMEM((rows_up, width), F32)
     received = swap(send, 1)
@@ -354,14 +342,14 @@
         key_parts = keys[:1] + [swap(keys[step], 2 * step) for step in range(1, chips)]
         value_parts = values[:1] + [swap(values[step], 2 * step) for step in range(1, chips)]
     pieces = [shares[0]] + [shift(shares[step], step) for step in range(1, ways)]
-    latent_grad, rope_key_grad = pl.pallas_call(
-        functools.partial(token_sum_kernel, ways), out_shape=(hbm(rows, lat), hbm(rows, ROPE)),
-        in_specs=[VMEM] * ways, out_specs=[VMEM] * 2, compiler_params=limit(4), name="token_sum",
-    )(*vmem(*pieces))
-    key_up_grad, value_up_grad = pl.pallas_call(
-        up_sum_kernel, out_shape=(hbm(rows_up, width), hbm(rows_up, width)),
-        in_specs=[VMEM] * (2 * len(key_parts)), out_specs=[VMEM] * 2, compiler_params=limit(4), name="up_sum",
-    )(*vmem(*key_parts, *value_parts))
+    finals = [(rows, lat), (rows, ROPE), (rows_up, width), (rows_up, width)]
+    counts = len(pieces), len(key_parts), len(value_parts)
+    latent_grad, rope_key_grad, key_up_grad, value_up_grad = pl.pallas_call(
+        functools.partial(sum_kernel, counts), out_shape=[hbm(*dims) for dims in finals],
+        in_specs=[VMEM] * sum(counts), out_specs=[HBM] * 4,
+        scratch_shapes=[pltpu.VMEM(dims, F32) for dims in finals] + [dma((4,))],
+        compiler_params=limit(6), name="sums",
+    )(*vmem(*pieces, *key_parts, *value_parts))
     return nope_grad, rope_grad, latent_grad, rope_key_grad, key_up_grad, value_up_grad
 
 

time: 51.5 us -> 52.2 us (1.014); the launches traced: 50.9 us -> 52.1 us
  starting transfers between devices: 21.1 us -> 26.5 us
  waiting for transfers between devices: 17.2 us -> 14.1 us
  Pallas kernels: 11.8 us -> 10.8 us
    ppermute x6, starting transfers between devices: 8.46 us -> 13.6 us  [shift(): lax.ppermute(x, 'head', [(i, (i + step) % ways) for i in range(ways)])]
    ppermute x6, waiting for transfers between devices: 11.9 us -> 8.6 us  [shift(): lax.ppermute(x, 'head', [(i, (i + step) % ways) for i in range(ways)])]
    pallas_call x3 -> x1, Pallas kernels: 2.48 us -> 0.81 us  [on_device(): pl.pallas_call(functools.partial(sum_kernel, counts), out_shape=[hbm(*dim...]
    pallas_call x1, Pallas kernels: 4.58 us -> 5.22 us  [on_device(): pl.pallas_call(functools.partial(attention_kernel, ways, chips), out_shap...]
  transfers between devices with their start and end apart: 20 -> 20, of which waited for: 9 -> 9; matrix products, arithmetic and copies ran while one was open for 0% -> 0% of each run, Pallas kernels for 11% -> 7%
where the time goes in v4:
time: 52.2 us; the launch traced here: 52.1 us
  starting transfers between devices  26.5 us (51%)
  waiting for transfers between devices  14.1 us (27%)
  Pallas kernels  10.8 us (21%)
  between operations  0.71 us (1%)
    ppermute x6, starting transfers between devices, shift(): lax.ppermute(x, 'head', [(i, (i + step) % ways) for i in range(ways)])  13.6 us
    ppermute x14, starting transfers between devices, swap(): return lax.ppermute(x, 'fsdp', [(i, i ^ step) for i in range(fsdp)])  12.8 us
    ppermute x6, waiting for transfers between devices, shift(): lax.ppermute(x, 'head', [(i, (i + step) % ways) for i in range(ways)])  8.6 us
    ppermute x14, waiting for transfers between devices, swap(): return lax.ppermute(x, 'fsdp', [(i, i ^ step) for i in range(fsdp)])  5.5 us
    pallas_call x1, Pallas kernels, on_device(): pl.pallas_call(functools.partial(attention_kernel, ways, chips), out_shap...  5.22 us
    pallas_call x1, Pallas kernels, on_device(): pl.pallas_call(query_kernel, out_shape=(hbm(*wide), hbm(*query_rope.shape...  1.78 us
    pallas_call x1, Pallas kernels, on_device(): pl.pallas_call(prepare_kernel, out_shape=[pltpu.VMEM((length, length), F3...  1.76 us
    pallas_call x1, Pallas kernels, on_device(): pl.pallas_call(pack_kernel, out_shape=(pltpu.VMEM((packed, lat), F32), pl...  1.09 us
  transfers between devices with their start and end apart: 20, of which 9 were waited for; matrix products, arithmetic and copies ran while one was open for 0% of the time, Pallas kernels for 7%

profile of v4, /device:TPU:0, one launch (start us, length us, event | category | flops | bytes accessed | tf_op | source)
XLA Modules:
  0.0 52.1 jit_solution(10032633612553593539)
XLA Ops:
  0.6 1.1 %pack.1 = (f32[72,512]{1,0:T(8,128)S(1)}, f32[128,512]{1,0:T(8,128)S(1)}) custom-call(f32[64,512]{1,0:T(8,128)} %latent_ref.1, f32[64,64]{1,0:T(8,128)} %rope_ref.2, f32[64,512]{1,0:T(8,128)} %key_ref.1, f32[64,512]{1,0:T(8,128)} %value_ref.1), custom_call_target="tpu_custom_call" | custom-call | tf_op jit(solution)/shard_map/pack/pallas_call | solution.py:284
  1.7 4.0 %collective-permute-start.8 = (f32[128,512]{1,0:T(8,128)S(1)}, f32[128,512]{1,0:T(8,128)S(1)}, u32[]{:S(2)}, u32[]{:S(2)}) collective-permute-start(f32[128,512]{1,0:T(8,128)S(1)} %get-tuple-element.46.refs_4_), channel_id=1, source_target_pairs={{0,24},{4,28},{8,16},{12,20},{16,8},{20,12},{24,0},{28,4},{1,25},{... | collective-permute-start | bytes 786440 | tf_op jit(solution)/shard_map/ppermute | solution.py:279
  5.7 0.5 collective-permute-start.6
  6.2 0.1 collective-permute-start.4
  6.4 2.0 %collective-permute-start.2 = (f32[72,512]{1,0:T(8,128)S(1)}, f32[72,512]{1,0:T(8,128)S(1)}, u32[]{:S(2)}, u32[]{:S(2)}) collective-permute-start(f32[72,512]{1,0:T(8,128)S(1)} %get-tuple-element.45.refs_0_), channel_id=1, source_target_pairs={{0,1},{1,2},{2,3},{3,0},{4,5},{5,6},{6,7},{7,4},{8,9},{9,10},{10,1... | collective-permute-start | bytes 442376 | tf_op jit(solution)/shard_map/ppermute | solution.py:282
  8.3 2.6 %collective-permute-start.1 = (f32[72,512]{1,0:T(8,128)S(1)}, f32[72,512]{1,0:T(8,128)S(1)}, u32[]{:S(2)}, u32[]{:S(2)}) collective-permute-start(f32[72,512]{1,0:T(8,128)S(1)} %get-tuple-element.45.refs_0_), channel_id=1, source_target_pairs={{0,2},{1,3},{2,0},{3,1},{4,6},{5,7},{6,4},{7,5},{8,10},{9,11},{10,... | collective-permute-start | bytes 442376 | tf_op jit(solution)/shard_map/ppermute | solution.py:282
  10.9 4.1 %collective-permute-done.2.refs_3_ = f32[72,512]{1,0:T(8,128)S(1)} collective-permute-done((f32[72,512]{1,0:T(8,128)S(1)}, f32[72,512]{1,0:T(8,128)S(1)}, u32[]{:S(2)}, u32[]{:S(2)}) %collective-permute-start.2) | collective-permute-done | bytes 147488 | tf_op jit(solution)/shard_map/ppermute | solution.py:282
  15.0 0.5 collective-permute-start.9
  15.6 2.1 %collective-permute-done.6.refs_8_ = f32[128,512]{1,0:T(8,128)S(1)} collective-permute-done((f32[128,512]{1,0:T(8,128)S(1)}, f32[128,512]{1,0:T(8,128)S(1)}, u32[]{:S(2)}, u32[]{:S(2)}) %collective-permute-start.6) | collective-permute-done | bytes 262176 | tf_op jit(solution)/shard_map/ppermute | solution.py:279
  17.7 0.3 collective-permute-done.4.refs_6_
  17.9 0.2 collective-permute-start.5
  18.2 1.5 %collective-permute-done.1.refs_2_ = f32[72,512]{1,0:T(8,128)S(1)} collective-permute-done((f32[72,512]{1,0:T(8,128)S(1)}, f32[72,512]{1,0:T(8,128)S(1)}, u32[]{:S(2)}, u32[]{:S(2)}) %collective-permute-start.1) | collective-permute-done | bytes 147488 | tf_op jit(solution)/shard_map/ppermute | solution.py:282
  19.7 2.3 %collective-permute-start = (f32[72,512]{1,0:T(8,128)S(1)}, f32[72,512]{1,0:T(8,128)S(1)}, u32[]{:S(2)}, u32[]{:S(2)}) collective-permute-start(f32[72,512]{1,0:T(8,128)S(1)} %get-tuple-element.45.refs_0_), channel_id=1, source_target_pairs={{0,3},{1,0},{2,1},{3,2},{4,7},{5,4},{6,5},{7,6},{8,11},{9,8},{10,9... | collective-permute-start | bytes 442376 | tf_op jit(solution)/shard_map/ppermute | solution.py:282
  22.0 1.8 %prepare.1 = (f32[256,256]{1,0:T(8,128)S(1)}, bf16[4,256,192]{2,1,0:T(8,128)(2,1)S(1)}, bf16[256,512]{1,0:T(8,128)(2,1)S(1)}, bf16[256,512]{1,0:T(8,128)(2,1)S(1...) custom-call(s32[1,2]{1,0:T(1,128)} %limit_ref.1, f32[256,512]{1,0:T(8,128)} %nope_ref.1, ...), custom_call_target="tpu_custom_call" | custom-call | tf_op jit(solution)/shard_map/prepare/pallas_call | solution.py:298
  23.7 1.7 %collective-permute-done.refs_1_ = f32[72,512]{1,0:T(8,128)S(1)} collective-permute-done((f32[72,512]{1,0:T(8,128)S(1)}, f32[72,512]{1,0:T(8,128)S(1)}, u32[]{:S(2)}, u32[]{:S(2)}) %collective-permute-start) | collective-permute-done | bytes 147488 | tf_op jit(solution)/shard_map/ppermute | solution.py:282
  25.5 5.2 %attention.1 = (f32[64,1024]{1,0:T(8,128)S(1)}, f32[64,1024]{1,0:T(8,128)S(1)}, f32[64,1024]{1,0:T(8,128)S(1)}, f32[64,1024]{1,0:T(8,128)S(1)}, f32[4,64,1024]{2...) custom-call(f32[72,512]{1,0:T(8,128)S(1)} %get-tuple-element.45.refs, ...), custom_call_target="tpu_custom_call" | custom-call | tf_op jit(solution)/shard_map/attention/pallas_call | solution.py:304
  30.8 0.4 collective-permute-start.10
  31.2 4.4 %collective-permute-start.11 = (f32[72,512]{1,0:T(8,128)S(1)}, f32[72,512]{1,0:T(8,128)S(1)}, u32[]{:S(2)}, u32[]{:S(2)}) collective-permute-start(f32[72,512]{1,0:T(8,128)S(1)} %get-tuple-element.63), channel_id=1, source_target_pairs={{0,2},{1,3},{2,0},{3,1},{4,6},{5,7},{6,4},{7,5},{8,10},{9,11},{10,... | collective-permute-start | bytes 442376 | tf_op jit(solution)/shard_map/ppermute | solution.py:282
  35.6 0.1 join.1
  35.7 1.6 %collective-permute-start.15 = (f32[64,512]{1,0:T(8,128)S(1)}, f32[64,512]{1,0:T(8,128)S(1)}, u32[]{:S(2)}, u32[]{:S(2)}) collective-permute-start(f32[64,512]{1,0:T(8,128)S(1)} %get-tuple-element.74), channel_id=1, source_target_pairs={{0,8},{4,12},{8,0},{12,4},{16,24},{20,28},{24,16},{28,20},{1,9},{5... | collective-permute-start | bytes 393224 | tf_op jit(solution)/shard_map/ppermute | solution.py:279
  37.2 0.8 %collective-permute-start.16 = (f32[64,512]{1,0:T(8,128)S(1)}, f32[64,512]{1,0:T(8,128)S(1)}, u32[]{:S(2)}, u32[]{:S(2)}) collective-permute-start(f32[64,512]{1,0:T(8,128)S(1)} %get-tuple-element.75), channel_id=1, source_target_pairs={{0,16},{4,20},{8,24},{12,28},{16,0},{20,4},{24,8},{28,12},{1,17},{... | collective-permute-start | bytes 393224 | tf_op jit(solution)/shard_map/ppermute | solution.py:279
  38.0 2.0 %collective-permute-start.12 = (f32[72,512]{1,0:T(8,128)S(1)}, f32[72,512]{1,0:T(8,128)S(1)}, u32[]{:S(2)}, u32[]{:S(2)}) collective-permute-start(f32[72,512]{1,0:T(8,128)S(1)} %get-tuple-element.64), channel_id=1, source_target_pairs={{0,3},{1,0},{2,1},{3,2},{4,7},{5,4},{6,5},{7,6},{8,11},{9,8},{10,9... | collective-permute-start | bytes 442376 | tf_op jit(solution)/shard_map/ppermute | solution.py:282
  40.0 1.0 %collective-permute-done.15.refs_2_ = f32[64,512]{1,0:T(8,128)S(1)} collective-permute-done((f32[64,512]{1,0:T(8,128)S(1)}, f32[64,512]{1,0:T(8,128)S(1)}, u32[]{:S(2)}, u32[]{:S(2)}) %collective-permute-start.15) | collective-permute-done | bytes 131104 | tf_op jit(solution)/shard_map/ppermute | solution.py:279
  41.0 1.5 %collective-permute-start.14 = (f32[64,512]{1,0:T(8,128)S(1)}, f32[64,512]{1,0:T(8,128)S(1)}, u32[]{:S(2)}, u32[]{:S(2)}) collective-permute-start(f32[64,512]{1,0:T(8,128)S(1)} %get-tuple-element.71), channel_id=1, source_target_pairs={{0,8},{4,12},{8,0},{12,4},{16,24},{20,28},{24,16},{28,20},{1,9},{5... | collective-permute-start | bytes 393224 | tf_op jit(solution)/shard_map/ppermute | solution.py:279
  42.5 0.8 %collective-permute-start.18 = (f32[64,512]{1,0:T(8,128)S(1)}, f32[64,512]{1,0:T(8,128)S(1)}, u32[]{:S(2)}, u32[]{:S(2)}) collective-permute-start(f32[64,512]{1,0:T(8,128)S(1)} %get-tuple-element.78), channel_id=1, source_target_pairs={{0,16},{4,20},{8,24},{12,28},{16,0},{20,4},{24,8},{28,12},{1,17},{... | collective-permute-start | bytes 393224 | tf_op jit(solution)/shard_map/ppermute | solution.py:279
  43.3 1.3 %collective-permute-start.17 = (f32[64,512]{1,0:T(8,128)S(1)}, f32[64,512]{1,0:T(8,128)S(1)}, u32[]{:S(2)}, u32[]{:S(2)}) collective-permute-start(f32[64,512]{1,0:T(8,128)S(1)} %get-tuple-element.76), channel_id=1, source_target_pairs={{0,16},{4,20},{8,24},{12,28},{16,0},{20,4},{24,8},{28,12},{1,17},{... | collective-permute-start | bytes 393224 | tf_op jit(solution)/shard_map/ppermute | solution.py:279
  44.6 1.2 %collective-permute-done.11.refs_2_ = f32[72,512]{1,0:T(8,128)S(1)} collective-permute-done((f32[72,512]{1,0:T(8,128)S(1)}, f32[72,512]{1,0:T(8,128)S(1)}, u32[]{:S(2)}, u32[]{:S(2)}) %collective-permute-start.11) | collective-permute-done | bytes 147488 | tf_op jit(solution)/shard_map/ppermute | solution.py:282
  45.9 1.5 %collective-permute-start.19 = (f32[64,512]{1,0:T(8,128)S(1)}, f32[64,512]{1,0:T(8,128)S(1)}, u32[]{:S(2)}, u32[]{:S(2)}) collective-permute-start(f32[64,512]{1,0:T(8,128)S(1)} %get-tuple-element.79), channel_id=1, source_target_pairs={{0,8},{4,12},{8,0},{12,4},{16,24},{20,28},{24,16},{28,20},{1,9},{5... | collective-permute-start | bytes 393224 | tf_op jit(solution)/shard_map/ppermute | solution.py:279
  47.3 1.8 %query.1 = (f32[256,512]{1,0:T(8,128)}, f32[256,256]{1,0:T(8,128)}) custom-call(bf16[4,256,256]{2,1,0:T(8,128)(2,1)S(1)} %get-tuple-element.53.refs_0_, bf16[4,256,256]{2,1,0:T(8,128)(2,1)S(1)} %get-tuple-element.54.refs_1_, bf16[256,512]{1,0:T(8,128)(2,1)S(1)} %get-tuple-element.55.refs_2_, bf16[256,512]{1,0:T(8,128)(2,1)S(1)} %get-tuple-element.56.refs_3_, ...), custom_call_target="tpu_custom_call" | custom-call | tf_op jit(solution)/shard_map/query/pallas_call | solution.py:320
  49.1 0.3 collective-permute-done.17.refs_6_
  49.5 1.8 %collective-permute-done.19.refs_9_ = f32[64,512]{1,0:T(8,128)S(1)} collective-permute-done((f32[64,512]{1,0:T(8,128)S(1)}, f32[64,512]{1,0:T(8,128)S(1)}, u32[]{:S(2)}, u32[]{:S(2)}) %collective-permute-start.19) | collective-permute-done | bytes 131104 | tf_op jit(solution)/shard_map/ppermute | solution.py:279
  51.3 0.8 %sums.1 = (f32[64,512]{1,0:T(8,128)}, f32[64,64]{1,0:T(8,128)}, f32[64,512]{1,0:T(8,128)}, f32[64,512]{1,0:T(8,128)}) custom-call(f32[72,512]{1,0:T(8,128)S(1)} %get-tuple-element.61.refs_0_, f32[72,512]{1,0:T(8,128)S(1)} %collective-permute-done.10.refs_1_, f32[72,512]{1,0:T(8,128)S(1)} %collective-permute-done.11.refs_2_, ...), custom_call_target="tpu_custom_call" | custom-call | tf_op jit(solution)/shard_map/sums/pallas_call | solution.py:347
  (15 shorter events, 0.1 us)
Async XLA Ops:
  1.7 13.3 %collective-permute-start.8 = (f32[128,512]{1,0:T(8,128)S(1)}, f32[128,512]{1,0:T(8,128)S(1)}, u32[]{:S(2)}, u32[]{:S(2)}) collective-permute-start(f32[128,512]{1,0:T(8,128)S(1)} %get-tuple-element.46.refs_4_), channel_id=1, source_target_pairs={{0,24},{4,28},{8,16},{12,20},{16,8},{20,12},{24,0},{28,4},{1,25},{... | collective-permute-start | bytes 786440 | tf_op jit(solution)/shard_map/ppermute | solution.py:279
  5.7 11.9 %collective-permute-start.6 = (f32[128,512]{1,0:T(8,128)S(1)}, f32[128,512]{1,0:T(8,128)S(1)}, u32[]{:S(2)}, u32[]{:S(2)}) collective-permute-start(f32[128,512]{1,0:T(8,128)S(1)} %get-tuple-element.46.refs_4_), channel_id=1, source_target_pairs={{0,16},{4,20},{8,24},{12,28},{16,0},{20,4},{24,8},{28,12},{1,17},{... | collective-permute-start | bytes 786440 | tf_op jit(solution)/shard_map/ppermute | solution.py:279
  6.2 11.7 %collective-permute-start.4 = (f32[128,512]{1,0:T(8,128)S(1)}, f32[128,512]{1,0:T(8,128)S(1)}, u32[]{:S(2)}, u32[]{:S(2)}) collective-permute-start(f32[128,512]{1,0:T(8,128)S(1)} %get-tuple-element.46.refs_4_), channel_id=1, source_target_pairs={{0,8},{4,12},{8,0},{12,4},{16,24},{20,28},{24,16},{28,20},{1,9},{5... | collective-permute-start | bytes 786440 | tf_op jit(solution)/shard_map/ppermute | solution.py:279
  6.4 8.7 %collective-permute-start.2 = (f32[72,512]{1,0:T(8,128)S(1)}, f32[72,512]{1,0:T(8,128)S(1)}, u32[]{:S(2)}, u32[]{:S(2)}) collective-permute-start(f32[72,512]{1,0:T(8,128)S(1)} %get-tuple-element.45.refs_0_), channel_id=1, source_target_pairs={{0,1},{1,2},{2,3},{3,0},{4,5},{5,6},{6,7},{7,4},{8,9},{9,10},{10,1... | collective-permute-start | bytes 442376 | tf_op jit(solution)/shard_map/ppermute | solution.py:282
  8.3 11.3 %collective-permute-start.1 = (f32[72,512]{1,0:T(8,128)S(1)}, f32[72,512]{1,0:T(8,128)S(1)}, u32[]{:S(2)}, u32[]{:S(2)}) collective-permute-start(f32[72,512]{1,0:T(8,128)S(1)} %get-tuple-element.45.refs_0_), channel_id=1, source_target_pairs={{0,2},{1,3},{2,0},{3,1},{4,6},{5,7},{6,4},{7,5},{8,10},{9,11},{10,... | collective-permute-start | bytes 442376 | tf_op jit(solution)/shard_map/ppermute | solution.py:282
  15.0 10.4 %collective-permute-start.3 = (f32[128,512]{1,0:T(8,128)S(1)}, f32[128,512]{1,0:T(8,128)S(1)}, u32[]{:S(2)}, u32[]{:S(2)}) collective-permute-start(f32[128,512]{1,0:T(8,128)S(1)} %get-tuple-element.46.refs_4_), channel_id=1, source_target_pairs={{0,4},{4,0},{8,12},{12,8},{16,20},{20,16},{24,28},{28,24},{1,5},{5... | collective-permute-start | bytes 786440 | tf_op jit(solution)/shard_map/ppermute | solution.py:279
  15.0 10.4 %collective-permute-start.9 = (f32[128,512]{1,0:T(8,128)S(1)}, f32[128,512]{1,0:T(8,128)S(1)}, u32[]{:S(2)}, u32[]{:S(2)}) collective-permute-start(f32[128,512]{1,0:T(8,128)S(1)} %collective-permute-done.8.refs_10_), channel_id=1, source_target_pairs={{0,4},{4,0},{8,12},{12,8},{16,20},{20,16},{24,28},{28,24},{1,5},{5... | collective-permute-start | bytes 786440 | tf_op jit(solution)/shard_map/ppermute | solution.py:279
  17.6 7.8 %collective-permute-start.7 = (f32[128,512]{1,0:T(8,128)S(1)}, f32[128,512]{1,0:T(8,128)S(1)}, u32[]{:S(2)}, u32[]{:S(2)}) collective-permute-start(f32[128,512]{1,0:T(8,128)S(1)} %collective-permute-done.6.refs_8_), channel_id=1, source_target_pairs={{0,4},{4,0},{8,12},{12,8},{16,20},{20,16},{24,28},{28,24},{1,5},{5... | collective-permute-start | bytes 786440 | tf_op jit(solution)/shard_map/ppermute | solution.py:279
  17.9 7.5 %collective-permute-start.5 = (f32[128,512]{1,0:T(8,128)S(1)}, f32[128,512]{1,0:T(8,128)S(1)}, u32[]{:S(2)}, u32[]{:S(2)}) collective-permute-start(f32[128,512]{1,0:T(8,128)S(1)} %collective-permute-done.4.refs_6_), channel_id=1, source_target_pairs={{0,4},{4,0},{8,12},{12,8},{16,20},{20,16},{24,28},{28,24},{1,5},{5... | collective-permute-start | bytes 786440 | tf_op jit(solution)/shard_map/ppermute | solution.py:279
  19.7 5.8 %collective-permute-start = (f32[72,512]{1,0:T(8,128)S(1)}, f32[72,512]{1,0:T(8,128)S(1)}, u32[]{:S(2)}, u32[]{:S(2)}) collective-permute-start(f32[72,512]{1,0:T(8,128)S(1)} %get-tuple-element.45.refs_0_), channel_id=1, source_target_pairs={{0,3},{1,0},{2,1},{3,2},{4,7},{5,4},{6,5},{7,6},{8,11},{9,8},{10,9... | collective-permute-start | bytes 442376 | tf_op jit(solution)/shard_map/ppermute | solution.py:282
  30.7 4.8 %collective-permute-start.13 = (f32[4,64,1024]{2,1,0:T(8,128)S(1)}, f32[4,64,1024]{2,1,0:T(8,128)S(1)}, u32[]{:S(2)}, u32[]{:S(2)}) collective-permute-start(f32[4,64,1024]{2,1,0:T(8,128)S(1)} %get-tuple-element.65), channel_id=1, source_target_pairs={{0,4},{4,0},{8,12},{12,8},{16,20},{20,16},{24,28},{28,24},{1,5},{5... | collective-permute-start | bytes 3145736 | tf_op jit(solution)/shard_map/ppermute | solution.py:279
  30.8 12.5 %collective-permute-start.10 = (f32[72,512]{1,0:T(8,128)S(1)}, f32[72,512]{1,0:T(8,128)S(1)}, u32[]{:S(2)}, u32[]{:S(2)}) collective-permute-start(f32[72,512]{1,0:T(8,128)S(1)} %get-tuple-element.62), channel_id=1, source_target_pairs={{0,1},{1,2},{2,3},{3,0},{4,5},{5,6},{6,7},{7,4},{8,9},{9,10},{10,1... | collective-permute-start | bytes 442376 | tf_op jit(solution)/shard_map/ppermute | solution.py:282
  31.2 14.7 %collective-permute-start.11 = (f32[72,512]{1,0:T(8,128)S(1)}, f32[72,512]{1,0:T(8,128)S(1)}, u32[]{:S(2)}, u32[]{:S(2)}) collective-permute-start(f32[72,512]{1,0:T(8,128)S(1)} %get-tuple-element.63), channel_id=1, source_target_pairs={{0,2},{1,3},{2,0},{3,1},{4,6},{5,7},{6,4},{7,5},{8,10},{9,11},{10,... | collective-permute-start | bytes 442376 | tf_op jit(solution)/shard_map/ppermute | solution.py:282
  35.7 5.4 %collective-permute-start.15 = (f32[64,512]{1,0:T(8,128)S(1)}, f32[64,512]{1,0:T(8,128)S(1)}, u32[]{:S(2)}, u32[]{:S(2)}) collective-permute-start(f32[64,512]{1,0:T(8,128)S(1)} %get-tuple-element.74), channel_id=1, source_target_pairs={{0,8},{4,12},{8,0},{12,4},{16,24},{20,28},{24,16},{28,20},{1,9},{5... | collective-permute-start | bytes 393224 | tf_op jit(solution)/shard_map/ppermute | solution.py:279
  37.2 5.3 %collective-permute-start.16 = (f32[64,512]{1,0:T(8,128)S(1)}, f32[64,512]{1,0:T(8,128)S(1)}, u32[]{:S(2)}, u32[]{:S(2)}) collective-permute-start(f32[64,512]{1,0:T(8,128)S(1)} %get-tuple-element.75), channel_id=1, source_target_pairs={{0,16},{4,20},{8,24},{12,28},{16,0},{20,4},{24,8},{28,12},{1,17},{... | collective-permute-start | bytes 393224 | tf_op jit(solution)/shard_map/ppermute | solution.py:279
  38.0 11.1 %collective-permute-start.12 = (f32[72,512]{1,0:T(8,128)S(1)}, f32[72,512]{1,0:T(8,128)S(1)}, u32[]{:S(2)}, u32[]{:S(2)}) collective-permute-start(f32[72,512]{1,0:T(8,128)S(1)} %get-tuple-element.64), channel_id=1, source_target_pairs={{0,3},{1,0},{2,1},{3,2},{4,7},{5,4},{6,5},{7,6},{8,11},{9,8},{10,9... | collective-permute-start | bytes 442376 | tf_op jit(solution)/shard_map/ppermute | solution.py:282
  41.0 8.1 %collective-permute-start.14 = (f32[64,512]{1,0:T(8,128)S(1)}, f32[64,512]{1,0:T(8,128)S(1)}, u32[]{:S(2)}, u32[]{:S(2)}) collective-permute-start(f32[64,512]{1,0:T(8,128)S(1)} %get-tuple-element.71), channel_id=1, source_target_pairs={{0,8},{4,12},{8,0},{12,4},{16,24},{20,28},{24,16},{28,20},{1,9},{5... | collective-permute-start | bytes 393224 | tf_op jit(solution)/shard_map/ppermute | solution.py:279
  42.5 6.6 %collective-permute-start.18 = (f32[64,512]{1,0:T(8,128)S(1)}, f32[64,512]{1,0:T(8,128)S(1)}, u32[]{:S(2)}, u32[]{:S(2)}) collective-permute-start(f32[64,512]{1,0:T(8,128)S(1)} %get-tuple-element.78), channel_id=1, source_target_pairs={{0,16},{4,20},{8,24},{12,28},{16,0},{20,4},{24,8},{28,12},{1,17},{... | collective-permute-start | bytes 393224 | tf_op jit(solution)/shard_map/ppermute | solution.py:279
  43.3 6.1 %collective-permute-start.17 = (f32[64,512]{1,0:T(8,128)S(1)}, f32[64,512]{1,0:T(8,128)S(1)}, u32[]{:S(2)}, u32[]{:S(2)}) collective-permute-start(f32[64,512]{1,0:T(8,128)S(1)} %get-tuple-element.76), channel_id=1, source_target_pairs={{0,16},{4,20},{8,24},{12,28},{16,0},{20,4},{24,8},{28,12},{1,17},{... | collective-permute-start | bytes 393224 | tf_op jit(solution)/shard_map/ppermute | solution.py:279
  45.9 5.4 %collective-permute-start.19 = (f32[64,512]{1,0:T(8,128)S(1)}, f32[64,512]{1,0:T(8,128)S(1)}, u32[]{:S(2)}, u32[]{:S(2)}) collective-permute-start(f32[64,512]{1,0:T(8,128)S(1)} %get-tuple-element.79), channel_id=1, source_target_pairs={{0,8},{4,12},{8,0},{12,4},{16,24},{20,28},{24,16},{28,20},{1,9},{5... | collective-permute-start | bytes 393224 | tf_op jit(solution)/shard_map/ppermute | solution.py:279

commit v5 on v4

--- a/solution.py
+++ b/solution.py
@@ -173,14 +173,12 @@
 
     value_grads, key_grads = [], []
     shared_grad = jnp.zeros((length, 2 * ROPE), F32)
-    ready = front(0)
+    fronts = [front(head) for head in range(head_count)]
     for head in range(head_count):
-        later = front(head + 1) if head + 1 < head_count else None
-        value_part, key_part, shared_part = back(head, *middle(head, *ready))
+        value_part, key_part, shared_part = back(head, *middle(head, *fronts[head]))
         value_grads.append(value_part)
         key_grads.append(key_part)
         shared_grad = shared_grad + shared_part
-        ready = later
     key_grad = split(jnp.concatenate(key_grads, axis=1))
     value_grad = split(jnp.concatenate(value_grads, axis=1))
 

time: 52.2 us -> 52.1 us (level)
  no operation moved by 1% of the time
where the time goes in v5:
time: 52.1 us; the launch traced here: 51.9 us
  starting transfers between devices  26.5 us (51%)
  waiting for transfers between devices  14.1 us (27%)
  Pallas kernels  10.6 us (20%)
  between operations  0.71 us (1%)
    ppermute x6, starting transfers between devices, shift(): lax.ppermute(x, 'head', [(i, (i + step) % ways) for i in range(ways)])  13.6 us
    ppermute x14, starting transfers between devices, swap(): return lax.ppermute(x, 'fsdp', [(i, i ^ step) for i in range(fsdp)])  12.9 us
    ppermute x6, waiting for transfers between devices, shift(): lax.ppermute(x, 'head', [(i, (i + step) % ways) for i in range(ways)])  8.6 us
    ppermute x14, waiting for transfers between devices, swap(): return lax.ppermute(x, 'fsdp', [(i, i ^ step) for i in range(fsdp)])  5.5 us
    pallas_call x1, Pallas kernels, on_device(): pl.pallas_call(functools.partial(attention_kernel, ways, chips), out_shap...  5.06 us
    pallas_call x1, Pallas kernels, on_device(): pl.pallas_call(query_kernel, out_shape=(hbm(*wide), hbm(*query_rope.shape...  1.78 us
    pallas_call x1, Pallas kernels, on_device(): pl.pallas_call(prepare_kernel, out_shape=[pltpu.VMEM((length, length), F3...  1.76 us
    pallas_call x1, Pallas kernels, on_device(): pl.pallas_call(pack_kernel, out_shape=(pltpu.VMEM((packed, lat), F32), pl...  1.09 us
  transfers between devices with their start and end apart: 20, of which 9 were waited for; matrix products, arithmetic and copies ran while one was open for 0% of the time, Pallas kernels for 7%

profile of v5, /device:TPU:0, one launch (start us, length us, event | category | flops | bytes accessed | tf_op | source)
XLA Modules:
  0.0 51.9 jit_solution(6796988502372673942)
XLA Ops:
  0.6 1.1 %pack.1 = (f32[72,512]{1,0:T(8,128)S(1)}, f32[128,512]{1,0:T(8,128)S(1)}) custom-call(f32[64,512]{1,0:T(8,128)} %latent_ref.1, f32[64,64]{1,0:T(8,128)} %rope_ref.2, f32[64,512]{1,0:T(8,128)} %key_ref.1, f32[64,512]{1,0:T(8,128)} %value_ref.1), custom_call_target="tpu_custom_call" | custom-call | tf_op jit(solution)/shard_map/pack/pallas_call | solution.py:282
  1.7 4.0 %collective-permute-start.8 = (f32[128,512]{1,0:T(8,128)S(1)}, f32[128,512]{1,0:T(8,128)S(1)}, u32[]{:S(2)}, u32[]{:S(2)}) collective-permute-start(f32[128,512]{1,0:T(8,128)S(1)} %get-tuple-element.46.refs_4_), channel_id=1, source_target_pairs={{0,24},{4,28},{8,16},{12,20},{16,8},{20,12},{24,0},{28,4},{1,25},{... | collective-permute-start | bytes 786440 | tf_op jit(solution)/shard_map/ppermute | solution.py:277
  5.7 0.5 collective-permute-start.6
  6.2 0.1 collective-permute-start.4
  6.4 2.0 %collective-permute-start.2 = (f32[72,512]{1,0:T(8,128)S(1)}, f32[72,512]{1,0:T(8,128)S(1)}, u32[]{:S(2)}, u32[]{:S(2)}) collective-permute-start(f32[72,512]{1,0:T(8,128)S(1)} %get-tuple-element.45.refs_0_), channel_id=1, source_target_pairs={{0,1},{1,2},{2,3},{3,0},{4,5},{5,6},{6,7},{7,4},{8,9},{9,10},{10,1... | collective-permute-start | bytes 442376 | tf_op jit(solution)/shard_map/ppermute | solution.py:280
  8.3 2.6 %collective-permute-start.1 = (f32[72,512]{1,0:T(8,128)S(1)}, f32[72,512]{1,0:T(8,128)S(1)}, u32[]{:S(2)}, u32[]{:S(2)}) collective-permute-start(f32[72,512]{1,0:T(8,128)S(1)} %get-tuple-element.45.refs_0_), channel_id=1, source_target_pairs={{0,2},{1,3},{2,0},{3,1},{4,6},{5,7},{6,4},{7,5},{8,10},{9,11},{10,... | collective-permute-start | bytes 442376 | tf_op jit(solution)/shard_map/ppermute | solution.py:280
  10.9 4.1 %collective-permute-done.2.refs_3_ = f32[72,512]{1,0:T(8,128)S(1)} collective-permute-done((f32[72,512]{1,0:T(8,128)S(1)}, f32[72,512]{1,0:T(8,128)S(1)}, u32[]{:S(2)}, u32[]{:S(2)}) %collective-permute-start.2) | collective-permute-done | bytes 147488 | tf_op jit(solution)/shard_map/ppermute | solution.py:280
  15.0 0.5 collective-permute-start.9
  15.6 2.1 %collective-permute-done.6.refs_8_ = f32[128,512]{1,0:T(8,128)S(1)} collective-permute-done((f32[128,512]{1,0:T(8,128)S(1)}, f32[128,512]{1,0:T(8,128)S(1)}, u32[]{:S(2)}, u32[]{:S(2)}) %collective-permute-start.6) | collective-permute-done | bytes 262176 | tf_op jit(solution)/shard_map/ppermute | solution.py:277
  17.7 0.3 collective-permute-done.4.refs_6_
  17.9 0.2 collective-permute-start.5
  18.2 1.5 %collective-permute-done.1.refs_2_ = f32[72,512]{1,0:T(8,128)S(1)} collective-permute-done((f32[72,512]{1,0:T(8,128)S(1)}, f32[72,512]{1,0:T(8,128)S(1)}, u32[]{:S(2)}, u32[]{:S(2)}) %collective-permute-start.1) | collective-permute-done | bytes 147488 | tf_op jit(solution)/shard_map/ppermute | solution.py:280
  19.7 2.3 %collective-permute-start = (f32[72,512]{1,0:T(8,128)S(1)}, f32[72,512]{1,0:T(8,128)S(1)}, u32[]{:S(2)}, u32[]{:S(2)}) collective-permute-start(f32[72,512]{1,0:T(8,128)S(1)} %get-tuple-element.45.refs_0_), channel_id=1, source_target_pairs={{0,3},{1,0},{2,1},{3,2},{4,7},{5,4},{6,5},{7,6},{8,11},{9,8},{10,9... | collective-permute-start | bytes 442376 | tf_op jit(solution)/shard_map/ppermute | solution.py:280
  22.0 1.8 %prepare.1 = (f32[256,256]{1,0:T(8,128)S(1)}, bf16[4,256,192]{2,1,0:T(8,128)(2,1)S(1)}, bf16[256,512]{1,0:T(8,128)(2,1)S(1)}, bf16[256,512]{1,0:T(8,128)(2,1)S(1...) custom-call(s32[1,2]{1,0:T(1,128)} %limit_ref.1, f32[256,512]{1,0:T(8,128)} %nope_ref.1, ...), custom_call_target="tpu_custom_call" | custom-call | tf_op jit(solution)/shard_map/prepare/pallas_call | solution.py:296
  23.7 1.7 %collective-permute-done.refs_1_ = f32[72,512]{1,0:T(8,128)S(1)} collective-permute-done((f32[72,512]{1,0:T(8,128)S(1)}, f32[72,512]{1,0:T(8,128)S(1)}, u32[]{:S(2)}, u32[]{:S(2)}) %collective-permute-start) | collective-permute-done | bytes 147488 | tf_op jit(solution)/shard_map/ppermute | solution.py:280
  25.5 5.1 %attention.1 = (f32[64,1024]{1,0:T(8,128)S(1)}, f32[64,1024]{1,0:T(8,128)S(1)}, f32[64,1024]{1,0:T(8,128)S(1)}, f32[64,1024]{1,0:T(8,128)S(1)}, f32[4,64,1024]{2...) custom-call(f32[72,512]{1,0:T(8,128)S(1)} %get-tuple-element.45.refs, ...), custom_call_target="tpu_custom_call" | custom-call | tf_op jit(solution)/shard_map/attention/pallas_call | solution.py:302
  30.6 0.4 collective-permute-start.10
  31.0 4.4 %collective-permute-start.11 = (f32[72,512]{1,0:T(8,128)S(1)}, f32[72,512]{1,0:T(8,128)S(1)}, u32[]{:S(2)}, u32[]{:S(2)}) collective-permute-start(f32[72,512]{1,0:T(8,128)S(1)} %get-tuple-element.63), channel_id=1, source_target_pairs={{0,2},{1,3},{2,0},{3,1},{4,6},{5,7},{6,4},{7,5},{8,10},{9,11},{10,... | collective-permute-start | bytes 442376 | tf_op jit(solution)/shard_map/ppermute | solution.py:280
  35.4 0.1 join.1
  35.5 1.6 %collective-permute-start.15 = (f32[64,512]{1,0:T(8,128)S(1)}, f32[64,512]{1,0:T(8,128)S(1)}, u32[]{:S(2)}, u32[]{:S(2)}) collective-permute-start(f32[64,512]{1,0:T(8,128)S(1)} %get-tuple-element.74), channel_id=1, source_target_pairs={{0,8},{4,12},{8,0},{12,4},{16,24},{20,28},{24,16},{28,20},{1,9},{5... | collective-permute-start | bytes 393224 | tf_op jit(solution)/shard_map/ppermute | solution.py:277
  37.1 0.8 %collective-permute-start.16 = (f32[64,512]{1,0:T(8,128)S(1)}, f32[64,512]{1,0:T(8,128)S(1)}, u32[]{:S(2)}, u32[]{:S(2)}) collective-permute-start(f32[64,512]{1,0:T(8,128)S(1)} %get-tuple-element.75), channel_id=1, source_target_pairs={{0,16},{4,20},{8,24},{12,28},{16,0},{20,4},{24,8},{28,12},{1,17},{... | collective-permute-start | bytes 393224 | tf_op jit(solution)/shard_map/ppermute | solution.py:277
  37.8 2.0 %collective-permute-start.12 = (f32[72,512]{1,0:T(8,128)S(1)}, f32[72,512]{1,0:T(8,128)S(1)}, u32[]{:S(2)}, u32[]{:S(2)}) collective-permute-start(f32[72,512]{1,0:T(8,128)S(1)} %get-tuple-element.64), channel_id=1, source_target_pairs={{0,3},{1,0},{2,1},{3,2},{4,7},{5,4},{6,5},{7,6},{8,11},{9,8},{10,9... | collective-permute-start | bytes 442376 | tf_op jit(solution)/shard_map/ppermute | solution.py:280
  39.9 1.0 %collective-permute-done.15.refs_2_ = f32[64,512]{1,0:T(8,128)S(1)} collective-permute-done((f32[64,512]{1,0:T(8,128)S(1)}, f32[64,512]{1,0:T(8,128)S(1)}, u32[]{:S(2)}, u32[]{:S(2)}) %collective-permute-start.15) | collective-permute-done | bytes 131104 | tf_op jit(solution)/shard_map/ppermute | solution.py:277
  40.9 1.5 %collective-permute-start.14 = (f32[64,512]{1,0:T(8,128)S(1)}, f32[64,512]{1,0:T(8,128)S(1)}, u32[]{:S(2)}, u32[]{:S(2)}) collective-permute-start(f32[64,512]{1,0:T(8,128)S(1)} %get-tuple-element.71), channel_id=1, source_target_pairs={{0,8},{4,12},{8,0},{12,4},{16,24},{20,28},{24,16},{28,20},{1,9},{5... | collective-permute-start | bytes 393224 | tf_op jit(solution)/shard_map/ppermute | solution.py:277
  42.4 0.8 %collective-permute-start.18 = (f32[64,512]{1,0:T(8,128)S(1)}, f32[64,512]{1,0:T(8,128)S(1)}, u32[]{:S(2)}, u32[]{:S(2)}) collective-permute-start(f32[64,512]{1,0:T(8,128)S(1)} %get-tuple-element.78), channel_id=1, source_target_pairs={{0,16},{4,20},{8,24},{12,28},{16,0},{20,4},{24,8},{28,12},{1,17},{... | collective-permute-start | bytes 393224 | tf_op jit(solution)/shard_map/ppermute | solution.py:277
  43.2 1.3 %collective-permute-start.17 = (f32[64,512]{1,0:T(8,128)S(1)}, f32[64,512]{1,0:T(8,128)S(1)}, u32[]{:S(2)}, u32[]{:S(2)}) collective-permute-start(f32[64,512]{1,0:T(8,128)S(1)} %get-tuple-element.76), channel_id=1, source_target_pairs={{0,16},{4,20},{8,24},{12,28},{16,0},{20,4},{24,8},{28,12},{1,17},{... | collective-permute-start | bytes 393224 | tf_op jit(solution)/shard_map/ppermute | solution.py:277
  44.5 1.2 %collective-permute-done.11.refs_2_ = f32[72,512]{1,0:T(8,128)S(1)} collective-permute-done((f32[72,512]{1,0:T(8,128)S(1)}, f32[72,512]{1,0:T(8,128)S(1)}, u32[]{:S(2)}, u32[]{:S(2)}) %collective-permute-start.11) | collective-permute-done | bytes 147488 | tf_op jit(solution)/shard_map/ppermute | solution.py:280
  45.7 1.5 %collective-permute-start.19 = (f32[64,512]{1,0:T(8,128)S(1)}, f32[64,512]{1,0:T(8,128)S(1)}, u32[]{:S(2)}, u32[]{:S(2)}) collective-permute-start(f32[64,512]{1,0:T(8,128)S(1)} %get-tuple-element.79), channel_id=1, source_target_pairs={{0,8},{4,12},{8,0},{12,4},{16,24},{20,28},{24,16},{28,20},{1,9},{5... | collective-permute-start | bytes 393224 | tf_op jit(solution)/shard_map/ppermute | solution.py:277
  47.2 1.8 %query.1 = (f32[256,512]{1,0:T(8,128)}, f32[256,256]{1,0:T(8,128)}) custom-call(bf16[4,256,256]{2,1,0:T(8,128)(2,1)S(1)} %get-tuple-element.53.refs_0_, bf16[4,256,256]{2,1,0:T(8,128)(2,1)S(1)} %get-tuple-element.54.refs_1_, bf16[256,512]{1,0:T(8,128)(2,1)S(1)} %get-tuple-element.55.refs_2_, bf16[256,512]{1,0:T(8,128)(2,1)S(1)} %get-tuple-element.56.refs_3_, ...), custom_call_target="tpu_custom_call" | custom-call | tf_op jit(solution)/shard_map/query/pallas_call | solution.py:318
  49.0 0.3 collective-permute-done.17.refs_6_
  49.3 1.8 %collective-permute-done.19.refs_9_ = f32[64,512]{1,0:T(8,128)S(1)} collective-permute-done((f32[64,512]{1,0:T(8,128)S(1)}, f32[64,512]{1,0:T(8,128)S(1)}, u32[]{:S(2)}, u32[]{:S(2)}) %collective-permute-start.19) | collective-permute-done | bytes 131104 | tf_op jit(solution)/shard_map/ppermute | solution.py:277
  51.1 0.8 %sums.1 = (f32[64,512]{1,0:T(8,128)}, f32[64,64]{1,0:T(8,128)}, f32[64,512]{1,0:T(8,128)}, f32[64,512]{1,0:T(8,128)}) custom-call(f32[72,512]{1,0:T(8,128)S(1)} %get-tuple-element.61.refs_0_, f32[72,512]{1,0:T(8,128)S(1)} %collective-permute-done.10.refs_1_, f32[72,512]{1,0:T(8,128)S(1)} %collective-permute-done.11.refs_2_, ...), custom_call_target="tpu_custom_call" | custom-call | tf_op jit(solution)/shard_map/sums/pallas_call | solution.py:345
  (15 shorter events, 0.1 us)
Async XLA Ops:
  1.7 13.3 %collective-permute-start.8 = (f32[128,512]{1,0:T(8,128)S(1)}, f32[128,512]{1,0:T(8,128)S(1)}, u32[]{:S(2)}, u32[]{:S(2)}) collective-permute-start(f32[128,512]{1,0:T(8,128)S(1)} %get-tuple-element.46.refs_4_), channel_id=1, source_target_pairs={{0,24},{4,28},{8,16},{12,20},{16,8},{20,12},{24,0},{28,4},{1,25},{... | collective-permute-start | bytes 786440 | tf_op jit(solution)/shard_map/ppermute | solution.py:277
  5.7 11.9 %collective-permute-start.6 = (f32[128,512]{1,0:T(8,128)S(1)}, f32[128,512]{1,0:T(8,128)S(1)}, u32[]{:S(2)}, u32[]{:S(2)}) collective-permute-start(f32[128,512]{1,0:T(8,128)S(1)} %get-tuple-element.46.refs_4_), channel_id=1, source_target_pairs={{0,16},{4,20},{8,24},{12,28},{16,0},{20,4},{24,8},{28,12},{1,17},{... | collective-permute-start | bytes 786440 | tf_op jit(solution)/shard_map/ppermute | solution.py:277
  6.2 11.7 %collective-permute-start.4 = (f32[128,512]{1,0:T(8,128)S(1)}, f32[128,512]{1,0:T(8,128)S(1)}, u32[]{:S(2)}, u32[]{:S(2)}) collective-permute-start(f32[128,512]{1,0:T(8,128)S(1)} %get-tuple-element.46.refs_4_), channel_id=1, source_target_pairs={{0,8},{4,12},{8,0},{12,4},{16,24},{20,28},{24,16},{28,20},{1,9},{5... | collective-permute-start | bytes 786440 | tf_op jit(solution)/shard_map/ppermute | solution.py:277
  6.4 8.7 %collective-permute-start.2 = (f32[72,512]{1,0:T(8,128)S(1)}, f32[72,512]{1,0:T(8,128)S(1)}, u32[]{:S(2)}, u32[]{:S(2)}) collective-permute-start(f32[72,512]{1,0:T(8,128)S(1)} %get-tuple-element.45.refs_0_), channel_id=1, source_target_pairs={{0,1},{1,2},{2,3},{3,0},{4,5},{5,6},{6,7},{7,4},{8,9},{9,10},{10,1... | collective-permute-start | bytes 442376 | tf_op jit(solution)/shard_map/ppermute | solution.py:280
  8.3 11.3 %collective-permute-start.1 = (f32[72,512]{1,0:T(8,128)S(1)}, f32[72,512]{1,0:T(8,128)S(1)}, u32[]{:S(2)}, u32[]{:S(2)}) collective-permute-start(f32[72,512]{1,0:T(8,128)S(1)} %get-tuple-element.45.refs_0_), channel_id=1, source_target_pairs={{0,2},{1,3},{2,0},{3,1},{4,6},{5,7},{6,4},{7,5},{8,10},{9,11},{10,... | collective-permute-start | bytes 442376 | tf_op jit(solution)/shard_map/ppermute | solution.py:280
  15.0 10.4 %collective-permute-start.3 = (f32[128,512]{1,0:T(8,128)S(1)}, f32[128,512]{1,0:T(8,128)S(1)}, u32[]{:S(2)}, u32[]{:S(2)}) collective-permute-start(f32[128,512]{1,0:T(8,128)S(1)} %get-tuple-element.46.refs_4_), channel_id=1, source_target_pairs={{0,4},{4,0},{8,12},{12,8},{16,20},{20,16},{24,28},{28,24},{1,5},{5... | collective-permute-start | bytes 786440 | tf_op jit(solution)/shard_map/ppermute | solution.py:277
  15.0 10.4 %collective-permute-start.9 = (f32[128,512]{1,0:T(8,128)S(1)}, f32[128,512]{1,0:T(8,128)S(1)}, u32[]{:S(2)}, u32[]{:S(2)}) collective-permute-start(f32[128,512]{1,0:T(8,128)S(1)} %collective-permute-done.8.refs_10_), channel_id=1, source_target_pairs={{0,4},{4,0},{8,12},{12,8},{16,20},{20,16},{24,28},{28,24},{1,5},{5... | collective-permute-start | bytes 786440 | tf_op jit(solution)/shard_map/ppermute | solution.py:277
  17.6 7.8 %collective-permute-start.7 = (f32[128,512]{1,0:T(8,128)S(1)}, f32[128,512]{1,0:T(8,128)S(1)}, u32[]{:S(2)}, u32[]{:S(2)}) collective-permute-start(f32[128,512]{1,0:T(8,128)S(1)} %collective-permute-done.6.refs_8_), channel_id=1, source_target_pairs={{0,4},{4,0},{8,12},{12,8},{16,20},{20,16},{24,28},{28,24},{1,5},{5... | collective-permute-start | bytes 786440 | tf_op jit(solution)/shard_map/ppermute | solution.py:277
  17.9 7.5 %collective-permute-start.5 = (f32[128,512]{1,0:T(8,128)S(1)}, f32[128,512]{1,0:T(8,128)S(1)}, u32[]{:S(2)}, u32[]{:S(2)}) collective-permute-start(f32[128,512]{1,0:T(8,128)S(1)} %collective-permute-done.4.refs_6_), channel_id=1, source_target_pairs={{0,4},{4,0},{8,12},{12,8},{16,20},{20,16},{24,28},{28,24},{1,5},{5... | collective-permute-start | bytes 786440 | tf_op jit(solution)/shard_map/ppermute | solution.py:277
  19.7 5.8 %collective-permute-start = (f32[72,512]{1,0:T(8,128)S(1)}, f32[72,512]{1,0:T(8,128)S(1)}, u32[]{:S(2)}, u32[]{:S(2)}) collective-permute-start(f32[72,512]{1,0:T(8,128)S(1)} %get-tuple-element.45.refs_0_), channel_id=1, source_target_pairs={{0,3},{1,0},{2,1},{3,2},{4,7},{5,4},{6,5},{7,6},{8,11},{9,8},{10,9... | collective-permute-start | bytes 442376 | tf_op jit(solution)/shard_map/ppermute | solution.py:280
  30.6 4.8 %collective-permute-start.13 = (f32[4,64,1024]{2,1,0:T(8,128)S(1)}, f32[4,64,1024]{2,1,0:T(8,128)S(1)}, u32[]{:S(2)}, u32[]{:S(2)}) collective-permute-start(f32[4,64,1024]{2,1,0:T(8,128)S(1)} %get-tuple-element.65), channel_id=1, source_target_pairs={{0,4},{4,0},{8,12},{12,8},{16,20},{20,16},{24,28},{28,24},{1,5},{5... | collective-permute-start | bytes 3145736 | tf_op jit(solution)/shard_map/ppermute | solution.py:277
  30.6 12.5 %collective-permute-start.10 = (f32[72,512]{1,0:T(8,128)S(1)}, f32[72,512]{1,0:T(8,128)S(1)}, u32[]{:S(2)}, u32[]{:S(2)}) collective-permute-start(f32[72,512]{1,0:T(8,128)S(1)} %get-tuple-element.62), channel_id=1, source_target_pairs={{0,1},{1,2},{2,3},{3,0},{4,5},{5,6},{6,7},{7,4},{8,9},{9,10},{10,1... | collective-permute-start | bytes 442376 | tf_op jit(solution)/shard_map/ppermute | solution.py:280
  31.0 14.7 %collective-permute-start.11 = (f32[72,512]{1,0:T(8,128)S(1)}, f32[72,512]{1,0:T(8,128)S(1)}, u32[]{:S(2)}, u32[]{:S(2)}) collective-permute-start(f32[72,512]{1,0:T(8,128)S(1)} %get-tuple-element.63), channel_id=1, source_target_pairs={{0,2},{1,3},{2,0},{3,1},{4,6},{5,7},{6,4},{7,5},{8,10},{9,11},{10,... | collective-permute-start | bytes 442376 | tf_op jit(solution)/shard_map/ppermute | solution.py:280
  35.5 5.4 %collective-permute-start.15 = (f32[64,512]{1,0:T(8,128)S(1)}, f32[64,512]{1,0:T(8,128)S(1)}, u32[]{:S(2)}, u32[]{:S(2)}) collective-permute-start(f32[64,512]{1,0:T(8,128)S(1)} %get-tuple-element.74), channel_id=1, source_target_pairs={{0,8},{4,12},{8,0},{12,4},{16,24},{20,28},{24,16},{28,20},{1,9},{5... | collective-permute-start | bytes 393224 | tf_op jit(solution)/shard_map/ppermute | solution.py:277
  37.1 5.3 %collective-permute-start.16 = (f32[64,512]{1,0:T(8,128)S(1)}, f32[64,512]{1,0:T(8,128)S(1)}, u32[]{:S(2)}, u32[]{:S(2)}) collective-permute-start(f32[64,512]{1,0:T(8,128)S(1)} %get-tuple-element.75), channel_id=1, source_target_pairs={{0,16},{4,20},{8,24},{12,28},{16,0},{20,4},{24,8},{28,12},{1,17},{... | collective-permute-start | bytes 393224 | tf_op jit(solution)/shard_map/ppermute | solution.py:277
  37.8 11.1 %collective-permute-start.12 = (f32[72,512]{1,0:T(8,128)S(1)}, f32[72,512]{1,0:T(8,128)S(1)}, u32[]{:S(2)}, u32[]{:S(2)}) collective-permute-start(f32[72,512]{1,0:T(8,128)S(1)} %get-tuple-element.64), channel_id=1, source_target_pairs={{0,3},{1,0},{2,1},{3,2},{4,7},{5,4},{6,5},{7,6},{8,11},{9,8},{10,9... | collective-permute-start | bytes 442376 | tf_op jit(solution)/shard_map/ppermute | solution.py:280
  40.9 8.1 %collective-permute-start.14 = (f32[64,512]{1,0:T(8,128)S(1)}, f32[64,512]{1,0:T(8,128)S(1)}, u32[]{:S(2)}, u32[]{:S(2)}) collective-permute-start(f32[64,512]{1,0:T(8,128)S(1)} %get-tuple-element.71), channel_id=1, source_target_pairs={{0,8},{4,12},{8,0},{12,4},{16,24},{20,28},{24,16},{28,20},{1,9},{5... | collective-permute-start | bytes 393224 | tf_op jit(solution)/shard_map/ppermute | solution.py:277
  42.4 6.6 %collective-permute-start.18 = (f32[64,512]{1,0:T(8,128)S(1)}, f32[64,512]{1,0:T(8,128)S(1)}, u32[]{:S(2)}, u32[]{:S(2)}) collective-permute-start(f32[64,512]{1,0:T(8,128)S(1)} %get-tuple-element.78), channel_id=1, source_target_pairs={{0,16},{4,20},{8,24},{12,28},{16,0},{20,4},{24,8},{28,12},{1,17},{... | collective-permute-start | bytes 393224 | tf_op jit(solution)/shard_map/ppermute | solution.py:277
  43.2 6.2 %collective-permute-start.17 = (f32[64,512]{1,0:T(8,128)S(1)}, f32[64,512]{1,0:T(8,128)S(1)}, u32[]{:S(2)}, u32[]{:S(2)}) collective-permute-start(f32[64,512]{1,0:T(8,128)S(1)} %get-tuple-element.76), channel_id=1, source_target_pairs={{0,16},{4,20},{8,24},{12,28},{16,0},{20,4},{24,8},{28,12},{1,17},{... | collective-permute-start | bytes 393224 | tf_op jit(solution)/shard_map/ppermute | solution.py:277
  45.7 5.4 %collective-permute-start.19 = (f32[64,512]{1,0:T(8,128)S(1)}, f32[64,512]{1,0:T(8,128)S(1)}, u32[]{:S(2)}, u32[]{:S(2)}) collective-permute-start(f32[64,512]{1,0:T(8,128)S(1)} %get-tuple-element.79), channel_id=1, source_target_pairs={{0,8},{4,12},{8,0},{12,4},{16,24},{20,28},{24,16},{28,20},{1,9},{5... | collective-permute-start | bytes 393224 | tf_op jit(solution)/shard_map/ppermute | solution.py:277
